TPU v7x, 32 devices: a whole 2x2x4 slice. The times are simulated.
32 devices in a mesh: blocks: 2 (over y), space: 4 (over z), view: 4 (over x, core).
Axes of the slice: x: 2, y: 2, z: 4, core: 2. Of those that a mesh axis runs over, the one named last changes fastest.
Arguments:
- estimate: float32 [64, 512, 128], P('space', 'blocks'), parts along dimension 1, may hold values from 0.5 to 7.5
- observed: float32 [4, 64, 512, 128], P('view', 'space', 'blocks'), parts along dimension 2, may hold values from 0.25 to 31.5
- valid: int32 [4, 64, 512, 128], P('view', 'space', 'blocks'), parts along dimension 2, may hold values 0 or 1
- psf_spectrum: float32 [4, 2, 64, 256, 128], P('view', None, None, 'space'), may hold values from -1 to 1
Outputs:
- refined: float32 [64, 512, 128], P('space', 'blocks'), parts along dimension 1
There are 2 independent parts, one for each index of `blocks`. A program takes and returns all parts, laid end to end along the dimension named above; an argument that names none is the same for every part. Nothing has to cross between parts.
Inputs may be any that keep to these rules, and one draw needn't show every extreme that they name: `valid`: 1 marks a voxel that the view records, 0 one that it does not.
All inputs are finite; a program needn't handle non-finite values. No bound on the sum of `valid` on one device may be relied on, other than what follows from the above.
Results may differ from a plain program's by a relative error of at most 0.00013.
Values sent between devices are 32-bit elements; how exact they have to be, the bound alone decides.
No kernel may reach another device: no remote copies, remote signals or barrier semaphores. Data moves between devices by JAX's collectives and lax.ppermute only.
A program may use at most 128 MiB of HBM per device.

v0:
```python
import math

import jax
import jax.numpy as jnp
from jax import lax
from jax.sharding import PartitionSpec as P

ITERS = 2


HIGHEST = lax.Precision.HIGHEST


def dft_tables(length):
    indices = jnp.arange(length, dtype=jnp.int32)
    phases = indices[:, None] * indices[None, :] % length
    angles = phases.astype(jnp.float32) * (2.0 * math.pi / length)
    return (jnp.cos(angles), jnp.sin(angles))


def along_depth(matrix, volume):
    return jnp.einsum(
        "kz,zxy->kxy", matrix, volume, precision=HIGHEST, preferred_element_type=jnp.float32
    )


def along_rows(matrix, volume):
    return jnp.einsum(
        "kx,zxy->zky", matrix, volume, precision=HIGHEST, preferred_element_type=jnp.float32
    )


def along_columns(matrix, volume):
    return jnp.einsum(
        "zxy,yk->zxk", volume, matrix, precision=HIGHEST, preferred_element_type=jnp.float32
    )


def along_picked(matrix, volume):
    return jnp.einsum(
        "kx,zky->zxy", matrix, volume, precision=HIGHEST, preferred_element_type=jnp.float32
    )


def complex_step(along, matrices, real_part, imaginary, sign_value):
    cosines, sines = matrices
    new_real = along(cosines, real_part) - sign_value * along(sines, imaginary)
    new_imaginary = along(cosines, imaginary) + sign_value * along(sines, real_part)
    return (new_real, new_imaginary)


def shards(estimate, observed, valid, psf_spectrum):
    space_count = lax.axis_size("space")
    view_devices = lax.axis_size("view")
    depth_total = estimate.shape[0] * space_count
    row_total = estimate.shape[1]
    column_total = estimate.shape[2]
    depth_tab = dft_tables(depth_total)
    rows_tab = dft_tables(row_total)
    columns_tab = dft_tables(column_total)
    norm_factor = 1.0 / (depth_total * row_total * column_total)
    local_views = observed.shape[0]
    view_count = local_views * view_devices

    def slab_forward(volume):
        first_real = along_rows(rows_tab[0], volume)
        first_imaginary = -along_rows(rows_tab[1], volume)
        return jnp.stack(
            complex_step(along_columns, columns_tab, first_real, first_imaginary, -1.0)
        )

    for iteration in range(ITERS):
        pencil = lax.all_to_all(
            slab_forward(estimate), "space", split_axis=2, concat_axis=1, tiled=True
        )
        spec_real, spec_imag = complex_step(along_depth, depth_tab, pencil[0], pencil[1], -1.0)
        accumulated = None
        kernel_real = psf_spectrum[0, 0]
        kernel_imag = psf_spectrum[0, 1]
        prod_real = spec_real * kernel_real - spec_imag * kernel_imag
        prod_imag = spec_real * kernel_imag + spec_imag * kernel_real
        returned = jnp.stack(complex_step(along_depth, depth_tab, prod_real, prod_imag, 1.0))
        slab_view = lax.all_to_all(returned, "space", split_axis=1, concat_axis=2, tiled=True)
        real_part, imaginary = complex_step(
            along_columns, columns_tab, slab_view[0], slab_view[1], 1.0
        )
        blurred = (
            along_rows(rows_tab[0], real_part) - along_rows(rows_tab[1], imaginary)
        ) * norm_factor
        valid_mask = valid[0].astype(jnp.float32)
        ratios = valid_mask * observed[0] / blurred + (1.0 - valid_mask)
        ratio_pencil = lax.all_to_all(
            slab_forward(ratios), "space", split_axis=2, concat_axis=1, tiled=True
        )
        ratio_real, ratio_imag = complex_step(
            along_depth, depth_tab, ratio_pencil[0], ratio_pencil[1], -1.0
        )
        adjoint_real = ratio_real * kernel_real + ratio_imag * kernel_imag
        adjoint_imag = ratio_imag * kernel_real - ratio_real * kernel_imag
        term = jnp.stack((adjoint_real, adjoint_imag))
        accumulated = term
        summed = lax.psum_scatter(accumulated, "view", scatter_dimension=2, tiled=True)
        inv_real, inv_imag = complex_step(along_depth, depth_tab, summed[0], summed[1], 1.0)
        inv_real, inv_imag = complex_step(along_columns, columns_tab, inv_real, inv_imag, 1.0)
        share_slab = lax.all_to_all(
            jnp.stack((inv_real, inv_imag)), "space", split_axis=1, concat_axis=2, tiled=True
        )
        pencil_rows = row_total // space_count
        share_rows = pencil_rows // view_devices
        view_index = lax.axis_index("view")
        picked = (
            jnp.arange(space_count, dtype=jnp.int32)[:, None] * pencil_rows
            + view_index * share_rows
            + jnp.arange(share_rows, dtype=jnp.int32)[None, :]
        ).reshape(-1)
        phases = picked[:, None] * jnp.arange(row_total, dtype=jnp.int32)[None, :] % row_total
        angles = phases.astype(jnp.float32) * (2.0 * math.pi / row_total)
        partial_value = (
            along_picked(jnp.cos(angles), share_slab[0])
            - along_picked(jnp.sin(angles), share_slab[1])
        ) * norm_factor
        combined = lax.psum(partial_value, "view")
        estimate = estimate * combined / view_count
    return estimate


def solution(mesh):
    return jax.shard_map(
        shards,
        mesh=mesh,
        in_specs=(
            P("space", "blocks", None),
            P("view", "space", "blocks", None),
            P("view", "space", "blocks", None),
            P("view", None, None, "space", None),
        ),
        out_specs=P("space", "blocks", None),
        check_vma=False,
    )
```

profile of v0, /device:TPU:0, one launch (start us, length us, event | category | flops | bytes accessed | tf_op | source)
XLA Modules:
  0.0 1100.8 jit_solution(13561027013564466077)
XLA Ops:
  6.5 4.6 fusion.110
  23.3 4.5 copy.129
  27.8 6.3 all-to-all-start
  34.1 4.1 fusion.636
  38.2 89.4 %all-to-all-done = f32[2,16,256,128]{3,1,0,2:T(8,128)} async-done(((f32[2,16,256,128]{3,1,0,2:T(8,128)}), f32[2,16,256,128]{3,1,0,2:T(8,128)}, u32[]{:S(2)}, u32[]{:S(2)}) %all-to-all-start) | async-done | bytes 4194336 | tf_op jit(solution)/shard_map/all_to_all | solution.py:73
  137.3 4.5 multiply_subtract_fusion.4
  151.0 4.5 copy.133
  155.4 4.9 all-to-all-start.1
  166.4 86.6 %all-to-all-done.1 = f32[2,64,64,128]{3,2,0,1:T(8,128)} async-done(((f32[2,64,64,128]{3,2,0,1:T(8,128)}), f32[2,64,64,128]{3,2,0,1:T(8,128)}, u32[]{:S(2)}, u32[]{:S(2)}) %all-to-all-start.1) | async-done | bytes 4194336 | tf_op jit(solution)/shard_map/all_to_all | solution.py:83
  265.1 4.8 fusion.37
  270.0 4.8 bitcast_add_fusion
  291.5 4.4 add_bitcast_fusion.5
  298.8 95.3 %all_to_all.120 = f32[2,16,256,128]{3,1,0,2:T(8,128)S(1)} all-to-all(f32[2,16,256,128]{3,1,0,2:T(8,128)S(1)} %copy.143), channel_id=1, replica_groups=mesh['blocks'=2,'space'=4,'view'=4] {'space'}, dimensions={2} | all-to-all | bytes 8388608 | tf_op jit(solution)/shard_map/all_to_all | solution.py:92
  401.7 4.5 add_bitcast_fusion.4
  407.4 4.5 copy.266
  411.9 43.9 %reduce-scatter.9.cloned.1.call-done = f32[16,16384]{1,0:T(8,128)} async-done(((f32[64,16384]{1,0:T(8,128)}), f32[16,16384]{1,0:T(8,128)}) %reduce-scatter.9.cloned.1.call-update) | async-done | bytes 1048592
  465.6 4.6 all-to-all-start.3
  470.3 25.4 %all-to-all-done.3 = f32[2,64,16,128]{3,2,0,1:T(8,128)S(1)} async-done(((f32[2,64,16,128]{3,2,0,1:T(8,128)}), f32[2,64,16,128]{3,2,0,1:T(8,128)S(1)}, u32[]{:S(2)}, u32[]{:S(2)}) %all-to-all-start.3) | async-done | bytes 1048608 | tf_op jit(solution)/shard_map/all_to_all | solution.py:105
  504.9 46.4 %all-reduce.3.cloned.1.call-done = f32[16,256,128]{1,2,0:T(8,128)} async-done(((f32[16,256,128]{1,2,0:T(8,128)}), f32[16,256,128]{1,2,0:T(8,128)}) %all-reduce.3.cloned.1.call-update) | async-done | bytes 2097168 | tf_op jit(solution)/shard_map/psum | solution.py:122
  551.3 5.1 fusion.105
  576.8 97.3 %all_to_all.121 = f32[2,16,256,128]{3,1,0,2:T(8,128)S(1)} all-to-all(f32[2,16,256,128]{3,1,0,2:T(8,128)S(1)} %copy.156), channel_id=1, replica_groups=mesh['blocks'=2,'space'=4,'view'=4] {'space'}, dimensions={2} | all-to-all | bytes 8388608 | tf_op jit(solution)/shard_map/all_to_all | solution.py:73
  681.7 4.4 multiply_subtract_fusion.1
  698.0 95.2 %all_to_all.122 = f32[2,64,64,128]{3,2,0,1:T(8,128)S(1)} all-to-all(f32[2,64,64,128]{3,2,0,1:T(8,128)S(1)} %copy.158), channel_id=1, replica_groups=mesh['blocks'=2,'space'=4,'view'=4] {'space'}, dimensions={1} | all-to-all | bytes 8388608 | tf_op jit(solution)/shard_map/all_to_all | solution.py:83
  803.2 4.6 fusion.33
  807.8 4.5 fusion.8
  829.4 4.1 add_bitcast_fusion.1
  836.4 95.2 %all_to_all.123 = f32[2,16,256,128]{3,1,0,2:T(8,128)S(1)} all-to-all(f32[2,16,256,128]{3,1,0,2:T(8,128)S(1)} %copy.168), channel_id=1, replica_groups=mesh['blocks'=2,'space'=4,'view'=4] {'space'}, dimensions={2} | all-to-all | bytes 8388608 | tf_op jit(solution)/shard_map/all_to_all | solution.py:92
  939.3 4.4 add_bitcast_fusion
  944.9 4.5 copy.265
  949.6 43.0 %reduce-scatter.11.cloned.1.call-done = f32[16,16384]{1,0:T(8,128)} async-done(((f32[64,16384]{1,0:T(8,128)}), f32[16,16384]{1,0:T(8,128)}) %reduce-scatter.11.cloned.1.call-update) | async-done | bytes 1048592
  1001.4 30.2 %all_to_all.124 = f32[2,64,16,128]{3,2,0,1:T(8,128)S(1)} all-to-all(f32[2,64,16,128]{3,2,0,1:T(8,128)S(1)} %copy.174), channel_id=1, replica_groups=mesh['blocks'=2,'space'=4,'view'=4] {'space'}, dimensions={1} | all-to-all | bytes 2097152 | tf_op jit(solution)/shard_map/all_to_all | solution.py:105
  1037.4 49.7 %all-reduce.5.cloned.1.call-done = f32[16,256,128]{1,2,0:T(8,128)} async-done(((f32[16,256,128]{1,2,0:T(8,128)}), f32[16,256,128]{1,2,0:T(8,128)}) %all-reduce.5.cloned.1.call-update) | async-done | bytes 2097168 | tf_op jit(solution)/shard_map/psum | solution.py:122
  (146 shorter events, 196.1 us)
Async XLA Ops:
  6.5 4.6 copy-start.6
  27.8 99.8 %all-to-all-start = ((f32[2,16,256,128]{3,1,0,2:T(8,128)}), f32[2,16,256,128]{3,1,0,2:T(8,128)}, u32[]{:S(2)}, u32[]{:S(2)}) async-start(f32[2,16,256,128]{3,1,0,2:T(8,128)} %copy.129), calls=%async_computation | async-start | bytes 8388608 | tf_op jit(solution)/shard_map/all_to_all | solution.py:73
  135.2 2.2 copy-start
  155.4 97.5 %all-to-all-start.1 = ((f32[2,64,64,128]{3,2,0,1:T(8,128)}), f32[2,64,64,128]{3,2,0,1:T(8,128)}, u32[]{:S(2)}, u32[]{:S(2)}) async-start(f32[2,64,64,128]{3,2,0,1:T(8,128)} %copy.133), calls=%async_computation.1 | async-start | bytes 8388608 | tf_op jit(solution)/shard_map/all_to_all | solution.py:83
  160.3 295.5 %reduce-scatter.9.cloned.1.call-start = ((), (), s32[]{:S(2)}) async-start(), calls=%async_computation.12 | async-start | bytes 5242880
  265.1 4.9 copy-start.7
  265.1 4.9 copy-start.9
  399.5 2.3 copy-start.1
  465.6 30.2 %all-to-all-start.3 = ((f32[2,64,16,128]{3,2,0,1:T(8,128)}), f32[2,64,16,128]{3,2,0,1:T(8,128)S(1)}, u32[]{:S(2)}, u32[]{:S(2)}) async-start(f32[2,64,16,128]{3,2,0,1:T(8,128)} %copy.149), calls=%async_computation.3 | async-start | bytes 2097152 | tf_op jit(solution)/shard_map/all_to_all | solution.py:105
  470.2 81.1 %all-reduce.3.cloned.1.call-start = ((), (), s32[]{:S(2)}) async-start(), calls=%async_computation.10 | async-start | bytes 4194304 | tf_op jit(solution)/shard_map/psum | solution.py:122
  501.6 491.0 %reduce-scatter.11.cloned.1.call-start = ((), (), s32[]{:S(2)}) async-start(), calls=%async_computation.13 | async-start | bytes 5242880
  559.9 3.6 copy-start.3
  560.0 3.6 copy-start.5
  679.6 2.2 copy-start.2
  803.2 4.6 copy-start.8
  803.2 4.6 copy-start.10
  949.5 137.5 %all-reduce.5.cloned.1.call-start = ((), (), s32[]{:S(2)}) async-start(), calls=%async_computation.11 | async-start | bytes 4194304 | tf_op jit(solution)/shard_map/psum | solution.py:122
  1037.3 49.7 %copy-start.4 = (f32[16,256,128]{1,2,0:T(8,128)S(1)}, f32[16,256,128]{1,2,0:T(8,128)}, u32[]{:S(2)}) copy-start(f32[16,256,128]{1,2,0:T(8,128)} %copy.151) | copy-start | bytes 6291460
Sparse Core Ops, SparseCore 0:
  412.0 43.7 reduce-scatter.8
  501.7 49.5 all-reduce.2
  949.6 42.9 reduce-scatter.10
  1037.5 49.5 all-reduce.4
where the time goes:
time: 1110 us; the launch traced here: 1100 us
  blocking collectives  413 us (37%)
  waiting for transfers between devices  384 us (35%)
  matrix products  202 us (18%)
  local copies, waits for them, and re-layouts  62 us (6%)
  starting transfers between devices  15.9 us (1%)
  between operations  14.6 us (1%)
    all_to_all x2, blocking collectives, shards(): lax.all_to_all(slab_forward(ratios), 'space', split_axis=2, concat_axis=1...  190 us
    all_to_all x1, blocking collectives, shards(): lax.all_to_all(slab_forward(estimate), 'space', split_axis=2, concat_axis...  97.3 us
    psum x2, waiting for transfers between devices, shards(): combined = lax.psum(partial_value, 'view')  96 us
    all_to_all x1, blocking collectives, shards(): lax.all_to_all(returned, 'space', split_axis=1, concat_axis=2, tiled=True)  95.2 us
    all_to_all x1, waiting for transfers between devices, shards(): lax.all_to_all(slab_forward(estimate), 'space', split_axis=2, concat_axis...  89.4 us
    unnamed x6, waiting for transfers between devices  87 us
    all_to_all x1, waiting for transfers between devices, shards(): lax.all_to_all(returned, 'space', split_axis=1, concat_axis=2, tiled=True)  86.6 us
    dot_general x32, matrix products, along_columns(): jnp.einsum('zxy,yk->zxk', volume, matrix, precision=HIGHEST, preferred_el...  78.5 us
  transfers between devices with their start and end apart: 7, of which 7 were waited for; matrix products, arithmetic and copies ran while one was open for 1% of the time, Pallas kernels for 0%

commit v1 on v0

v1 whole, which is shorter than its diff:
```python
import functools

import jax
import jax.numpy as jnp
import ml_dtypes
import numpy as np
from jax import lax
from jax.experimental import pallas as pl
from jax.experimental.pallas import tpu as pltpu
from jax.sharding import PartitionSpec as P

ITERS = 2
INTERPRET = False


def split_np(matrix):
    high = matrix.astype(ml_dtypes.bfloat16)
    low = (matrix - high.astype(np.float64)).astype(ml_dtypes.bfloat16)
    return high, low


def angles_np(length):
    index = np.arange(length)
    return (np.outer(index, index) % length) * (2.0 * np.pi / length)


def column_tables(length, scale):
    half = length // 2
    angles = angles_np(length)
    cosines, sines = np.cos(angles), np.sin(angles)
    alternating = np.where(np.arange(length) % 2 == 0, 1.0, -1.0)
    forward = np.zeros((length, length))
    forward[:, :half] = cosines[:, :half]
    forward[:, half:] = -sines[:, :half]
    forward[:, half] = alternating
    inverse = np.zeros((length, length))
    inverse[:half] = 2.0 * cosines[:half]
    inverse[half:] = -2.0 * sines[:half]
    inverse[0] = 1.0
    inverse[half] = alternating
    inverse *= scale
    tables = []
    for matrix in (forward, inverse):
        high, low = split_np(matrix)
        both = np.concatenate([high, low], axis=1)
        tables.append(np.concatenate([both, both], axis=0))
    return tables


def row_tables(length, lanes):
    middle, half = length // 2, lanes // 2
    angles = angles_np(length)
    cosines, sines = np.cos(angles), np.sin(angles)
    sines[0] = -cosines[middle]
    sines[middle] = -cosines[0]
    high, low = split_np(np.concatenate([cosines, sines], axis=0))
    forward = np.concatenate([high, low], axis=0)
    high, low = split_np(np.concatenate([cosines.T, sines.T], axis=1))
    inverse = np.concatenate([high, low], axis=0)
    row = np.arange(length)[:, None]
    lane = np.arange(lanes)[None, :]
    plain = (lane % half) != 0
    lower = row < middle
    inner = (row % middle) != 0
    first, second = lane == 0, lane == half
    sign = np.where(lane < half, 1.0, -1.0)
    weight = np.where(inner, 2.0, 1.0)
    one = np.ones((length, lanes))
    forward_masks = np.stack(
        [
            one * (plain | (first & lower)),
            one * (first & ~lower),
            -one * (second & ~lower),
            sign * (plain & inner) - one * (second & lower),
        ]
    )
    inverse_masks = np.stack(
        [
            one * plain + weight * (first & lower),
            weight * (second & ~lower),
            -weight * (second & ~lower),
            -sign * (plain & inner) - weight * (first & lower),
        ]
    )
    return forward, inverse, forward_masks.astype(np.float32), inverse_masks.astype(np.float32)


def depth_forward(order):
    angles = angles_np(len(order))[:, order]
    high, low = split_np(np.concatenate([np.cos(angles), np.sin(angles)], axis=0))
    both = np.concatenate([high, low], axis=0)
    return np.concatenate([both, both], axis=1)


def depth_inverse(order):
    angles = angles_np(len(order))[order, :]
    high, low = split_np(np.concatenate([np.cos(angles), np.sin(angles)], axis=0))
    both = np.concatenate([high, low], axis=0)
    return np.concatenate([both, both], axis=1)


def split(value):
    high = value.astype(jnp.bfloat16)
    low = (value - high.astype(jnp.float32)).astype(jnp.bfloat16)
    return high, low


def dot(left, right):
    return lax.dot_general(
        left, right, (((1,), (0,)), ((), ())), preferred_element_type=jnp.float32
    )


def fold_lanes(value):
    lanes = value.shape[1] // 2
    return value[:, :lanes] + value[:, lanes:]


def fold_rows(value):
    rows = value.shape[0] // 2
    return value[:rows] + value[rows:]


def plane_forward(plane, columns, rows, masks):
    step = fold_lanes(dot(jnp.concatenate(split(plane), axis=1), columns[...]))
    both = fold_lanes(fold_rows(dot(rows[...], jnp.concatenate(split(step), axis=1))))
    count, half = both.shape[0] // 2, both.shape[1] // 2
    cos_part, sin_part = both[:count], both[count:]
    return (
        cos_part * masks[0]
        + pltpu.roll(cos_part, half, 1) * masks[1]
        + sin_part * masks[2]
        + pltpu.roll(sin_part, half, 1) * masks[3]
    )


def plane_inverse(spectrum, columns, rows, masks):
    rolled = pltpu.roll(spectrum, spectrum.shape[1] // 2, 1)
    both = jnp.concatenate(
        [spectrum * masks[0] + rolled * masks[1], spectrum * masks[2] + rolled * masks[3]], axis=0
    )
    step = fold_lanes(fold_rows(dot(rows[...], jnp.concatenate(split(both), axis=1))))
    return fold_lanes(dot(jnp.concatenate(split(step), axis=1), columns[...]))


def whole_spec(array):
    rank = array.ndim
    return pl.BlockSpec(array.shape, lambda *_: (0,) * rank)


def read_plane(ref, index):
    return ref[:, index].reshape(-1, ref.shape[-1])


def write_plane(ref, index, value):
    ref[:, index] = value.reshape(ref.shape[0], ref.shape[2], ref.shape[3])


def step_planes(planes):
    return 2 if planes % 2 == 0 else 1


def lateral_forward(volume, tables, parts):
    planes, rows, lanes = volume.shape
    step = step_planes(planes)

    def body(volume_ref, columns, row_table, masks, out_ref):
        for index in range(step):
            write_plane(out_ref, index, plane_forward(volume_ref[index], columns, row_table, masks))

    constants = (tables["columns_f"], tables["rows_f"], tables["masks_f"])
    return pl.pallas_call(
        body,
        grid=(planes // step,),
        out_shape=jax.ShapeDtypeStruct((parts, planes, rows // parts, lanes), jnp.float32),
        in_specs=[pl.BlockSpec((step, rows, lanes), lambda i: (i, 0, 0))]
        + [whole_spec(c) for c in constants],
        out_specs=pl.BlockSpec((parts, step, rows // parts, lanes), lambda i: (0, i, 0, 0)),
        interpret=INTERPRET,
        name="lateral_forward",
    )(volume, *constants)


def ratio_step(spectrum, observed, valid, tables):
    parts, planes, part_rows, lanes = spectrum.shape
    rows = parts * part_rows
    step = step_planes(planes)

    def body(
        spectrum_ref, observed_ref, valid_ref, columns_i, rows_i, masks_i, columns_f, rows_f, masks_f, out_ref
    ):
        for index in range(step):
            blurred = plane_inverse(read_plane(spectrum_ref, index), columns_i, rows_i, masks_i)
            mask = valid_ref[index].astype(jnp.float32)
            ratio = mask * observed_ref[index] / blurred + (1.0 - mask)
            write_plane(out_ref, index, plane_forward(ratio, columns_f, rows_f, masks_f))

    constants = tuple(
        tables[name] for name in ("columns_i", "rows_i", "masks_i", "columns_f", "rows_f", "masks_f")
    )
    block = pl.BlockSpec((parts, step, part_rows, lanes), lambda i: (0, i, 0, 0))
    plane = pl.BlockSpec((step, rows, lanes), lambda i: (i, 0, 0))
    return pl.pallas_call(
        body,
        grid=(planes // step,),
        out_shape=jax.ShapeDtypeStruct(spectrum.shape, jnp.float32),
        in_specs=[block, plane, plane] + [whole_spec(c) for c in constants],
        out_specs=block,
        interpret=INTERPRET,
        name="ratio_step",
    )(spectrum, observed, valid, *constants)


def update_step(spectrum, estimate, view_count, tables, last):
    parts, planes, part_rows, lanes = spectrum.shape
    rows = parts * part_rows
    step = step_planes(planes)

    def body(spectrum_ref, estimate_ref, columns_i, rows_i, masks_i, columns_f, rows_f, masks_f, *outs):
        for index in range(step):
            combined = plane_inverse(read_plane(spectrum_ref, index), columns_i, rows_i, masks_i)
            updated = estimate_ref[index] * combined / view_count
            outs[0][index] = updated
            if not last:
                write_plane(outs[1], index, plane_forward(updated, columns_f, rows_f, masks_f))

    constants = tuple(
        tables[name] for name in ("columns_i", "rows_i", "masks_i", "columns_f", "rows_f", "masks_f")
    )
    block = pl.BlockSpec((parts, step, part_rows, lanes), lambda i: (0, i, 0, 0))
    plane = pl.BlockSpec((step, rows, lanes), lambda i: (i, 0, 0))
    shapes = [
        jax.ShapeDtypeStruct(estimate.shape, jnp.float32),
        jax.ShapeDtypeStruct(spectrum.shape, jnp.float32),
    ]
    count = 1 if last else 2
    return pl.pallas_call(
        body,
        grid=(planes // step,),
        out_shape=shapes[:count],
        in_specs=[block, plane] + [whole_spec(c) for c in constants],
        out_specs=[plane, block][:count],
        interpret=INTERPRET,
        name="update_step",
    )(spectrum, estimate, *constants)


def depth_step(pieces, transfer, forward, inverse, out_planes, adjoint):
    parts, _, rows, lanes = pieces[0].shape
    half = lanes // 2
    block_rows = 8
    depth = sum(p.shape[1] for p in pieces) * parts
    main, cross = transfer
    in_count = len(pieces)

    def body(*refs):
        ins = refs[:in_count]
        main_ref, cross_ref, forward_ref, inverse_ref = refs[in_count : in_count + 4]
        outs = refs[in_count + 4 :]
        lane = lax.broadcasted_iota(jnp.int32, (depth, lanes), 1)
        sign = jnp.where(lane < half, 1.0, -1.0)
        side = -1.0 if adjoint else 1.0
        for pair in range(block_rows // 2):
            columns = []
            for k in (2 * pair, 2 * pair + 1):
                columns.append(
                    jnp.concatenate(
                        [
                            ref.reshape(parts * ref.shape[1] * block_rows, lanes)[
                                pl.ds(k, parts * ref.shape[1], stride=block_rows), :
                            ]
                            for ref in ins
                        ],
                        axis=0,
                    )
                )
            both = jnp.concatenate(columns, axis=1)
            grown = fold_rows(dot(forward_ref[...], jnp.concatenate(split(both), axis=0)))
            results = []
            for index in range(2):
                k = 2 * pair + index
                lanes_of = slice(index * lanes, (index + 1) * lanes)
                cos_part, sin_part = grown[:depth, lanes_of], grown[depth:, lanes_of]
                sin_roll = pltpu.roll(sin_part, half, 1)
                spectrum = cos_part + sign * sin_roll
                result = (
                    spectrum * main_ref[0, k]
                    + pltpu.roll(spectrum, half, 1) * main_ref[1, k] * side
                )
                if k == 0:
                    mirrored = sign * cos_part - sin_roll
                    extra = (
                        mirrored * cross_ref[0]
                        + pltpu.roll(mirrored, half, 1) * cross_ref[1] * side
                    )
                    result = result + jnp.where(pl.program_id(0) == 0, extra, 0.0)
                results.append(result)
            both = jnp.concatenate(results, axis=1)
            grown = fold_rows(dot(inverse_ref[...], jnp.concatenate(split(both), axis=0)))
            for index in range(2):
                k = 2 * pair + index
                lanes_of = slice(index * lanes, (index + 1) * lanes)
                cos_part, sin_part = grown[:depth, lanes_of], grown[depth:, lanes_of]
                volume = cos_part - sign * pltpu.roll(sin_part, half, 1)
                start = 0
                for ref in outs:
                    count = parts * ref.shape[1]
                    ref.reshape(count * block_rows, lanes)[
                        pl.ds(k, count, stride=block_rows), :
                    ] = volume[start : start + count]
                    start += count

    def piece_spec(planes):
        return pl.BlockSpec((parts, planes, block_rows, lanes), lambda i: (0, 0, i, 0))

    return pl.pallas_call(
        body,
        grid=(rows // block_rows,),
        out_shape=[jax.ShapeDtypeStruct((parts, n, rows, lanes), jnp.float32) for n in out_planes],
        in_specs=[piece_spec(p.shape[1]) for p in pieces]
        + [
            pl.BlockSpec((2, block_rows, depth, lanes), lambda i: (0, i, 0, 0)),
            whole_spec(cross),
            whole_spec(forward),
            whole_spec(inverse),
        ],
        out_specs=[piece_spec(n) for n in out_planes],
        interpret=INTERPRET,
        name="depth_step",
    )(*pieces, main, cross, forward, inverse)


def transfer_tables(psf, space_count):
    half = psf.shape[-1] // 2
    device = lax.axis_index("space")
    upper = device >= space_count // 2
    special = (device % (space_count // 2)) == 0
    pairs = [(0, space_count // 2), (space_count // 2, 0)]
    own = jnp.where(upper, psf[:, :, 0, half], psf[:, :, 0, 0])
    given = jnp.where(upper, psf[:, :, 0, 0], psf[:, :, 0, half])
    other = lax.ppermute(given, "space", pairs)
    mean = jnp.where(special, 0.5 * (own + other), own)
    cross = jnp.where(special, 0.5 * (own - other), jnp.zeros_like(own))
    column = jnp.where(upper, psf[..., half], psf[..., 0])
    first_row = lax.broadcasted_iota(jnp.int32, column.shape, 2) == 0
    column = jnp.where(first_row, mean[:, :, None], column)
    first_lane = lax.broadcasted_iota(jnp.int32, psf.shape[:3] + (half,), 3) == 0
    packed = jnp.where(first_lane, column[..., None], psf[..., :half])
    packed = packed.transpose(0, 2, 1, 3)
    main = jnp.stack(
        [
            jnp.concatenate([packed[0], packed[0]], axis=-1),
            jnp.concatenate([-packed[1], packed[1]], axis=-1),
        ]
    )
    lane = lax.broadcasted_iota(jnp.int32, (psf.shape[1], 2 * half), 1)
    cross = jnp.stack(
        [
            jnp.where(lane % half == 0, cross[0][:, None], 0.0),
            jnp.where(lane == 0, -cross[1][:, None], jnp.where(lane == half, cross[1][:, None], 0.0)),
        ]
    )
    return main, cross


def exchange(array):
    return lax.all_to_all(array, "space", split_axis=0, concat_axis=0, tiled=True)


def partner(array, count, stride):
    return lax.ppermute(array, "view", [(i, i ^ stride) for i in range(count)])


def shards(estimate, observed, valid, psf_spectrum):
    space_count = lax.axis_size("space")
    views = lax.axis_size("view")
    planes, row_total, lanes = estimate.shape
    depth_total = planes * space_count
    view_count = views * observed.shape[0]
    columns_f, columns_i = column_tables(lanes, 1.0 / (depth_total * row_total * lanes))
    rows_f, rows_i, masks_f, masks_i = row_tables(row_total, lanes)
    tables = {
        "columns_f": jnp.asarray(columns_f),
        "columns_i": jnp.asarray(columns_i),
        "rows_f": jnp.asarray(rows_f),
        "rows_i": jnp.asarray(rows_i),
        "masks_f": jnp.asarray(masks_f),
        "masks_i": jnp.asarray(masks_i),
    }
    observed, valid = observed[0], valid[0]
    transfer = transfer_tables(psf_spectrum[0], space_count)

    shared = planes % views == 0 and views & (views - 1) == 0
    blocks = views if shared else 1
    share = planes // blocks
    strides = []
    while 1 << len(strides) < blocks:
        strides.append(1 << len(strides))
    flips = [0]
    for stride in reversed(strides):
        flips = flips + [f ^ stride for f in flips]
    slabs = np.arange(space_count)[:, None] * planes

    def order_of(starts, count):
        return np.concatenate([(slabs + start + np.arange(count)[None, :]).reshape(-1) for start in starts])

    if shared:
        me = lax.axis_index("view")
        view_orders = [order_of([(v ^ f) * share for f in flips], share) for v in range(views)]
        view_forward = jnp.asarray(np.stack([depth_forward(o) for o in view_orders]))[me]
        view_inverse = jnp.asarray(np.stack([depth_inverse(o) for o in view_orders]))[me]
        own = lax.dynamic_slice_in_dim(estimate, me * share, share, 0)
    else:
        view_forward = jnp.asarray(depth_forward(order_of([0], planes)))
        view_inverse = jnp.asarray(depth_inverse(order_of([0], planes)))
        own = estimate
    slab_forward = jnp.asarray(depth_forward(order_of([0], planes)))
    slab_inverse = jnp.asarray(depth_inverse(order_of([0], planes)))

    spectrum = lateral_forward(own, tables, space_count)
    for iteration in range(ITERS):
        last = iteration == ITERS - 1
        pieces = [exchange(spectrum)]
        for stride in reversed(strides):
            pieces = pieces + [partner(p, views, stride) for p in pieces]
        (blurred,) = depth_step(pieces, transfer, view_forward, slab_inverse, [planes], False)
        ratios = ratio_step(exchange(blurred), observed, valid, tables)
        parts = depth_step(
            [exchange(ratios)], transfer, slab_forward, view_inverse, [share] * blocks, True
        )
        if shared:
            for stride in strides:
                middle = len(parts) // 2
                moved = [partner(p, views, stride) for p in parts[middle:]]
                parts = [kept + new for kept, new in zip(parts[:middle], moved)]
            total = parts[0]
        else:
            total = lax.psum(parts[0], "view")
        results = update_step(exchange(total), own, float(view_count), tables, last)
        own = results[0]
        if not last:
            spectrum = results[1]
    if shared:
        own = lax.all_gather(own, "view", axis=0, tiled=True)
    return own


def solution(mesh):
    return jax.shard_map(
        shards,
        mesh=mesh,
        in_specs=(
            P("space", "blocks", None),
            P("view", "space", "blocks", None),
            P("view", "space", "blocks", None),
            P("view", None, None, "space", None),
        ),
        out_specs=P("space", "blocks", None),
        check_vma=False,
    )
```

time: 1110 us -> 498 us (0.45)
  waiting for transfers between devices: 384 us -> 118 us
  matrix products: 202 us -> 0 us
  blocking collectives: 413 us -> 211 us
  Pallas kernels: 0 us -> 87.7 us
  local copies, waits for them, and re-layouts: 62 us -> 24 us
  other arithmetic: 8.23 us -> 20.6 us
    dot_general x80 -> x0, matrix products: 202 us -> none  [the longest x32 78.5 us: along_columns(): jnp.einsum('zxy,yk->zxk', volume, matrix, precision=HIGHEST, preferred_el...]
    all_to_all x5 -> x6, blocking collectives: 413 us -> 211 us  [exchange(): lax.all_to_all(array, 'space', split_axis=0, concat_axis=0, tiled=True)]
    all_to_all x3 -> x2, waiting for transfers between devices: 201 us -> 46.4 us  [exchange(): lax.all_to_all(array, 'space', split_axis=0, concat_axis=0, tiled=True)]
    psum x2 -> x0, waiting for transfers between devices: 96 us -> none  [shards(): combined = lax.psum(partial_value, 'view')]
    pallas_call x0 -> x9, Pallas kernels: none -> 87.7 us  [the longest x4 40.9 us: depth_step(): pl.pallas_call(body, grid=(rows // block_rows,), out_shape=[jax.ShapeDtyp...]
    unnamed x6 -> x1, waiting for transfers between devices: 87 us -> 0.02 us
    ppermute x0 -> x13, waiting for transfers between devices: none -> 50.2 us  [the longest x12 50.2 us: partner(): return lax.ppermute(array, 'view', [(i, i ^ stride) for i in range(count)])]
    all_gather x0 -> x1, waiting for transfers between devices: none -> 21.8 us  [shards(): own = lax.all_gather(own, 'view', axis=0, tiled=True)]
  transfers between devices with their start and end apart: 7 -> 16, of which waited for: 7 -> 9; matrix products, arithmetic and copies ran while one was open for 1% -> 5% of each run, Pallas kernels for 0% -> 1%
where the time goes in v1:
time: 498 us; the launch traced here: 496 us
  blocking collectives  211 us (42%)
  waiting for transfers between devices  118 us (24%)
  Pallas kernels  87.7 us (18%)
  local copies, waits for them, and re-layouts  24 us (5%)
  other arithmetic  20.6 us (4%)
  starting transfers between devices  20.4 us (4%)
  between operations  13.7 us (3%)
    all_to_all x6, blocking collectives, exchange(): lax.all_to_all(array, 'space', split_axis=0, concat_axis=0, tiled=True)  211 us
    ppermute x12, waiting for transfers between devices, partner(): return lax.ppermute(array, 'view', [(i, i ^ stride) for i in range(count)])  50.2 us
    all_to_all x2, waiting for transfers between devices, exchange(): lax.all_to_all(array, 'space', split_axis=0, concat_axis=0, tiled=True)  46.4 us
    pallas_call x4, Pallas kernels, depth_step(): pl.pallas_call(body, grid=(rows // block_rows,), out_shape=[jax.ShapeDtyp...  40.9 us
    pallas_call x2, Pallas kernels, ratio_step(): pl.pallas_call(body, grid=(planes // step,), out_shape=jax.ShapeDtypeStru...  32.9 us
    all_gather x1, waiting for transfers between devices, shards(): own = lax.all_gather(own, 'view', axis=0, tiled=True)  21.8 us
    unnamed x24, local copies, waits for them, and re-layouts  14.7 us
    pallas_call x2, Pallas kernels, update_step(): pl.pallas_call(body, grid=(planes // step,), out_shape=shapes[:count], in...  10.4 us
  transfers between devices with their start and end apart: 16, of which 9 were waited for; matrix products, arithmetic and copies ran while one was open for 5% of the time, Pallas kernels for 1%

profile of v1, /device:TPU:0, one launch (start us, length us, event | category | flops | bytes accessed | tf_op | source)
XLA Modules:
  0.0 495.7 jit_solution(14935601281125718513)
XLA Ops:
  6.5 6.7 %copy.24 = f32[1,2,64,64,128]{4,2,3,1,0:T(8,128)} copy(f32[1,2,64,64,128]{4,3,2,1,0:T(8,128)} %param.17) | data formatting | bytes 8388608 | tf_op args[3]
  14.4 6.0 %collective-permute-start.3 = (f32[2,64]{1,0:T(2,128)S(1)}, f32[2,64]{1,0:T(2,128)S(1)}, u32[]{:S(2)}, u32[]{:S(2)}) collective-permute-start(f32[2,64]{1,0:T(2,128)S(1)} %get-tuple-element.25), channel_id=1, source_target_pairs={{0,8},{8,0},{1,9},{9,1},{2,10},{10,2},{3,11},{11,3},{16,24},{24,16... | collective-permute-start | bytes 1544 | tf_op jit(solution)/shard_map/ppermute | solution.py:341
  21.2 3.5 lateral_forward.1
  24.7 3.5 all-to-all-start
  29.7 6.9 %fusion.1 = f32[2,64,64,1]{3,1,2,0:T(8,128)} fusion(f32[2,64,64,128]{3,1,2,0:T(8,128)} %bitcast.30, f32[2,64]{1,0:T(2,128)S(1)} %get-tuple-element.30, pred[64]{0:T(512)(128)(4,1)S(1)} %iota_compare_fusion.2, pred[]{:T(512)S(6)} %ge.3), kind=kLoop, calls=%fused_computation.3 | loop fusion | flops 16384 | bytes 98881 | tf_op jit(solution)/shard_map/jit(_where)/select_n | solution.py:346
  36.7 3.0 copy.22
  39.7 3.6 fusion
  43.3 2.0 copy-done.2
  47.1 2.5 slice_bitcast_fusion.1
  49.8 9.2 %collective-permute-done.refs_1_ = f32[4,4,64,128]{3,2,1,0:T(8,128)S(1)} collective-permute-done((f32[4,4,64,128]{3,2,1,0:T(8,128)S(1)}, f32[4,4,64,128]{3,2,1,0:T(8,128)S(1)}, u32[]{:S(2)}, u32[]{:S(2)}) %collective-permute-start) | collective-permute-done | bytes 524320 | tf_op jit(solution)/shard_map/ppermute | solution.py:371
  60.8 2.3 pad_maximum_fusion.refs_4_.refs_1_
  63.9 10.3 %depth_step.4 = f32[4,16,64,128]{3,2,1,0:T(8,128)} custom-call(f32[4,4,64,128]{3,2,1,0:T(8,128)} %copy-done.4, f32[4,4,64,128]{3,2,1,0:T(8,128)} %copy-done.6, f32[4,4,64,128]{3,2,1,0:T(8,128)} %copy-done.7, f32[4,4,64,128]{3,2,1,0:T(8,128)} %collective-permute-done.2.refs_3_, f32[2,64,64,128]{3,2,1,0:T(8,128)} %pad_maximum_fusion.refs_4_.refs_1_, ...), custom_call_target="tpu_custom_call" | custom-call | tf_op jit(solution)/shard_map/depth_step/pallas_call | solution.py:316
  74.2 53.7 %all_to_all.40.spectrum_ref = f32[4,16,64,128]{3,2,1,0:T(8,128)} all-to-all(f32[4,16,64,128]{3,2,1,0:T(8,128)} %depth_step.4), channel_id=1, replica_groups=mesh['blocks'=2,'space'=4,'view'=4] {'space'}, dimensions={0} | all-to-all | bytes 4194304 | tf_op jit(solution)/shard_map/all_to_all | solution.py:367
  127.9 16.4 %ratio_step.2 = f32[4,16,64,128]{3,2,1,0:T(8,128)} custom-call(f32[4,16,64,128]{3,2,1,0:T(8,128)} %all_to_all.40.spectrum_ref, f32[16,256,128]{2,1,0:T(8,128)} %bitcast.32, s32[16,256,128]{2,1,0:T(8,128)} %bitcast.34, bf16[256,256]{1,0:T(8,128)(2,1)} %constant.68.clone.columns_i, bf16[512,512]{1,0:T(8,128)(2,1)} %constant.70.clone.rows_i, ...), custom_call_target="tpu_custom_call" | custom-call | tf_op jit(solution)/shard_map/ratio_step/pallas_call | solution.py:203
  144.3 3.6 all-to-all-start.2
  149.5 46.4 %all-to-all-done.2.refs_0_ = f32[4,16,64,128]{3,2,1,0:T(8,128)S(1)} async-done(((f32[4,16,64,128]{3,2,1,0:T(8,128)}), f32[4,16,64,128]{3,2,1,0:T(8,128)S(1)}, u32[]{:S(2)}, u32[]{:S(2)}) %all-to-all-start.2) | async-done | bytes 2097184 | tf_op jit(solution)/shard_map/all_to_all | solution.py:367
  197.2 10.2 %depth_step.5 = (f32[4,4,64,128]{3,2,1,0:T(8,128)}, f32[4,4,64,128]{3,2,1,0:T(8,128)}, f32[4,4,64,128]{3,2,1,0:T(8,128)}, f32[4,4,64,128]{3,2,1,0:T(8,128)}) custom-call(f32[4,16,64,128]{3,2,1,0:T(8,128)} %copy-done.3, f32[2,64,64,128]{3,2,1,0:T(8,128)} %pad_maximum_fusion.refs_4_.refs_1_, f32[2,64,128]{2,1,0:T(8,128)} %pad_maximum_fusion.1.refs_5_.refs_2_, ...), custom_call_target="tpu_custom_call" | custom-call | tf_op jit(solution)/shard_map/depth_step/pallas_call | solution.py:316
  212.2 12.5 %collective-permute-done.6 = f32[4,4,64,128]{3,2,1,0:T(8,128)S(1)} collective-permute-done((f32[4,4,64,128]{3,2,1,0:T(8,128)S(1)}, f32[4,4,64,128]{3,2,1,0:T(8,128)S(1)}, u32[]{:S(2)}, u32[]{:S(2)}) %collective-permute-start.6) | collective-permute-done | bytes 524320 | tf_op jit(solution)/shard_map/ppermute | solution.py:371
  225.8 17.3 %all_to_all.41.spectrum_ref = f32[4,4,64,128]{3,2,1,0:T(8,128)} all-to-all(f32[4,4,64,128]{3,2,1,0:T(8,128)S(1)} %add_add_fusion.1), channel_id=1, replica_groups=mesh['blocks'=2,'space'=4,'view'=4] {'space'}, dimensions={0} | all-to-all | bytes 1048576 | tf_op jit(solution)/shard_map/all_to_all | solution.py:367
  243.1 5.9 %update_step.2 = (f32[4,256,128]{2,1,0:T(8,128)}, f32[4,4,64,128]{3,2,1,0:T(8,128)}) custom-call(f32[4,4,64,128]{3,2,1,0:T(8,128)} %all_to_all.41.spectrum_ref, f32[4,256,128]{2,1,0:T(8,128)} %constant_dynamic-slice_fusion.volume_ref.estimate_ref, bf16[256,256]{1,0:T(8,128)(2,1)} %constant.68.clone.columns_i, bf16[512,512]{1,0:T(8,128)(2,1)} %constant.70.clone.rows_i, ...), custom_call_target="tpu_custom_call" | custom-call | tf_op jit(solution)/shard_map/update_step/pallas_call | solution.py:237
  249.0 16.9 %all_to_all.42.refs_0_ = f32[4,4,64,128]{3,2,1,0:T(8,128)S(1)} all-to-all(f32[4,4,64,128]{3,2,1,0:T(8,128)} %get-tuple-element.19), channel_id=1, replica_groups=mesh['blocks'=2,'space'=4,'view'=4] {'space'}, dimensions={0} | all-to-all | bytes 1048576 | tf_op jit(solution)/shard_map/all_to_all | solution.py:367
  267.4 11.0 %collective-permute-done.7.refs_1_ = f32[4,4,64,128]{3,2,1,0:T(8,128)S(1)} collective-permute-done((f32[4,4,64,128]{3,2,1,0:T(8,128)S(1)}, f32[4,4,64,128]{3,2,1,0:T(8,128)S(1)}, u32[]{:S(2)}, u32[]{:S(2)}) %collective-permute-start.7) | collective-permute-done | bytes 524320 | tf_op jit(solution)/shard_map/ppermute | solution.py:371
  281.1 10.3 %depth_step.6 = f32[4,16,64,128]{3,2,1,0:T(8,128)} custom-call(f32[4,4,64,128]{3,2,1,0:T(8,128)} %copy-done.5, f32[4,4,64,128]{3,2,1,0:T(8,128)} %copy-done.8, f32[4,4,64,128]{3,2,1,0:T(8,128)} %copy-done.9, f32[4,4,64,128]{3,2,1,0:T(8,128)} %copy-done.10, f32[2,64,64,128]{3,2,1,0:T(8,128)} %pad_maximum_fusion.refs_4_.refs_1_, ...), custom_call_target="tpu_custom_call" | custom-call | tf_op jit(solution)/shard_map/depth_step/pallas_call | solution.py:316
  291.4 53.2 %all_to_all.43.spectrum_ref = f32[4,16,64,128]{3,2,1,0:T(8,128)} all-to-all(f32[4,16,64,128]{3,2,1,0:T(8,128)} %depth_step.6), channel_id=1, replica_groups=mesh['blocks'=2,'space'=4,'view'=4] {'space'}, dimensions={0} | all-to-all | bytes 4194304 | tf_op jit(solution)/shard_map/all_to_all | solution.py:367
  344.6 16.4 %ratio_step.3 = f32[4,16,64,128]{3,2,1,0:T(8,128)} custom-call(f32[4,16,64,128]{3,2,1,0:T(8,128)} %all_to_all.43.spectrum_ref, f32[16,256,128]{2,1,0:T(8,128)} %bitcast.33, s32[16,256,128]{2,1,0:T(8,128)} %bitcast.35, bf16[256,256]{1,0:T(8,128)(2,1)} %constant.68.clone.columns_i, bf16[512,512]{1,0:T(8,128)(2,1)} %constant.70.clone.rows_i, ...), custom_call_target="tpu_custom_call" | custom-call | tf_op jit(solution)/shard_map/ratio_step/pallas_call | solution.py:203
  361.1 52.4 %all_to_all.44.refs_0_ = f32[4,16,64,128]{3,2,1,0:T(8,128)} all-to-all(f32[4,16,64,128]{3,2,1,0:T(8,128)} %ratio_step.3), channel_id=1, replica_groups=mesh['blocks'=2,'space'=4,'view'=4] {'space'}, dimensions={0} | all-to-all | bytes 4194304 | tf_op jit(solution)/shard_map/all_to_all | solution.py:367
  413.4 10.1 %depth_step.7 = (f32[4,4,64,128]{3,2,1,0:T(8,128)}, f32[4,4,64,128]{3,2,1,0:T(8,128)}, f32[4,4,64,128]{3,2,1,0:T(8,128)}, f32[4,4,64,128]{3,2,1,0:T(8,128)}) custom-call(f32[4,16,64,128]{3,2,1,0:T(8,128)} %all_to_all.44.refs_0_, f32[2,64,64,128]{3,2,1,0:T(8,128)} %pad_maximum_fusion.refs_4_.refs_1_, f32[2,64,128]{2,1,0:T(8,128)} %pad_maximum_fusion.1.refs_5_.refs_2_, ...), custom_call_target="tpu_custom_call" | custom-call | tf_op jit(solution)/shard_map/depth_step/pallas_call | solution.py:316
  428.4 12.5 %collective-permute-done.12 = f32[4,4,64,128]{3,2,1,0:T(8,128)S(1)} collective-permute-done((f32[4,4,64,128]{3,2,1,0:T(8,128)S(1)}, f32[4,4,64,128]{3,2,1,0:T(8,128)S(1)}, u32[]{:S(2)}, u32[]{:S(2)}) %collective-permute-start.12) | collective-permute-done | bytes 524320 | tf_op jit(solution)/shard_map/ppermute | solution.py:371
  442.0 17.3 %all_to_all.45.spectrum_ref = f32[4,4,64,128]{3,2,1,0:T(8,128)} all-to-all(f32[4,4,64,128]{3,2,1,0:T(8,128)S(1)} %add_add_fusion), channel_id=1, replica_groups=mesh['blocks'=2,'space'=4,'view'=4] {'space'}, dimensions={0} | all-to-all | bytes 1048576 | tf_op jit(solution)/shard_map/all_to_all | solution.py:367
  459.3 4.5 update_step.3
  463.9 21.8 %all-gather.2.cloned.1.call-done = f32[16,256,128]{2,1,0:T(8,128)} async-done(((f32[4,256,128]{2,1,0:T(8,128)}), f32[16,256,128]{2,1,0:T(8,128)}) %all-gather.2.cloned.1.call-update) | async-done | bytes 2097168 | tf_op jit(solution)/shard_map/all_gather | solution.py:444
  485.7 3.1 copy.26
  (65 shorter events, 27.0 us)
Async XLA Ops:
  6.5 13.8 %copy-start = (f32[16,256,128]{2,1,0:T(8,128)S(1)}, f32[16,256,128]{2,1,0:T(8,128)}, u32[]{:S(2)}) copy-start(f32[16,256,128]{2,1,0:T(8,128)} %param.14) | copy-start | bytes 6291460
  14.4 15.3 %collective-permute-start.3 = (f32[2,64]{1,0:T(2,128)S(1)}, f32[2,64]{1,0:T(2,128)S(1)}, u32[]{:S(2)}, u32[]{:S(2)}) collective-permute-start(f32[2,64]{1,0:T(2,128)S(1)} %get-tuple-element.25), channel_id=1, source_target_pairs={{0,8},{8,0},{1,9},{9,1},{2,10},{10,2},{3,11},{11,3},{16,24},{24,16... | collective-permute-start | bytes 1544 | tf_op jit(solution)/shard_map/ppermute | solution.py:341
  24.7 20.8 %all-to-all-start = ((f32[4,4,64,128]{3,2,1,0:T(8,128)}), f32[4,4,64,128]{3,2,1,0:T(8,128)S(1)}, u32[]{:S(2)}, u32[]{:S(2)}) async-start(f32[4,4,64,128]{3,2,1,0:T(8,128)} %lateral_forward.1), calls=%async_computation | async-start | bytes 1048576 | tf_op jit(solution)/shard_map/all_to_all | solution.py:367
  43.3 2.0 copy-start.2
  45.5 4.2 copy-start.4
  45.5 13.4 %collective-permute-start = (f32[4,4,64,128]{3,2,1,0:T(8,128)S(1)}, f32[4,4,64,128]{3,2,1,0:T(8,128)S(1)}, u32[]{:S(2)}, u32[]{:S(2)}) collective-permute-start(f32[4,4,64,128]{3,2,1,0:T(8,128)S(1)} %all-to-all-done.refs_0_), channel_id=1, source_target_pairs={{0,2},{1,3},{2,0},{3,1},{4,6},{5,7},{6,4},{7,5},{8,10},{9,11},{10,... | collective-permute-start | bytes 1572872 | tf_op jit(solution)/shard_map/ppermute | solution.py:371
  49.7 13.4 %collective-permute-start.1 = (f32[4,4,64,128]{3,2,1,0:T(8,128)S(1)}, f32[4,4,64,128]{3,2,1,0:T(8,128)S(1)}, u32[]{:S(2)}, u32[]{:S(2)}) collective-permute-start(f32[4,4,64,128]{3,2,1,0:T(8,128)S(1)} %all-to-all-done.refs_0_), channel_id=1, source_target_pairs={{0,1},{1,0},{2,3},{3,2},{4,5},{5,4},{6,7},{7,6},{8,9},{9,8},{10,11... | collective-permute-start | bytes 1572872 | tf_op jit(solution)/shard_map/ppermute | solution.py:371
  59.0 1.9 copy-start.6
  59.0 5.0 %collective-permute-start.2 = (f32[4,4,64,128]{3,2,1,0:T(8,128)S(1)}, f32[4,4,64,128]{3,2,1,0:T(8,128)}, u32[]{:S(2)}, u32[]{:S(2)}) collective-permute-start(f32[4,4,64,128]{3,2,1,0:T(8,128)S(1)} %collective-permute-done.refs_1_), channel_id=1, source_target_pairs={{0,1},{1,0},{2,3},{3,2},{4,5},{5,4},{6,7},{7,6},{8,9},{9,8},{10,11... | collective-permute-start | bytes 1572872 | tf_op jit(solution)/shard_map/ppermute | solution.py:371
  63.1 0.8 copy-start.7
  144.3 51.5 %all-to-all-start.2 = ((f32[4,16,64,128]{3,2,1,0:T(8,128)}), f32[4,16,64,128]{3,2,1,0:T(8,128)S(1)}, u32[]{:S(2)}, u32[]{:S(2)}) async-start(f32[4,16,64,128]{3,2,1,0:T(8,128)} %ratio_step.2), calls=%async_computation.2 | async-start | bytes 4194304 | tf_op jit(solution)/shard_map/all_to_all | solution.py:367
  147.9 337.8 %all-gather.2.cloned.1.call-start = ((), (), s32[]{:S(2)}) async-start(), calls=%async_computation.8 | async-start | bytes 2621440 | tf_op jit(solution)/shard_map/all_gather | solution.py:444
  195.9 1.3 copy-start.3
  207.4 2.1 collective-permute-start.5
  207.4 4.8 collective-permute-start.4
  210.6 14.0 %collective-permute-start.6 = (f32[4,4,64,128]{3,2,1,0:T(8,128)S(1)}, f32[4,4,64,128]{3,2,1,0:T(8,128)S(1)}, u32[]{:S(2)}, u32[]{:S(2)}) collective-permute-start(f32[4,4,64,128]{3,2,1,0:T(8,128)S(1)} %add.45), channel_id=1, source_target_pairs={{0,2},{1,3},{2,0},{3,1},{4,6},{5,7},{6,4},{7,5},{8,10},{9,11},{10,... | collective-permute-start | bytes 1572872 | tf_op jit(solution)/shard_map/ppermute | solution.py:371
  265.9 14.4 %copy-start.5 = (f32[4,4,64,128]{3,2,1,0:T(8,128)}, f32[4,4,64,128]{3,2,1,0:T(8,128)S(1)}, u32[]{:S(2)}) copy-start(f32[4,4,64,128]{3,2,1,0:T(8,128)S(1)} %all_to_all.42.refs_0_) | copy-start | bytes 1572868
  265.9 12.5 %collective-permute-start.7 = (f32[4,4,64,128]{3,2,1,0:T(8,128)S(1)}, f32[4,4,64,128]{3,2,1,0:T(8,128)S(1)}, u32[]{:S(2)}, u32[]{:S(2)}) collective-permute-start(f32[4,4,64,128]{3,2,1,0:T(8,128)S(1)} %all_to_all.42.refs_0_), channel_id=1, source_target_pairs={{0,2},{1,3},{2,0},{3,1},{4,6},{5,7},{6,4},{7,5},{8,10},{9,11},{10,... | collective-permute-start | bytes 1572872 | tf_op jit(solution)/shard_map/ppermute | solution.py:371
  267.4 11.0 %collective-permute-start.8 = (f32[4,4,64,128]{3,2,1,0:T(8,128)S(1)}, f32[4,4,64,128]{3,2,1,0:T(8,128)S(1)}, u32[]{:S(2)}, u32[]{:S(2)}) collective-permute-start(f32[4,4,64,128]{3,2,1,0:T(8,128)S(1)} %all_to_all.42.refs_0_), channel_id=1, source_target_pairs={{0,1},{1,0},{2,3},{3,2},{4,5},{5,4},{6,7},{7,6},{8,9},{9,8},{10,11... | collective-permute-start | bytes 1572872 | tf_op jit(solution)/shard_map/ppermute | solution.py:371
  278.4 1.9 copy-start.8
  278.4 1.9 collective-permute-start.9
  278.4 1.9 copy-start.9
  280.3 0.8 copy-start.10
  423.6 2.2 collective-permute-start.11
  423.6 4.8 collective-permute-start.10
  426.8 14.0 %collective-permute-start.12 = (f32[4,4,64,128]{3,2,1,0:T(8,128)S(1)}, f32[4,4,64,128]{3,2,1,0:T(8,128)S(1)}, u32[]{:S(2)}, u32[]{:S(2)}) collective-permute-start(f32[4,4,64,128]{3,2,1,0:T(8,128)S(1)} %add.48), channel_id=1, source_target_pairs={{0,2},{1,3},{2,0},{3,1},{4,6},{5,7},{6,4},{7,5},{8,10},{9,11},{10,... | collective-permute-start | bytes 1572872 | tf_op jit(solution)/shard_map/ppermute | solution.py:371
  463.9 24.9 %copy-start.1 = (f32[16,256,128]{2,1,0:T(8,128)S(1)}, f32[16,256,128]{2,1,0:T(8,128)}, u32[]{:S(2)}) copy-start(f32[16,256,128]{2,1,0:T(8,128)} %param.14) | copy-start | bytes 6291460
Sparse Core Ops, SparseCore 0:
  464.0 21.6 all-gather.1

commit v2 on v1

v2 whole, which is shorter than its diff:
```python
import functools

import jax
import jax.numpy as jnp
import ml_dtypes
import numpy as np
from jax import lax
from jax.experimental import pallas as pl
from jax.experimental.pallas import tpu as pltpu
from jax.sharding import PartitionSpec as P

ITERS = 2
INTERPRET = False


def split_np(matrix):
    high = matrix.astype(ml_dtypes.bfloat16)
    low = (matrix - high.astype(np.float64)).astype(ml_dtypes.bfloat16)
    return high, low


def angles_np(length):
    index = np.arange(length)
    return (np.outer(index, index) % length) * (2.0 * np.pi / length)


def column_tables(length, scale):
    half = length // 2
    angles = angles_np(length)
    cosines, sines = np.cos(angles), np.sin(angles)
    alternating = np.where(np.arange(length) % 2 == 0, 1.0, -1.0)
    forward = np.zeros((length, length))
    forward[:, :half] = cosines[:, :half]
    forward[:, half:] = -sines[:, :half]
    forward[:, half] = alternating
    inverse = np.zeros((length, length))
    inverse[:half] = 2.0 * cosines[:half]
    inverse[half:] = -2.0 * sines[:half]
    inverse[0] = 1.0
    inverse[half] = alternating
    inverse *= scale
    tables = []
    for matrix in (forward, inverse):
        high, low = split_np(matrix)
        both = np.concatenate([high, low], axis=1)
        tables.append(np.concatenate([both, both], axis=0))
    return tables


def row_tables(length, lanes):
    middle, half = length // 2, lanes // 2
    angles = angles_np(length)
    cosines, sines = np.cos(angles), np.sin(angles)
    sines[0] = -cosines[middle]
    sines[middle] = -cosines[0]
    high, low = split_np(np.concatenate([cosines, sines], axis=0))
    forward = np.concatenate([high, low], axis=0)
    high, low = split_np(np.concatenate([cosines.T, sines.T], axis=1))
    inverse = np.concatenate([high, low], axis=0)
    row = np.arange(length)[:, None]
    lane = np.arange(lanes)[None, :]
    plain = (lane % half) != 0
    lower = row < middle
    inner = (row % middle) != 0
    first, second = lane == 0, lane == half
    sign = np.where(lane < half, 1.0, -1.0)
    weight = np.where(inner, 2.0, 1.0)
    one = np.ones((length, lanes))
    forward_masks = np.stack(
        [
            one * (plain | (first & lower)),
            one * (first & ~lower),
            -one * (second & ~lower),
            sign * (plain & inner) - one * (second & lower),
        ]
    )
    inverse_masks = np.stack(
        [
            one * plain + weight * (first & lower),
            weight * (second & ~lower),
            -weight * (second & ~lower),
            -sign * (plain & inner) - weight * (first & lower),
        ]
    )
    return forward, inverse, forward_masks.astype(np.float32), inverse_masks.astype(np.float32)


def split(value):
    high = value.astype(jnp.bfloat16)
    low = (value - high.astype(jnp.float32)).astype(jnp.bfloat16)
    return high, low


def dot(left, right):
    return lax.dot_general(
        left, right, (((1,), (0,)), ((), ())), preferred_element_type=jnp.float32
    )


def fold_lanes(value):
    lanes = value.shape[1] // 2
    return value[:, :lanes] + value[:, lanes:]


def fold_rows(value):
    rows = value.shape[0] // 2
    return value[:rows] + value[rows:]


def plane_forward(plane, columns, rows, masks):
    step = fold_lanes(dot(jnp.concatenate(split(plane), axis=1), columns[...]))
    both = fold_lanes(fold_rows(dot(rows[...], jnp.concatenate(split(step), axis=1))))
    count, half = both.shape[0] // 2, both.shape[1] // 2
    cos_part, sin_part = both[:count], both[count:]
    return (
        cos_part * masks[0]
        + pltpu.roll(cos_part, half, 1) * masks[1]
        + sin_part * masks[2]
        + pltpu.roll(sin_part, half, 1) * masks[3]
    )


def plane_inverse(spectrum, columns, rows, masks):
    rolled = pltpu.roll(spectrum, spectrum.shape[1] // 2, 1)
    both = jnp.concatenate(
        [spectrum * masks[0] + rolled * masks[1], spectrum * masks[2] + rolled * masks[3]], axis=0
    )
    step = fold_lanes(fold_rows(dot(rows[...], jnp.concatenate(split(both), axis=1))))
    return fold_lanes(dot(jnp.concatenate(split(step), axis=1), columns[...]))


def depth_table(order, depth, inverse):
    frequency = jnp.arange(depth, dtype=jnp.int32)
    if inverse:
        phases = order[:, None] * frequency[None, :] % depth
    else:
        phases = frequency[:, None] * order[None, :] % depth
    angles = phases.astype(jnp.float32) * (2.0 * np.pi / depth)
    matrix = jnp.concatenate([jnp.cos(angles), jnp.sin(angles)], axis=0)
    high = lax.reduce_precision(matrix, 8, 7)
    both = jnp.concatenate([high, matrix - high], axis=0)
    return jnp.concatenate([both, both], axis=1).astype(jnp.bfloat16)


def whole_spec(array):
    rank = array.ndim
    return pl.BlockSpec(array.shape, lambda *_: (0,) * rank)


def start_of(device_ref, k, count):
    return pl.multiple_of(jnp.bitwise_xor(device_ref[0], k) * count, count)


def gather_rows(device_ref, refs, index, scratch):
    count = refs[0].shape[1]
    for k, ref in enumerate(refs):
        scratch[index, pl.ds(start_of(device_ref, k, count), count), :] = ref[index]
    return scratch[index]


def scatter_rows(device_ref, refs, index, scratch, value):
    count = refs[0].shape[1]
    scratch[index] = value
    for k, ref in enumerate(refs):
        ref[index] = scratch[index, pl.ds(start_of(device_ref, k, count), count), :]


def lateral_call(body, name, planes, rows, lanes, parts, device, operands, offsets, pieces, constants, out_planes, out_pieces):
    step = 2 if planes % 2 == 0 else 1
    count = rows // parts
    piece = pl.BlockSpec((step, count, lanes), lambda i, *_: (i, 0, 0))
    plane = pl.BlockSpec((step, rows, lanes), lambda i, *_: (i, 0, 0))

    def plane_at(offset):
        return pl.BlockSpec((step, rows, lanes), lambda i, *_: (i + offset // step, 0, 0))

    def kernel(device_ref, *refs):
        spans = np.cumsum([0, len(operands), len(pieces), len(constants), out_planes, out_pieces, 2])
        groups = [refs[a:b] for a, b in zip(spans[:-1], spans[1:])]
        for index in range(step):
            body(device_ref, index, *groups)

    return pl.pallas_call(
        kernel,
        grid_spec=pltpu.PrefetchScalarGridSpec(
            num_scalar_prefetch=1,
            grid=(planes // step,),
            in_specs=[plane_at(o) for o in offsets]
            + [piece] * len(pieces)
            + [whole_spec(c) for c in constants],
            out_specs=[plane] * out_planes + [piece] * out_pieces,
            scratch_shapes=[pltpu.VMEM((step, rows, lanes), jnp.float32)] * 2,
        ),
        out_shape=[jax.ShapeDtypeStruct((planes, rows, lanes), jnp.float32)] * out_planes
        + [jax.ShapeDtypeStruct((planes, count, lanes), jnp.float32)] * out_pieces,
        interpret=INTERPRET,
        name=name,
    )(device, *operands, *pieces, *constants)


def lateral_forward(volume, device, tables, parts):
    planes, rows, lanes = volume.shape

    def body(device_ref, index, ins, _, constants, __, outs, scratch):
        value = plane_forward(ins[0][index], *constants)
        scatter_rows(device_ref, outs, index, scratch[0], value)

    return lateral_call(
        body, "lateral_forward", planes, rows, lanes, parts, device,
        [volume], [0], [], tables["forward"], 0, parts,
    )


def ratio_step(pieces, observed, valid, offset, device, tables):
    planes, part_rows, lanes = pieces[0].shape
    parts = len(pieces)

    def body(device_ref, index, ins, spectrum, constants, _, outs, scratch):
        value = gather_rows(device_ref, spectrum, index, scratch[0])
        blurred = plane_inverse(value, *constants[:3])
        mask = ins[1][index].astype(jnp.float32)
        ratio = mask * ins[0][index] / blurred + (1.0 - mask)
        value = plane_forward(ratio, *constants[3:])
        scatter_rows(device_ref, outs, index, scratch[1], value)

    return lateral_call(
        body, "ratio_step", planes, parts * part_rows, lanes, parts, device,
        [observed, valid], [offset, offset], pieces, tables["inverse"] + tables["forward"], 0, parts,
    )


def update_step(pieces, estimate, view_count, device, tables, last):
    planes, part_rows, lanes = pieces[0].shape
    parts = len(pieces)

    def body(device_ref, index, ins, spectrum, constants, planes_out, outs, scratch):
        value = gather_rows(device_ref, spectrum, index, scratch[0])
        combined = plane_inverse(value, *constants[:3])
        updated = ins[0][index] * combined / view_count
        planes_out[0][index] = updated
        if not last:
            value = plane_forward(updated, *constants[3:])
            scatter_rows(device_ref, outs, index, scratch[1], value)

    constants = tables["inverse"] + (() if last else tables["forward"])
    results = lateral_call(
        body, "update_step", planes, parts * part_rows, lanes, parts, device,
        [estimate], [0], pieces, constants, 1, 0 if last else parts,
    )
    return results[0], results[1:]


BLOCK_ROWS = 8


def rows_of(ref, k):
    planes, count, lanes = ref.shape
    return ref.reshape(planes * count, lanes).at[pl.ds(k, planes, stride=count), :]


def depth_step(pieces, added, transfer, forward, inverse, out_planes, keep, adjoint, depth):
    main, cross = transfer
    _, rows, _, lanes = main.shape
    half = lanes // 2
    block = BLOCK_ROWS
    stored = pl.BlockSpec((block, depth, lanes), lambda i: (i, 0, 0))
    operands, specs = [], []

    def piece_spec(planes):
        return pl.BlockSpec((planes, block, lanes), lambda i: (0, i, 0))

    for piece in pieces:
        operands.append(piece)
        specs.append(piece_spec(piece.shape[0]))
    if pieces:
        operands += [main, cross, forward]
        specs += [
            pl.BlockSpec((2, block, depth, lanes), lambda i: (0, i, 0, 0)),
            whole_spec(cross),
            whole_spec(forward),
        ]
    if added is not None:
        operands.append(added)
        specs.append(stored)
    if out_planes:
        operands.append(inverse)
        specs.append(whole_spec(inverse))
    out_shape = [jax.ShapeDtypeStruct((n, rows, lanes), jnp.float32) for n in out_planes]
    out_specs = [piece_spec(n) for n in out_planes]
    if keep:
        out_shape.append(jax.ShapeDtypeStruct((rows, depth, lanes), jnp.float32))
        out_specs.append(stored)
    side = -1.0 if adjoint else 1.0

    def body(*refs):
        refs = list(refs)
        ins = [refs.pop(0) for _ in pieces]
        if pieces:
            main_ref, cross_ref, forward_ref = refs.pop(0), refs.pop(0), refs.pop(0)
        added_ref = refs.pop(0) if added is not None else None
        inverse_ref = refs.pop(0) if out_planes else None
        outs = [refs.pop(0) for _ in out_planes]
        keep_ref = refs.pop(0) if keep else None

        def sign(count):
            lane = lax.broadcasted_iota(jnp.int32, (count, lanes), 1)
            return jnp.where(lane < half, 1.0, -1.0)

        for pair in range(block // 2):
            ks = (2 * pair, 2 * pair + 1)
            results = []
            if pieces:
                columns = [jnp.concatenate([rows_of(ref, k)[...] for ref in ins], axis=0) for k in ks]
                both = jnp.concatenate(columns, axis=1)
                grown = fold_rows(dot(forward_ref[...], jnp.concatenate(split(both), axis=0)))
                for index, k in enumerate(ks):
                    lanes_of = slice(index * lanes, (index + 1) * lanes)
                    cos_part, sin_part = grown[:depth, lanes_of], grown[depth:, lanes_of]
                    sin_roll = pltpu.roll(sin_part, half, 1)
                    spectrum = cos_part + sign(depth) * sin_roll
                    result = (
                        spectrum * main_ref[0, k]
                        + pltpu.roll(spectrum, half, 1) * main_ref[1, k] * side
                    )
                    if k == 0:
                        change = sign(depth) * cos_part - sin_roll - spectrum
                        extra = (
                            change * cross_ref[0]
                            + pltpu.roll(change, half, 1) * cross_ref[1] * side
                        )
                        result = result + jnp.where(pl.program_id(0) == 0, extra, 0.0)
                    if added is not None:
                        result = result + added_ref[k]
                    results.append(result)
            else:
                results = [added_ref[k] for k in ks]
            if keep:
                for k, result in zip(ks, results):
                    keep_ref[k] = result
            if not out_planes:
                continue
            total = sum(out_planes)
            both = jnp.concatenate(results, axis=1)
            grown = fold_rows(dot(inverse_ref[...], jnp.concatenate(split(both), axis=0)))
            for index, k in enumerate(ks):
                lanes_of = slice(index * lanes, (index + 1) * lanes)
                cos_part, sin_part = grown[:total, lanes_of], grown[total:, lanes_of]
                volume = cos_part - sign(total) * pltpu.roll(sin_part, half, 1)
                start = 0
                for ref in outs:
                    rows_of(ref, k)[...] = volume[start : start + ref.shape[0]]
                    start += ref.shape[0]

    results = pl.pallas_call(
        body,
        grid=(rows // block,),
        out_shape=out_shape,
        in_specs=specs,
        out_specs=out_specs,
        interpret=INTERPRET,
        name="depth_step",
    )(*operands)
    outs = results[: len(out_planes)]
    return outs, (results[-1] if keep else None)


def transfer_tables(psf, after, space_count):
    _, depth, rows, lanes = psf.shape
    half = lanes // 2
    device = lax.axis_index("space")
    upper = device >= space_count // 2
    special = (device % (space_count // 2)) == 0
    block = BLOCK_ROWS

    def body(upper_ref, psf_ref, _, main_ref, first_ref):
        lane = lax.broadcasted_iota(jnp.int32, (depth, lanes), 1)
        for k in range(block):
            for part in range(2):
                value = rows_of(psf_ref.at[part], k)[...]
                if k == 0:
                    first_ref[part] = value
                rolled = pltpu.roll(value, half, 1)
                doubled = jnp.where(lane < half, value, rolled)
                other = jnp.where(lane < half, rolled, value)
                packed = jnp.where((lane % half == 0) & (upper_ref[0] > 0), other, doubled)
                if part == 1:
                    packed = jnp.where(lane < half, -packed, packed)
                main_ref[part, k] = packed

    main, first = pl.pallas_call(
        body,
        grid_spec=pltpu.PrefetchScalarGridSpec(
            num_scalar_prefetch=1,
            grid=(rows // block,),
            in_specs=[
                pl.BlockSpec((2, depth, block, lanes), lambda i, *_: (0, 0, i, 0)),
                pl.BlockSpec(memory_space=pl.ANY),
            ],
            out_specs=[
                pl.BlockSpec((2, block, depth, lanes), lambda i, *_: (0, i, 0, 0)),
                pl.BlockSpec((2, depth, lanes), lambda i, *_: (0, i, 0)),
            ],
        ),
        out_shape=[
            jax.ShapeDtypeStruct((2, rows, depth, lanes), jnp.float32),
            jax.ShapeDtypeStruct((2, depth * (rows // block), lanes), jnp.float32),
        ],
        interpret=INTERPRET,
        name="transfer_tables",
    )(upper.astype(jnp.int32).reshape(1), psf, after)
    first = first[:, :depth]
    pairs = [(0, space_count // 2), (space_count // 2, 0)]
    other = lax.ppermute(first, "space", pairs)
    change = jnp.where(special, 0.5 * (first - other), 0.0)
    column = jnp.where(upper, change[:, :, half], change[:, :, 0])[:, :, None]
    lane = lax.broadcasted_iota(jnp.int32, (depth, lanes), 1)
    cross = jnp.stack(
        [
            jnp.where(lane % half == 0, column[0], 0.0),
            jnp.where(lane == 0, -column[1], jnp.where(lane == half, column[1], 0.0)),
        ]
    )
    return main, cross


def send(array, axis, count, flip):
    if flip == 0:
        return array
    return lax.ppermute(array, axis, [(i, i ^ flip) for i in range(count)])


def shards(estimate, observed, valid, psf_spectrum):
    space_count = lax.axis_size("space")
    views = lax.axis_size("view")
    planes, row_total, lanes = estimate.shape
    depth = planes * space_count
    view_count = views * observed.shape[0]
    columns_f, columns_i = column_tables(lanes, 1.0 / (depth * row_total * lanes))
    rows_f, rows_i, masks_f, masks_i = row_tables(row_total, lanes)
    tables = {
        "forward": (jnp.asarray(columns_f), jnp.asarray(rows_f), jnp.asarray(masks_f)),
        "inverse": (jnp.asarray(columns_i), jnp.asarray(rows_i), jnp.asarray(masks_i)),
    }
    observed, valid = observed[0], valid[0]
    place = lax.axis_index("space")
    me = lax.axis_index("view")
    device = place.astype(jnp.int32).reshape(1)

    shared = planes % views == 0 and views & (views - 1) == 0
    blocks = views if shared else 1
    share = planes // blocks
    strides = [1 << bit for bit in range(blocks.bit_length() - 1)]
    flips = [0]
    for stride in reversed(strides):
        flips = flips + [f ^ stride for f in flips]
    half_space = space_count // 2
    groups = [list(range(half_space, space_count)), list(range(half_space))]
    chunk = planes // 2 if planes % 2 == 0 else planes
    chunks = range(0, planes, chunk)

    def plane_order(entries, count):
        starts = [(place ^ k) * planes + first for k, first in entries]
        return (jnp.stack(starts)[:, None] + jnp.arange(count, dtype=jnp.int32)[None, :]).reshape(-1)

    def first_of(flip):
        return (me ^ flip) * share if shared else 0

    own = lax.dynamic_slice_in_dim(estimate, me * share, share, 0) if shared else estimate
    spectrum = lateral_forward(own, device, tables, space_count)
    transfer = transfer_tables(psf_spectrum[0], spectrum[0], space_count)

    gathered_forward = depth_table(
        plane_order([(k, first_of(f)) for k in range(space_count) for f in flips], share), depth, False
    )
    shared_inverse = depth_table(
        plane_order([(k, first_of(f)) for f in flips for group in groups for k in group], share), depth, True
    )
    slab_entries = [[(k, start) for k in range(space_count)] for start in chunks]
    slab_forward = [depth_table(plane_order(e, chunk), depth, False) for e in slab_entries]
    slab_inverse = [depth_table(plane_order(e, chunk), depth, True) for e in slab_entries]

    def spread(pieces):
        moved = {k: send(pieces[k], "space", space_count, k) for k in reversed(range(space_count))}
        return [moved[k] for k in range(space_count)]

    for iteration in range(ITERS):
        last = iteration == ITERS - 1
        pieces = []
        for piece in spread(spectrum):
            copies = [piece]
            for stride in reversed(strides):
                copies = copies + [send(c, "view", views, stride) for c in copies]
            pieces += copies
        kept = None
        ratios = []
        for number, start in enumerate(chunks):
            final = number == len(chunks) - 1
            outs, stored = depth_step(
                pieces, kept, transfer, gathered_forward, slab_inverse[number],
                [chunk] * space_count, number == 0 and not final, False, depth,
            )
            pieces, kept = [], (stored if stored is not None else kept)
            ratios.append(ratio_step(spread(outs), observed, valid, start, device, tables))
        kept = None
        for number, ratio in enumerate(ratios):
            final = number == len(ratios) - 1
            counts = [share * len(group) for _ in flips for group in groups] if final else []
            outs, kept = depth_step(
                spread(ratio), kept, transfer, slab_forward[number], shared_inverse,
                counts, not final, True, depth,
            )
        summed = {}
        for number, group in enumerate(groups):
            parts = [outs[index * len(groups) + number] for index in range(blocks)]
            for stride in strides:
                middle = len(parts) // 2
                moved = [send(p, "view", views, stride) for p in parts[middle:]]
                if len(parts) == 2:
                    for index, k in enumerate(group):
                        window = slice(index * share, (index + 1) * share)
                        summed[k] = parts[0][window] + moved[0][window]
                parts = [kept_part + new for kept_part, new in zip(parts[:middle], moved)]
            if not shared:
                total = lax.psum(parts[0], "view")
                for index, k in enumerate(group):
                    summed[k] = total[index * share : (index + 1) * share]
            elif not strides:
                for index, k in enumerate(group):
                    summed[k] = parts[0][index * share : (index + 1) * share]
        own, spectrum = update_step(
            spread([summed[k] for k in range(space_count)]), own, float(view_count), device, tables, last
        )
    if not shared:
        return own
    copies = [own]
    for stride in reversed(strides):
        copies = copies + [send(c, "view", views, stride) for c in copies]
    refined = jnp.zeros_like(estimate)
    for flip, copy in zip(flips, copies):
        refined = lax.dynamic_update_slice_in_dim(refined, copy, first_of(flip), 0)
    return refined


def solution(mesh):
    return jax.shard_map(
        shards,
        mesh=mesh,
        in_specs=(
            P("space", "blocks", None),
            P("view", "space", "blocks", None),
            P("view", "space", "blocks", None),
            P("view", None, None, "space", None),
        ),
        out_specs=P("space", "blocks", None),
        check_vma=False,
    )
```

time: 498 us -> 396 us (0.80)
  blocking collectives: 211 us -> 0 us
  starting transfers between devices: 20.4 us -> 131 us
  Pallas kernels: 87.7 us -> 143 us
  waiting for transfers between devices: 118 us -> 83.8 us
  between operations: 13.7 us -> 0.82 us
  local copies, waits for them, and re-layouts: 24 us -> 18.1 us
    all_to_all x6 -> x0, blocking collectives: 211 us -> none  [exchange(): lax.all_to_all(array, 'space', split_axis=0, concat_axis=0, tiled=True)]
    ppermute x13 -> x76, starting transfers between devices: 13.3 us -> 131 us  [the longest x75 126 us: send(): return lax.ppermute(array, axis, [(i, i ^ flip) for i in range(count)])]
    pallas_call x9 -> x16, Pallas kernels: 87.7 us -> 143 us  [the longest x8 82.4 us: depth_step(): pl.pallas_call(body, grid=(rows // block,), out_shape=out_shape, in_specs...]
    all_to_all x2 -> x0, waiting for transfers between devices: 46.4 us -> none  [exchange(): lax.all_to_all(array, 'space', split_axis=0, concat_axis=0, tiled=True)]
    ppermute x13 -> x76, waiting for transfers between devices: 50.2 us -> 83.8 us  [the longest x75 80.9 us: send(): return lax.ppermute(array, axis, [(i, i ^ flip) for i in range(count)])]
    all_gather x1 -> x0, waiting for transfers between devices: 21.8 us -> none  [shards(): own = lax.all_gather(own, 'view', axis=0, tiled=True)]
    all_to_all x2 -> x0, starting transfers between devices: 7.08 us -> none  [exchange(): lax.all_to_all(array, 'space', split_axis=0, concat_axis=0, tiled=True)]
    select_n x5 -> x4, other arithmetic: 8.17 us -> 2.25 us  [the longest x1 0.85 us: transfer_tables(): change = jnp.where(special, 0.5 * (first - other), 0.0)]
  transfers between devices with their start and end apart: 16 -> 76, of which waited for: 9 -> 26; matrix products, arithmetic and copies ran while one was open for 5% -> 5% of each run, Pallas kernels for 1% -> 19%
where the time goes in v2:
time: 396 us; the launch traced here: 394 us
  Pallas kernels  143 us (36%)
  starting transfers between devices  131 us (33%)
  waiting for transfers between devices  83.8 us (21%)
  local copies, waits for them, and re-layouts  18.1 us (5%)
  other arithmetic  17.8 us (4%)
    ppermute x75, starting transfers between devices, send(): return lax.ppermute(array, axis, [(i, i ^ flip) for i in range(count)])  126 us
    pallas_call x8, Pallas kernels, depth_step(): pl.pallas_call(body, grid=(rows // block,), out_shape=out_shape, in_specs...  82.4 us
    ppermute x75, waiting for transfers between devices, send(): return lax.ppermute(array, axis, [(i, i ^ flip) for i in range(count)])  80.9 us
    pallas_call x7, Pallas kernels, lateral_call(): pl.pallas_call(kernel, grid_spec=pltpu.PrefetchScalarGridSpec(num_scalar_...  53 us
    unnamed x130, local copies, waits for them, and re-layouts  12.3 us
  transfers between devices with their start and end apart: 76, of which 26 were waited for; matrix products, arithmetic and copies ran while one was open for 5% of the time, Pallas kernels for 19%

profile of v2, /device:TPU:0, one launch (start us, length us, event | category | flops | bytes accessed | tf_op | source)
XLA Modules:
  0.0 394.2 jit_solution(18132015849759726958)
XLA Ops:
  9.0 7.4 %transfer_tables.1 = (f32[2,64,64,128]{3,2,1,0:T(8,128)}, f32[2,512,128]{2,1,0:T(8,128)}) custom-call(s32[1]{0:T(128)} %bitcast.3.upper_ref, f32[2,64,64,128]{3,2,1,0:T(8,128)} %bitcast.37, f32[4,64,128]{2,1,0:T(8,128)} %get-tuple-element.66._.refs_0_), custom_call_target="tpu_custom_call" | custom-call | tf_op jit(solution)/shard_map/transfer_tables/pallas_call | solution.py:390
  17.2 4.5 %collective-permute-start.15 = (f32[2,64,128]{2,1,0:T(8,128)S(1)}, f32[2,64,128]{2,1,0:T(8,128)S(1)}, u32[]{:S(2)}, u32[]{:S(2)}) collective-permute-start(f32[2,64,128]{2,1,0:T(8,128)S(1)} %slice.70), channel_id=1, source_target_pairs={{0,8},{8,0},{1,9},{9,1},{2,10},{10,2},{3,11},{11,3},{16,24},{24,16... | collective-permute-start | bytes 196616 | tf_op jit(solution)/shard_map/ppermute | solution.py:413
  46.5 16.3 %depth_step.8 = (f32[8,64,128]{2,1,0:T(8,128)}, f32[8,64,128]{2,1,0:T(8,128)}, f32[8,64,128]{2,1,0:T(8,128)}, f32[8,64,128]{2,1,0:T(8,128)}, f32[64,64,128]{2,1,0:T(8,128)}) custom-call(f32[4,64,128]{2,1,0:T(8,128)} %get-tuple-element.66._.refs_0_, f32[4,64,128]{2,1,0:T(8,128)} %copy-done.25, f32[4,64,128]{2,1,0:T(8,128)} %copy-done.26, ...), custom_call_target="tpu_custom_call" | custom-call | tf_op jit(solution)/shard_map/depth_step/pallas_call | solution.py:354
  70.4 6.5 %depth_step.9 = (f32[8,64,128]{2,1,0:T(8,128)}, f32[8,64,128]{2,1,0:T(8,128)}, f32[8,64,128]{2,1,0:T(8,128)}, f32[8,64,128]{2,1,0:T(8,128)}) custom-call(f32[64,64,128]{2,1,0:T(8,128)} %get-tuple-element.72.refs_0_, bf16[128,128]{1,0:T(8,128)(2,1)} %pad_maximum_fusion.10.refs_1_), custom_call_target="tpu_custom_call" | custom-call | tf_op jit(solution)/shard_map/depth_step/pallas_call | solution.py:354
  81.3 7.2 %collective-permute-done.23.refs_4_ = f32[8,64,128]{2,1,0:T(8,128)S(1)} collective-permute-done((f32[8,64,128]{2,1,0:T(8,128)}, f32[8,64,128]{2,1,0:T(8,128)S(1)}, u32[]{:S(2)}, u32[]{:S(2)}) %collective-permute-start.23) | collective-permute-done | bytes 262176 | tf_op jit(solution)/shard_map/ppermute | solution.py:429
  89.2 9.7 %ratio_step.5 = (f32[8,64,128]{2,1,0:T(8,128)}, f32[8,64,128]{2,1,0:T(8,128)}, f32[8,64,128]{2,1,0:T(8,128)}, f32[8,64,128]{2,1,0:T(8,128)}) custom-call(s32[1]{0:T(128)} %bitcast.device_ref, f32[16,256,128]{2,1,0:T(8,128)} %bitcast.29, s32[16,256,128]{2,1,0:T(8,128)} %bitcast.33, f32[8,64,128]{2,1,0:T(8,128)} %get-tuple-element.81.refs_2_, ...), custom_call_target="tpu_custom_call" | custom-call | tf_op jit(solution)/shard_map/ratio_step/pallas_call | solution.py:183
  99.0 16.9 %collective-permute-start.25 = (f32[8,64,128]{2,1,0:T(8,128)}, f32[8,64,128]{2,1,0:T(8,128)S(1)}, u32[]{:S(2)}, u32[]{:S(2)}) collective-permute-start(f32[8,64,128]{2,1,0:T(8,128)} %get-tuple-element.86), channel_id=1, source_target_pairs={{0,4},{4,0},{8,12},{12,8},{1,5},{5,1},{9,13},{13,9},{2,6},{6,2},{1... | collective-permute-start | bytes 786440 | tf_op jit(solution)/shard_map/ppermute | solution.py:429
  119.9 9.8 %ratio_step.4 = (f32[8,64,128]{2,1,0:T(8,128)}, f32[8,64,128]{2,1,0:T(8,128)}, f32[8,64,128]{2,1,0:T(8,128)}, f32[8,64,128]{2,1,0:T(8,128)}) custom-call(s32[1]{0:T(128)} %bitcast.device_ref, f32[16,256,128]{2,1,0:T(8,128)} %bitcast.30, s32[16,256,128]{2,1,0:T(8,128)} %bitcast.34, f32[8,64,128]{2,1,0:T(8,128)} %get-tuple-element.73.refs_2_, ...), custom_call_target="tpu_custom_call" | custom-call | tf_op jit(solution)/shard_map/ratio_step/pallas_call | solution.py:183
  133.4 6.5 %collective-permute-start.20 = (f32[8,64,128]{2,1,0:T(8,128)}, f32[8,64,128]{2,1,0:T(8,128)S(1)}, u32[]{:S(2)}, u32[]{:S(2)}) collective-permute-start(f32[8,64,128]{2,1,0:T(8,128)} %get-tuple-element.79), channel_id=1, source_target_pairs={{0,8},{4,12},{8,0},{12,4},{1,9},{5,13},{9,1},{13,5},{2,10},{6,14},... | collective-permute-start | bytes 786440 | tf_op jit(solution)/shard_map/ppermute | solution.py:429
  143.7 8.1 %depth_step.10.refs_7_ = f32[64,64,128]{2,1,0:T(8,128)} custom-call(f32[8,64,128]{2,1,0:T(8,128)} %get-tuple-element.85.refs_0_, f32[8,64,128]{2,1,0:T(8,128)} %copy-done.3, f32[8,64,128]{2,1,0:T(8,128)} %copy-done.7, f32[8,64,128]{2,1,0:T(8,128)} %collective-permute-done.27.refs_3_, f32[2,64,64,128]{3,2,1,0:T(8,128)} %get-tuple-element.70.refs_16_.refs_4_, ...), custom_call_target="tpu_custom_call" | custom-call | tf_op jit(solution)/shard_map/depth_step/pallas_call | solution.py:354
  156.7 10.4 %depth_step.11 = (f32[8,64,128]{2,1,0:T(8,128)}, f32[8,64,128]{2,1,0:T(8,128)}, f32[8,64,128]{2,1,0:T(8,128)}, f32[8,64,128]{2,1,0:T(8,128)}, f32[8,64,128]{2,1,...) custom-call(f32[8,64,128]{2,1,0:T(8,128)} %get-tuple-element.77.refs_0_, ...), custom_call_target="tpu_custom_call" | custom-call | tf_op jit(solution)/shard_map/depth_step/pallas_call | solution.py:354
  174.2 5.0 %collective-permute-done.34 = f32[8,64,128]{2,1,0:T(8,128)S(1)} collective-permute-done((f32[8,64,128]{2,1,0:T(8,128)S(1)}, f32[8,64,128]{2,1,0:T(8,128)S(1)}, u32[]{:S(2)}, u32[]{:S(2)}) %collective-permute-start.34) | collective-permute-done | bytes 262176 | tf_op jit(solution)/shard_map/ppermute | solution.py:429
  179.2 5.8 %collective-permute-start.35 = (f32[4,64,128]{2,1,0:T(8,128)S(1)}, f32[4,64,128]{2,1,0:T(8,128)S(1)}, u32[]{:S(2)}, u32[]{:S(2)}) collective-permute-start(f32[4,64,128]{2,1,0:T(8,128)S(1)} %get-tuple-element.134), channel_id=1, source_target_pairs={{0,8},{4,12},{8,0},{12,4},{1,9},{5,13},{9,1},{13,5},{2,10},{6,14},... | collective-permute-start | bytes 393224 | tf_op jit(solution)/shard_map/ppermute | solution.py:429
  189.6 4.6 %collective-permute-done.35.refs_3_ = f32[4,64,128]{2,1,0:T(8,128)S(1)} collective-permute-done((f32[4,64,128]{2,1,0:T(8,128)S(1)}, f32[4,64,128]{2,1,0:T(8,128)S(1)}, u32[]{:S(2)}, u32[]{:S(2)}) %collective-permute-start.35) | collective-permute-done | bytes 131104 | tf_op jit(solution)/shard_map/ppermute | solution.py:429
  195.9 6.1 %update_step.2 = (f32[4,256,128]{2,1,0:T(8,128)}, f32[4,64,128]{2,1,0:T(8,128)}, f32[4,64,128]{2,1,0:T(8,128)}, f32[4,64,128]{2,1,0:T(8,128)}, f32[4,64,128]{2,1,0:T(8,128)}) custom-call(s32[1]{0:T(128)} %bitcast.device_ref, f32[4,256,128]{2,1,0:T(8,128)} %constant_dynamic-slice_fusion.refs_0_, f32[4,64,128]{2,1,0:T(8,128)} %get-tuple-element.136.refs_1_, ...), custom_call_target="tpu_custom_call" | custom-call | tf_op jit(solution)/shard_map/update_step/pallas_call | solution.py:183
  209.3 6.2 %collective-permute-done.44.refs_8_ = f32[4,64,128]{2,1,0:T(8,128)S(1)} collective-permute-done((f32[4,64,128]{2,1,0:T(8,128)}, f32[4,64,128]{2,1,0:T(8,128)S(1)}, u32[]{:S(2)}, u32[]{:S(2)}) %collective-permute-start.44) | collective-permute-done | bytes 131104 | tf_op jit(solution)/shard_map/ppermute | solution.py:429
  224.6 16.1 %depth_step.12 = (f32[8,64,128]{2,1,0:T(8,128)}, f32[8,64,128]{2,1,0:T(8,128)}, f32[8,64,128]{2,1,0:T(8,128)}, f32[8,64,128]{2,1,0:T(8,128)}, f32[64,64,128]{2,1,0:T(8,128)}) custom-call(f32[4,64,128]{2,1,0:T(8,128)} %get-tuple-element.98.refs_0_, f32[4,64,128]{2,1,0:T(8,128)} %copy-done.34, f32[4,64,128]{2,1,0:T(8,128)} %copy-done.36, ...), custom_call_target="tpu_custom_call" | custom-call | tf_op jit(solution)/shard_map/depth_step/pallas_call | solution.py:354
  245.2 6.5 %depth_step.13 = (f32[8,64,128]{2,1,0:T(8,128)}, f32[8,64,128]{2,1,0:T(8,128)}, f32[8,64,128]{2,1,0:T(8,128)}, f32[8,64,128]{2,1,0:T(8,128)}) custom-call(f32[64,64,128]{2,1,0:T(8,128)} %get-tuple-element.102.refs_0_, bf16[128,128]{1,0:T(8,128)(2,1)} %pad_maximum_fusion.10.refs_1_), custom_call_target="tpu_custom_call" | custom-call | tf_op jit(solution)/shard_map/depth_step/pallas_call | solution.py:354
  256.2 6.8 %collective-permute-done.59.refs_4_ = f32[8,64,128]{2,1,0:T(8,128)S(1)} collective-permute-done((f32[8,64,128]{2,1,0:T(8,128)}, f32[8,64,128]{2,1,0:T(8,128)S(1)}, u32[]{:S(2)}, u32[]{:S(2)}) %collective-permute-start.59) | collective-permute-done | bytes 262176 | tf_op jit(solution)/shard_map/ppermute | solution.py:429
  263.8 9.8 %ratio_step.7 = (f32[8,64,128]{2,1,0:T(8,128)}, f32[8,64,128]{2,1,0:T(8,128)}, f32[8,64,128]{2,1,0:T(8,128)}, f32[8,64,128]{2,1,0:T(8,128)}) custom-call(s32[1]{0:T(128)} %bitcast.device_ref, f32[16,256,128]{2,1,0:T(8,128)} %bitcast.31, s32[16,256,128]{2,1,0:T(8,128)} %bitcast.35, f32[8,64,128]{2,1,0:T(8,128)} %get-tuple-element.111.refs_2_, ...), custom_call_target="tpu_custom_call" | custom-call | tf_op jit(solution)/shard_map/ratio_step/pallas_call | solution.py:183
  273.5 16.9 %collective-permute-start.61 = (f32[8,64,128]{2,1,0:T(8,128)}, f32[8,64,128]{2,1,0:T(8,128)S(1)}, u32[]{:S(2)}, u32[]{:S(2)}) collective-permute-start(f32[8,64,128]{2,1,0:T(8,128)} %get-tuple-element.116), channel_id=1, source_target_pairs={{0,4},{4,0},{8,12},{12,8},{1,5},{5,1},{9,13},{13,9},{2,6},{6,2},{1... | collective-permute-start | bytes 786440 | tf_op jit(solution)/shard_map/ppermute | solution.py:429
  293.7 9.8 %ratio_step.6 = (f32[8,64,128]{2,1,0:T(8,128)}, f32[8,64,128]{2,1,0:T(8,128)}, f32[8,64,128]{2,1,0:T(8,128)}, f32[8,64,128]{2,1,0:T(8,128)}) custom-call(s32[1]{0:T(128)} %bitcast.device_ref, f32[16,256,128]{2,1,0:T(8,128)} %bitcast.32, s32[16,256,128]{2,1,0:T(8,128)} %bitcast.36, f32[8,64,128]{2,1,0:T(8,128)} %get-tuple-element.103.refs_2_, ...), custom_call_target="tpu_custom_call" | custom-call | tf_op jit(solution)/shard_map/ratio_step/pallas_call | solution.py:183
  303.5 4.4 %collective-permute-start.55 = (f32[8,64,128]{2,1,0:T(8,128)}, f32[8,64,128]{2,1,0:T(8,128)S(1)}, u32[]{:S(2)}, u32[]{:S(2)}) collective-permute-start(f32[8,64,128]{2,1,0:T(8,128)} %get-tuple-element.108), channel_id=1, source_target_pairs={{0,4},{4,0},{8,12},{12,8},{1,5},{5,1},{9,13},{13,9},{2,6},{6,2},{1... | collective-permute-start | bytes 786440 | tf_op jit(solution)/shard_map/ppermute | solution.py:429
  307.9 6.6 %collective-permute-start.56 = (f32[8,64,128]{2,1,0:T(8,128)}, f32[8,64,128]{2,1,0:T(8,128)S(1)}, u32[]{:S(2)}, u32[]{:S(2)}) collective-permute-start(f32[8,64,128]{2,1,0:T(8,128)} %get-tuple-element.109), channel_id=1, source_target_pairs={{0,8},{4,12},{8,0},{12,4},{1,9},{5,13},{9,1},{13,5},{2,10},{6,14},... | collective-permute-start | bytes 786440 | tf_op jit(solution)/shard_map/ppermute | solution.py:429
  316.8 8.1 %depth_step.14.refs_7_ = f32[64,64,128]{2,1,0:T(8,128)} custom-call(f32[8,64,128]{2,1,0:T(8,128)} %get-tuple-element.115.refs_0_, f32[8,64,128]{2,1,0:T(8,128)} %copy-done.10, f32[8,64,128]{2,1,0:T(8,128)} %copy-done.13, f32[8,64,128]{2,1,0:T(8,128)} %collective-permute-done.63.refs_3_, f32[2,64,64,128]{3,2,1,0:T(8,128)} %get-tuple-element.70.refs_16_.refs_4_, ...), custom_call_target="tpu_custom_call" | custom-call | tf_op jit(solution)/shard_map/depth_step/pallas_call | solution.py:354
  324.9 5.6 %collective-permute-done.56.refs_2_ = f32[8,64,128]{2,1,0:T(8,128)S(1)} collective-permute-done((f32[8,64,128]{2,1,0:T(8,128)}, f32[8,64,128]{2,1,0:T(8,128)S(1)}, u32[]{:S(2)}, u32[]{:S(2)}) %collective-permute-start.56) | collective-permute-done | bytes 262176 | tf_op jit(solution)/shard_map/ppermute | solution.py:429
  331.3 10.4 %depth_step.15 = (f32[8,64,128]{2,1,0:T(8,128)}, f32[8,64,128]{2,1,0:T(8,128)}, f32[8,64,128]{2,1,0:T(8,128)}, f32[8,64,128]{2,1,0:T(8,128)}, f32[8,64,128]{2,1,...) custom-call(f32[8,64,128]{2,1,0:T(8,128)} %get-tuple-element.107.refs_0_, ...), custom_call_target="tpu_custom_call" | custom-call | tf_op jit(solution)/shard_map/depth_step/pallas_call | solution.py:354
  349.4 5.0 %collective-permute-done.70 = f32[8,64,128]{2,1,0:T(8,128)S(1)} collective-permute-done((f32[8,64,128]{2,1,0:T(8,128)S(1)}, f32[8,64,128]{2,1,0:T(8,128)S(1)}, u32[]{:S(2)}, u32[]{:S(2)}) %collective-permute-start.70) | collective-permute-done | bytes 262176 | tf_op jit(solution)/shard_map/ppermute | solution.py:429
  354.5 5.5 %collective-permute-start.71 = (f32[4,64,128]{2,1,0:T(8,128)S(1)}, f32[4,64,128]{2,1,0:T(8,128)S(1)}, u32[]{:S(2)}, u32[]{:S(2)}) collective-permute-start(f32[4,64,128]{2,1,0:T(8,128)S(1)} %get-tuple-element.130), channel_id=1, source_target_pairs={{0,8},{4,12},{8,0},{12,4},{1,9},{5,13},{9,1},{13,5},{2,10},{6,14},... | collective-permute-start | bytes 393224 | tf_op jit(solution)/shard_map/ppermute | solution.py:429
  364.8 4.9 %collective-permute-done.71.refs_3_ = f32[4,64,128]{2,1,0:T(8,128)S(1)} collective-permute-done((f32[4,64,128]{2,1,0:T(8,128)S(1)}, f32[4,64,128]{2,1,0:T(8,128)S(1)}, u32[]{:S(2)}, u32[]{:S(2)}) %collective-permute-start.71) | collective-permute-done | bytes 131104 | tf_op jit(solution)/shard_map/ppermute | solution.py:429
  371.6 4.3 %update_step.3 = f32[4,256,128]{2,1,0:T(8,128)} custom-call(s32[1]{0:T(128)} %bitcast.device_ref, f32[4,256,128]{2,1,0:T(8,128)} %get-tuple-element.97.refs_0_, f32[4,64,128]{2,1,0:T(8,128)} %get-tuple-element.132.refs_1_, f32[4,64,128]{2,1,0:T(8,128)} %copy-done.59, f32[4,64,128]{2,1,0:T(8,128)} %copy-done.55, f32[4,64,128]{2,1,0:T(8,128)} %copy-done.57, ...), custom_call_target="tpu_custom_call" | custom-call | tf_op jit(solution)/shard_map/update_step/pallas_call | solution.py:183
  377.1 12.5 %collective-permute-done.73 = f32[4,256,128]{2,1,0:T(8,128)S(1)} collective-permute-done((f32[4,256,128]{2,1,0:T(8,128)}, f32[4,256,128]{2,1,0:T(8,128)S(1)}, u32[]{:S(2)}, u32[]{:S(2)}) %collective-permute-start.73) | collective-permute-done | bytes 524320 | tf_op jit(solution)/shard_map/ppermute | solution.py:429
  (332 shorter events, 129.1 us)
Async XLA Ops:
  6.0 26.2 %collective-permute-start = (f32[4,64,128]{2,1,0:T(8,128)}, f32[4,64,128]{2,1,0:T(8,128)S(1)}, u32[]{:S(2)}, u32[]{:S(2)}) collective-permute-start(f32[4,64,128]{2,1,0:T(8,128)} %get-tuple-element.66._.refs_0_), channel_id=1, source_target_pairs={{0,2},{1,3},{2,0},{3,1},{4,6},{5,7},{6,4},{7,5},{8,10},{9,11},{10,... | collective-permute-start | bytes 393224 | tf_op jit(solution)/shard_map/ppermute | solution.py:429
  8.9 27.2 %collective-permute-start.1 = (f32[4,64,128]{2,1,0:T(8,128)}, f32[4,64,128]{2,1,0:T(8,128)S(1)}, u32[]{:S(2)}, u32[]{:S(2)}) collective-permute-start(f32[4,64,128]{2,1,0:T(8,128)} %get-tuple-element.66._.refs_0_), channel_id=1, source_target_pairs={{0,1},{1,0},{2,3},{3,2},{4,5},{5,4},{6,7},{7,6},{8,9},{9,8},{10,11... | collective-permute-start | bytes 393224 | tf_op jit(solution)/shard_map/ppermute | solution.py:429
  62.8 16.9 %collective-permute-start.22 = (f32[8,64,128]{2,1,0:T(8,128)}, f32[8,64,128]{2,1,0:T(8,128)S(1)}, u32[]{:S(2)}, u32[]{:S(2)}) collective-permute-start(f32[8,64,128]{2,1,0:T(8,128)} %get-tuple-element.82), channel_id=1, source_target_pairs={{0,4},{4,0},{8,12},{12,8},{1,5},{5,1},{9,13},{13,9},{2,6},{6,2},{1... | collective-permute-start | bytes 786440 | tf_op jit(solution)/shard_map/ppermute | solution.py:429
  67.0 21.6 %collective-permute-start.23 = (f32[8,64,128]{2,1,0:T(8,128)}, f32[8,64,128]{2,1,0:T(8,128)S(1)}, u32[]{:S(2)}, u32[]{:S(2)}) collective-permute-start(f32[8,64,128]{2,1,0:T(8,128)} %get-tuple-element.83), channel_id=1, source_target_pairs={{0,8},{4,12},{8,0},{12,4},{1,9},{5,13},{9,1},{13,5},{2,10},{6,14},... | collective-permute-start | bytes 786440 | tf_op jit(solution)/shard_map/ppermute | solution.py:429
  67.7 20.8 %collective-permute-start.24 = (f32[8,64,128]{2,1,0:T(8,128)}, f32[8,64,128]{2,1,0:T(8,128)}, u32[]{:S(2)}, u32[]{:S(2)}) collective-permute-start(f32[8,64,128]{2,1,0:T(8,128)} %get-tuple-element.84), channel_id=1, source_target_pairs={{0,12},{4,8},{8,4},{12,0},{1,13},{5,9},{9,5},{13,1},{2,14},{6,10},... | collective-permute-start | bytes 786440 | tf_op jit(solution)/shard_map/ppermute | solution.py:429
  76.9 40.5 %collective-permute-start.16 = (f32[8,64,128]{2,1,0:T(8,128)}, f32[8,64,128]{2,1,0:T(8,128)S(1)}, u32[]{:S(2)}, u32[]{:S(2)}) collective-permute-start(f32[8,64,128]{2,1,0:T(8,128)} %get-tuple-element.74), channel_id=1, source_target_pairs={{0,4},{4,0},{8,12},{12,8},{1,5},{5,1},{9,13},{13,9},{2,6},{6,2},{1... | collective-permute-start | bytes 786440 | tf_op jit(solution)/shard_map/ppermute | solution.py:429
  77.9 41.1 %collective-permute-start.17 = (f32[8,64,128]{2,1,0:T(8,128)}, f32[8,64,128]{2,1,0:T(8,128)S(1)}, u32[]{:S(2)}, u32[]{:S(2)}) collective-permute-start(f32[8,64,128]{2,1,0:T(8,128)} %get-tuple-element.75), channel_id=1, source_target_pairs={{0,8},{4,12},{8,0},{12,4},{1,9},{5,13},{9,1},{13,5},{2,10},{6,14},... | collective-permute-start | bytes 786440 | tf_op jit(solution)/shard_map/ppermute | solution.py:429
  79.6 39.4 %collective-permute-start.18 = (f32[8,64,128]{2,1,0:T(8,128)}, f32[8,64,128]{2,1,0:T(8,128)S(1)}, u32[]{:S(2)}, u32[]{:S(2)}) collective-permute-start(f32[8,64,128]{2,1,0:T(8,128)} %get-tuple-element.76), channel_id=1, source_target_pairs={{0,12},{4,8},{8,4},{12,0},{1,13},{5,9},{9,5},{13,1},{2,14},{6,10},... | collective-permute-start | bytes 786440 | tf_op jit(solution)/shard_map/ppermute | solution.py:429
  99.0 40.9 %collective-permute-start.25 = (f32[8,64,128]{2,1,0:T(8,128)}, f32[8,64,128]{2,1,0:T(8,128)S(1)}, u32[]{:S(2)}, u32[]{:S(2)}) collective-permute-start(f32[8,64,128]{2,1,0:T(8,128)} %get-tuple-element.86), channel_id=1, source_target_pairs={{0,4},{4,0},{8,12},{12,8},{1,5},{5,1},{9,13},{13,9},{2,6},{6,2},{1... | collective-permute-start | bytes 786440 | tf_op jit(solution)/shard_map/ppermute | solution.py:429
  116.6 26.3 %collective-permute-start.26 = (f32[8,64,128]{2,1,0:T(8,128)}, f32[8,64,128]{2,1,0:T(8,128)S(1)}, u32[]{:S(2)}, u32[]{:S(2)}) collective-permute-start(f32[8,64,128]{2,1,0:T(8,128)} %get-tuple-element.87), channel_id=1, source_target_pairs={{0,8},{4,12},{8,0},{12,4},{1,9},{5,13},{9,1},{13,5},{2,10},{6,14},... | collective-permute-start | bytes 786440 | tf_op jit(solution)/shard_map/ppermute | solution.py:429
  117.4 25.5 %collective-permute-start.27 = (f32[8,64,128]{2,1,0:T(8,128)}, f32[8,64,128]{2,1,0:T(8,128)}, u32[]{:S(2)}, u32[]{:S(2)}) collective-permute-start(f32[8,64,128]{2,1,0:T(8,128)} %get-tuple-element.88), channel_id=1, source_target_pairs={{0,12},{4,8},{8,4},{12,0},{1,13},{5,9},{9,5},{13,1},{2,14},{6,10},... | collective-permute-start | bytes 786440 | tf_op jit(solution)/shard_map/ppermute | solution.py:429
  129.6 22.1 %collective-permute-start.19 = (f32[8,64,128]{2,1,0:T(8,128)}, f32[8,64,128]{2,1,0:T(8,128)S(1)}, u32[]{:S(2)}, u32[]{:S(2)}) collective-permute-start(f32[8,64,128]{2,1,0:T(8,128)} %get-tuple-element.78), channel_id=1, source_target_pairs={{0,4},{4,0},{8,12},{12,8},{1,5},{5,1},{9,13},{13,9},{2,6},{6,2},{1... | collective-permute-start | bytes 786440 | tf_op jit(solution)/shard_map/ppermute | solution.py:429
  133.4 22.6 %collective-permute-start.20 = (f32[8,64,128]{2,1,0:T(8,128)}, f32[8,64,128]{2,1,0:T(8,128)S(1)}, u32[]{:S(2)}, u32[]{:S(2)}) collective-permute-start(f32[8,64,128]{2,1,0:T(8,128)} %get-tuple-element.79), channel_id=1, source_target_pairs={{0,8},{4,12},{8,0},{12,4},{1,9},{5,13},{9,1},{13,5},{2,10},{6,14},... | collective-permute-start | bytes 786440 | tf_op jit(solution)/shard_map/ppermute | solution.py:429
  139.9 16.1 %collective-permute-start.21 = (f32[8,64,128]{2,1,0:T(8,128)}, f32[8,64,128]{2,1,0:T(8,128)S(1)}, u32[]{:S(2)}, u32[]{:S(2)}) collective-permute-start(f32[8,64,128]{2,1,0:T(8,128)} %get-tuple-element.80), channel_id=1, source_target_pairs={{0,12},{4,8},{8,4},{12,0},{1,13},{5,9},{9,5},{13,1},{2,14},{6,10},... | collective-permute-start | bytes 786440 | tf_op jit(solution)/shard_map/ppermute | solution.py:429
  171.6 15.1 %collective-permute-start.30 = (f32[8,64,128]{2,1,0:T(8,128)S(1)}, f32[8,64,128]{2,1,0:T(8,128)S(1)}, u32[]{:S(2)}, u32[]{:S(2)}) collective-permute-start(f32[8,64,128]{2,1,0:T(8,128)S(1)} %add.330), channel_id=1, source_target_pairs={{0,2},{1,3},{2,0},{3,1},{4,6},{5,7},{6,4},{7,5},{8,10},{9,11},{10,... | collective-permute-start | bytes 786440 | tf_op jit(solution)/shard_map/ppermute | solution.py:429
  179.2 15.0 %collective-permute-start.35 = (f32[4,64,128]{2,1,0:T(8,128)S(1)}, f32[4,64,128]{2,1,0:T(8,128)S(1)}, u32[]{:S(2)}, u32[]{:S(2)}) collective-permute-start(f32[4,64,128]{2,1,0:T(8,128)S(1)} %get-tuple-element.134), channel_id=1, source_target_pairs={{0,8},{4,12},{8,0},{12,4},{1,9},{5,13},{9,1},{13,5},{2,10},{6,14},... | collective-permute-start | bytes 393224 | tf_op jit(solution)/shard_map/ppermute | solution.py:429
  240.7 14.2 %collective-permute-start.58 = (f32[8,64,128]{2,1,0:T(8,128)}, f32[8,64,128]{2,1,0:T(8,128)S(1)}, u32[]{:S(2)}, u32[]{:S(2)}) collective-permute-start(f32[8,64,128]{2,1,0:T(8,128)} %get-tuple-element.112), channel_id=1, source_target_pairs={{0,4},{4,0},{8,12},{12,8},{1,5},{5,1},{9,13},{13,9},{2,6},{6,2},{1... | collective-permute-start | bytes 786440 | tf_op jit(solution)/shard_map/ppermute | solution.py:429
  241.5 21.6 %collective-permute-start.59 = (f32[8,64,128]{2,1,0:T(8,128)}, f32[8,64,128]{2,1,0:T(8,128)S(1)}, u32[]{:S(2)}, u32[]{:S(2)}) collective-permute-start(f32[8,64,128]{2,1,0:T(8,128)} %get-tuple-element.113), channel_id=1, source_target_pairs={{0,8},{4,12},{8,0},{12,4},{1,9},{5,13},{9,1},{13,5},{2,10},{6,14},... | collective-permute-start | bytes 786440 | tf_op jit(solution)/shard_map/ppermute | solution.py:429
  243.6 19.5 %collective-permute-start.60 = (f32[8,64,128]{2,1,0:T(8,128)}, f32[8,64,128]{2,1,0:T(8,128)}, u32[]{:S(2)}, u32[]{:S(2)}) collective-permute-start(f32[8,64,128]{2,1,0:T(8,128)} %get-tuple-element.114), channel_id=1, source_target_pairs={{0,12},{4,8},{8,4},{12,0},{1,13},{5,9},{9,5},{13,1},{2,14},{6,10},... | collective-permute-start | bytes 786440 | tf_op jit(solution)/shard_map/ppermute | solution.py:429
  251.6 39.8 %collective-permute-start.52 = (f32[8,64,128]{2,1,0:T(8,128)}, f32[8,64,128]{2,1,0:T(8,128)S(1)}, u32[]{:S(2)}, u32[]{:S(2)}) collective-permute-start(f32[8,64,128]{2,1,0:T(8,128)} %get-tuple-element.104), channel_id=1, source_target_pairs={{0,4},{4,0},{8,12},{12,8},{1,5},{5,1},{9,13},{13,9},{2,6},{6,2},{1... | collective-permute-start | bytes 786440 | tf_op jit(solution)/shard_map/ppermute | solution.py:429
  251.6 41.2 %collective-permute-start.53 = (f32[8,64,128]{2,1,0:T(8,128)}, f32[8,64,128]{2,1,0:T(8,128)S(1)}, u32[]{:S(2)}, u32[]{:S(2)}) collective-permute-start(f32[8,64,128]{2,1,0:T(8,128)} %get-tuple-element.105), channel_id=1, source_target_pairs={{0,8},{4,12},{8,0},{12,4},{1,9},{5,13},{9,1},{13,5},{2,10},{6,14},... | collective-permute-start | bytes 786440 | tf_op jit(solution)/shard_map/ppermute | solution.py:429
  254.9 38.0 %collective-permute-start.54 = (f32[8,64,128]{2,1,0:T(8,128)}, f32[8,64,128]{2,1,0:T(8,128)S(1)}, u32[]{:S(2)}, u32[]{:S(2)}) collective-permute-start(f32[8,64,128]{2,1,0:T(8,128)} %get-tuple-element.106), channel_id=1, source_target_pairs={{0,12},{4,8},{8,4},{12,0},{1,13},{5,9},{9,5},{13,1},{2,14},{6,10},... | collective-permute-start | bytes 786440 | tf_op jit(solution)/shard_map/ppermute | solution.py:429
  273.5 41.0 %collective-permute-start.61 = (f32[8,64,128]{2,1,0:T(8,128)}, f32[8,64,128]{2,1,0:T(8,128)S(1)}, u32[]{:S(2)}, u32[]{:S(2)}) collective-permute-start(f32[8,64,128]{2,1,0:T(8,128)} %get-tuple-element.116), channel_id=1, source_target_pairs={{0,4},{4,0},{8,12},{12,8},{1,5},{5,1},{9,13},{13,9},{2,6},{6,2},{1... | collective-permute-start | bytes 786440 | tf_op jit(solution)/shard_map/ppermute | solution.py:429
  290.4 25.6 %collective-permute-start.62 = (f32[8,64,128]{2,1,0:T(8,128)}, f32[8,64,128]{2,1,0:T(8,128)S(1)}, u32[]{:S(2)}, u32[]{:S(2)}) collective-permute-start(f32[8,64,128]{2,1,0:T(8,128)} %get-tuple-element.117), channel_id=1, source_target_pairs={{0,8},{4,12},{8,0},{12,4},{1,9},{5,13},{9,1},{13,5},{2,10},{6,14},... | collective-permute-start | bytes 786440 | tf_op jit(solution)/shard_map/ppermute | solution.py:429
  291.4 24.6 %collective-permute-start.63 = (f32[8,64,128]{2,1,0:T(8,128)}, f32[8,64,128]{2,1,0:T(8,128)}, u32[]{:S(2)}, u32[]{:S(2)}) collective-permute-start(f32[8,64,128]{2,1,0:T(8,128)} %get-tuple-element.118), channel_id=1, source_target_pairs={{0,12},{4,8},{8,4},{12,0},{1,13},{5,9},{9,5},{13,1},{2,14},{6,10},... | collective-permute-start | bytes 786440 | tf_op jit(solution)/shard_map/ppermute | solution.py:429
  303.5 21.4 %collective-permute-start.55 = (f32[8,64,128]{2,1,0:T(8,128)}, f32[8,64,128]{2,1,0:T(8,128)S(1)}, u32[]{:S(2)}, u32[]{:S(2)}) collective-permute-start(f32[8,64,128]{2,1,0:T(8,128)} %get-tuple-element.108), channel_id=1, source_target_pairs={{0,4},{4,0},{8,12},{12,8},{1,5},{5,1},{9,13},{13,9},{2,6},{6,2},{1... | collective-permute-start | bytes 786440 | tf_op jit(solution)/shard_map/ppermute | solution.py:429
  307.9 22.6 %collective-permute-start.56 = (f32[8,64,128]{2,1,0:T(8,128)}, f32[8,64,128]{2,1,0:T(8,128)S(1)}, u32[]{:S(2)}, u32[]{:S(2)}) collective-permute-start(f32[8,64,128]{2,1,0:T(8,128)} %get-tuple-element.109), channel_id=1, source_target_pairs={{0,8},{4,12},{8,0},{12,4},{1,9},{5,13},{9,1},{13,5},{2,10},{6,14},... | collective-permute-start | bytes 786440 | tf_op jit(solution)/shard_map/ppermute | solution.py:429
  314.5 15.9 %collective-permute-start.57 = (f32[8,64,128]{2,1,0:T(8,128)}, f32[8,64,128]{2,1,0:T(8,128)S(1)}, u32[]{:S(2)}, u32[]{:S(2)}) collective-permute-start(f32[8,64,128]{2,1,0:T(8,128)} %get-tuple-element.110), channel_id=1, source_target_pairs={{0,12},{4,8},{8,4},{12,0},{1,13},{5,9},{9,5},{13,1},{2,14},{6,10},... | collective-permute-start | bytes 786440 | tf_op jit(solution)/shard_map/ppermute | solution.py:429
  348.3 13.2 %collective-permute-start.66 = (f32[8,64,128]{2,1,0:T(8,128)S(1)}, f32[8,64,128]{2,1,0:T(8,128)S(1)}, u32[]{:S(2)}, u32[]{:S(2)}) collective-permute-start(f32[8,64,128]{2,1,0:T(8,128)S(1)} %add.338), channel_id=1, source_target_pairs={{0,2},{1,3},{2,0},{3,1},{4,6},{5,7},{6,4},{7,5},{8,10},{9,11},{10,... | collective-permute-start | bytes 786440 | tf_op jit(solution)/shard_map/ppermute | solution.py:429
  354.5 15.2 %collective-permute-start.71 = (f32[4,64,128]{2,1,0:T(8,128)S(1)}, f32[4,64,128]{2,1,0:T(8,128)S(1)}, u32[]{:S(2)}, u32[]{:S(2)}) collective-permute-start(f32[4,64,128]{2,1,0:T(8,128)S(1)} %get-tuple-element.130), channel_id=1, source_target_pairs={{0,8},{4,12},{8,0},{12,4},{1,9},{5,13},{9,1},{13,5},{2,10},{6,14},... | collective-permute-start | bytes 393224 | tf_op jit(solution)/shard_map/ppermute | solution.py:429
  375.9 13.7 %collective-permute-start.73 = (f32[4,256,128]{2,1,0:T(8,128)}, f32[4,256,128]{2,1,0:T(8,128)S(1)}, u32[]{:S(2)}, u32[]{:S(2)}) collective-permute-start(f32[4,256,128]{2,1,0:T(8,128)} %update_step.3), channel_id=1, source_target_pairs={{0,2},{1,3},{2,0},{3,1},{4,6},{5,7},{6,4},{7,5},{8,10},{9,11},{10,... | collective-permute-start | bytes 1572872 | tf_op jit(solution)/shard_map/ppermute | solution.py:429
  377.1 12.8 %collective-permute-start.74 = (f32[4,256,128]{2,1,0:T(8,128)}, f32[4,256,128]{2,1,0:T(8,128)}, u32[]{:S(2)}, u32[]{:S(2)}) collective-permute-start(f32[4,256,128]{2,1,0:T(8,128)} %update_step.3), channel_id=1, source_target_pairs={{0,1},{1,0},{2,3},{3,2},{4,5},{5,4},{6,7},{7,6},{8,9},{9,8},{10,11... | collective-permute-start | bytes 1572872 | tf_op jit(solution)/shard_map/ppermute | solution.py:429
  (109 other events, 613.9 us)

commit v3 on v2

v3 whole, which is shorter than its diff:
```python
import jax
import jax.numpy as jnp
import ml_dtypes
import numpy as np
from jax import lax
from jax.experimental import pallas as pl
from jax.experimental.pallas import tpu as pltpu
from jax.sharding import PartitionSpec as P

ITERS = 2
INTERPRET = False
VMEM_LIMIT = 16 * 2**20


def split_np(matrix):
    high = matrix.astype(ml_dtypes.bfloat16)
    low = (matrix - high.astype(np.float64)).astype(ml_dtypes.bfloat16)
    return high, low


def three_np(matrix):
    high, low = split_np(matrix)
    return np.concatenate([high, high, low], axis=1)


def angles_np(length):
    index = np.arange(length)
    return (np.outer(index, index) % length) * (2.0 * np.pi / length)


def column_tables(length, scale):
    half = length // 2
    angles = angles_np(length)
    cosines, sines = np.cos(angles), np.sin(angles)
    alternating = np.where(np.arange(length) % 2 == 0, 1.0, -1.0)
    forward = np.zeros((length, length))
    forward[:, :half] = cosines[:, :half]
    forward[:, half:] = -sines[:, :half]
    forward[:, half] = alternating
    inverse = np.zeros((length, length))
    inverse[:half] = 2.0 * cosines[:half]
    inverse[half:] = -2.0 * sines[:half]
    inverse[0] = 1.0
    inverse[half] = alternating
    inverse *= scale
    tables = []
    for matrix in (forward, inverse):
        high, low = split_np(matrix)
        both = np.concatenate([high, low], axis=1)
        tables.append(np.concatenate([both, both], axis=0))
    return tables


def row_tables(length, lanes):
    middle, half = length // 2, lanes // 2
    angles = angles_np(length)
    cosines, sines = np.cos(angles), np.sin(angles)
    sines[0] = -cosines[middle]
    sines[middle] = -cosines[0]
    forward = three_np(np.concatenate([cosines, sines], axis=0))
    inverse = three_np(np.concatenate([cosines.T, sines.T], axis=1))
    row = np.arange(length)[:, None]
    lane = np.arange(lanes)[None, :]
    plain = (lane % half) != 0
    lower = row < middle
    inner = (row % middle) != 0
    first, second = lane == 0, lane == half
    sign = np.where(lane < half, 1.0, -1.0)
    weight = np.where(inner, 2.0, 1.0)
    one = np.ones((length, lanes))
    forward_masks = np.stack(
        [
            one * (plain | (first & lower)),
            one * (first & ~lower),
            -one * (second & ~lower),
            sign * (plain & inner) - one * (second & lower),
        ]
    )
    inverse_masks = np.stack(
        [
            one * plain + weight * (first & lower),
            weight * (second & ~lower),
            -weight * (second & ~lower),
            -sign * (plain & inner) - weight * (first & lower),
        ]
    )
    return forward, inverse, forward_masks.astype(np.float32), inverse_masks.astype(np.float32)


def depth_tables(depth, order):
    angles = angles_np(depth)[:, order]
    forward = np.concatenate([np.cos(angles), np.sin(angles)], axis=0)
    inverse = np.concatenate([np.cos(angles.T), np.sin(angles.T)], axis=0)
    return jnp.asarray(three_np(forward)), jnp.asarray(three_np(inverse))


def split(value):
    high = value.astype(jnp.bfloat16)
    low = (value - high.astype(jnp.float32)).astype(jnp.bfloat16)
    return high, low


def three(value):
    high, low = split(value)
    return jnp.concatenate([high, low, high], axis=0)


def dot(left, right):
    return lax.dot_general(
        left, right, (((1,), (0,)), ((), ())), preferred_element_type=jnp.float32
    )


def along_columns(planes, columns):
    rows = planes[0].shape[0]
    value = dot(jnp.concatenate(split(jnp.concatenate(planes, axis=0)), axis=1), columns[...])
    lanes = value.shape[1] // 2
    value = value[:, :lanes] + value[:, lanes:]
    return [value[i * rows : (i + 1) * rows] for i in range(len(planes))]


def along_rows(planes, table):
    lanes = planes[0].shape[1]
    value = dot(table[...], three(jnp.concatenate(planes, axis=1)))
    return [value[:, i * lanes : (i + 1) * lanes] for i in range(len(planes))]


def planes_forward(planes, columns, rows, masks):
    spectra = []
    for both in along_rows(along_columns(planes, columns), rows):
        count, half = both.shape[0] // 2, both.shape[1] // 2
        cos_part, sin_part = both[:count], both[count:]
        spectra.append(
            cos_part * masks[0]
            + pltpu.roll(cos_part, half, 1) * masks[1]
            + sin_part * masks[2]
            + pltpu.roll(sin_part, half, 1) * masks[3]
        )
    return spectra


def planes_inverse(spectra, columns, rows, masks):
    sides = []
    for spectrum in spectra:
        rolled = pltpu.roll(spectrum, spectrum.shape[1] // 2, 1)
        sides.append(
            jnp.concatenate(
                [spectrum * masks[0] + rolled * masks[1], spectrum * masks[2] + rolled * masks[3]],
                axis=0,
            )
        )
    return along_columns(along_rows(sides, rows), columns)


VMEM = pl.BlockSpec(memory_space=pltpu.VMEM)
SMEM = pl.BlockSpec(memory_space=pltpu.SMEM)
ANY = pl.BlockSpec(memory_space=pl.ANY)


def flipped(ids_ref, axis, flip, count):
    return pl.multiple_of(jnp.bitwise_xor(ids_ref[axis], flip) * count, count)


def lateral_call(body, ids, operands, pieces, places, constants, shape, out_planes, out_places):
    planes, rows, lanes, part_rows = shape
    step = 2 if planes % 2 == 0 else 1

    def kernel(ids_ref, *refs):
        spans = np.cumsum(
            [0, len(operands), len(pieces), len(constants), out_planes, len(out_places), step, step]
        )
        groups = [refs[a:b] for a, b in zip(spans[:-1], spans[1:])]
        ins, piece_refs, constant_refs, plane_refs, out_refs, scratch_in, scratch_out = groups

        def row_range(place):
            k, first, count = place
            return pl.ds(pl.multiple_of(flipped(ids_ref, 0, k, part_rows) + first, count), count)

        def turn(number, carry):
            indices = [number * step + i for i in range(step)]

            def read():
                for i, index in enumerate(indices):
                    for place, ref in zip(places, piece_refs):
                        scratch_in[i][row_range(place), :] = ref[index]
                return [scratch[...] for scratch in scratch_in]

            def write(values):
                for i, index in enumerate(indices):
                    scratch_out[i][...] = values[i]
                    for place, ref in zip(out_places, out_refs):
                        ref[index] = scratch_out[i][row_range(place), :]

            body(indices, ins, read, constant_refs, plane_refs, write)
            return carry

        lax.fori_loop(0, planes // step, turn, 0)

    return pl.pallas_call(
        kernel,
        in_specs=[SMEM] + [VMEM] * (len(operands) + len(pieces) + len(constants)),
        out_specs=[VMEM] * (out_planes + len(out_places)),
        scratch_shapes=[pltpu.VMEM((rows, lanes), jnp.float32)] * (2 * step),
        out_shape=[jax.ShapeDtypeStruct((planes, rows, lanes), jnp.float32)] * out_planes
        + [jax.ShapeDtypeStruct((planes, place[2], lanes), jnp.float32) for place in out_places],
        interpret=INTERPRET,
        compiler_params=pltpu.CompilerParams(vmem_limit_bytes=VMEM_LIMIT),
    )(ids, *operands, *pieces, *constants)


def lateral_forward(volume, ids, tables, part_rows, out_places):
    def body(indices, ins, read, constants, _, write):
        write(planes_forward([ins[0][i] for i in indices], *constants))

    return lateral_call(
        body, ids, [volume], [], [], tables["forward"],
        volume.shape + (part_rows,), 0, out_places,
    )


def ratio_step(pieces, places, observed, valid, offset, ids, tables, part_rows, out_places):
    planes = pieces[0].shape[0]

    def body(indices, ins, read, constants, _, write):
        ratios = []
        for index, blurred in zip(indices, planes_inverse(read(), *constants[:3])):
            mask = ins[1][offset + index].astype(jnp.float32)
            ratios.append(mask * ins[0][offset + index] / blurred + (1.0 - mask))
        write(planes_forward(ratios, *constants[3:]))

    return lateral_call(
        body, ids, [observed, valid], pieces, places,
        tables["inverse"] + tables["forward"], (planes,) + observed.shape[1:] + (part_rows,), 0, out_places,
    )


def update_step(pieces, places, estimate, view_count, ids, tables, part_rows, out_places):
    last = not out_places

    def body(indices, ins, read, constants, outs, write):
        updated = []
        for index, combined in zip(indices, planes_inverse(read(), *constants[:3])):
            updated.append(ins[0][index] * combined / view_count)
            outs[0][index] = updated[-1]
        if not last:
            write(planes_forward(updated, *constants[3:]))

    constants = tables["inverse"] + (() if last else tables["forward"])
    results = lateral_call(
        body, ids, [estimate], pieces, places, constants,
        estimate.shape + (part_rows,), 1, out_places,
    )
    return results[0], results[1:]


BLOCK_ROWS = 8


def depth_step(ids, pieces, places, added, transfer, forward, inverse, outs, keep, adjoint, span, shape):
    main, cross = transfer
    _, _, depth, lanes = main.shape
    first_row, rows = shape
    half = lanes // 2
    block = BLOCK_ROWS
    in_count = forward.shape[1] // 3
    out_count = inverse.shape[0] // 2
    operands = list(pieces)
    if pieces:
        operands += [main, cross, forward]
    if added is not None:
        operands.append(added)
    if outs:
        operands.append(inverse)
    out_shape = [
        jax.ShapeDtypeStruct((sum(place[1] for place in places_), rows, lanes), jnp.float32)
        for places_ in outs
    ]
    if keep:
        out_shape.append(jax.ShapeDtypeStruct((rows, depth, lanes), jnp.float32))
    side = -1.0 if adjoint else 1.0
    scratch = []
    if pieces:
        scratch.append(pltpu.VMEM((in_count * rows, lanes), jnp.float32))
    if outs:
        scratch.append(pltpu.VMEM((out_count * rows, lanes), jnp.float32))

    def body(ids_ref, *refs):
        refs = list(refs)
        ins = [refs.pop(0) for _ in pieces]
        if pieces:
            main_ref, cross_ref, forward_ref = refs.pop(0), refs.pop(0), refs.pop(0)
        added_ref = refs.pop(0) if added is not None else None
        inverse_ref = refs.pop(0) if outs else None
        out_refs = [refs.pop(0) for _ in outs]
        keep_ref = refs.pop(0) if keep else None
        gathered = refs.pop(0) if pieces else None
        grown_out = refs.pop(0) if outs else None

        def planes_of(place, span):
            _, count, k, extra, flip, share = place
            start = flipped(ids_ref, 0, k, span) + extra
            if share:
                start = start + flipped(ids_ref, 1, flip, share)
            return lambda turn, total: pl.ds(
                pl.multiple_of((turn * total + start) * block, count * block), count * block
            )

        def sign(count):
            lane = lax.broadcasted_iota(jnp.int32, (count, lanes), 1)
            return jnp.where(lane < half, 1.0, -1.0)

        for ref, places_ in zip(ins, places):
            for place in places_:
                count = place[1]
                at = planes_of(place, span[0])
                for turn in range(rows // block):
                    gathered[at(turn, in_count), :] = ref[
                        place[0] : place[0] + count, turn * block : (turn + 1) * block
                    ].reshape(count * block, lanes)

        def some(turn, carry):
            for pair in range(block // 2):
                one_pair(turn, (2 * pair, 2 * pair + 1))
            return carry

        def one_pair(turn, lines):
            ks = [turn * block + line for line in lines]
            results = []
            if pieces:
                both = jnp.concatenate(
                    [
                        gathered[pl.ds(turn * in_count * block + line, in_count, stride=block), :]
                        for line in lines
                    ],
                    axis=1,
                )
                grown = dot(forward_ref[...], three(both))
                for index, k in enumerate(ks):
                    lanes_of = slice(index * lanes, (index + 1) * lanes)
                    cos_part, sin_part = grown[:depth, lanes_of], grown[depth:, lanes_of]
                    sin_roll = pltpu.roll(sin_part, half, 1)
                    spectrum = cos_part + sign(depth) * sin_roll
                    result = (
                        spectrum * main_ref[0, first_row + k]
                        + pltpu.roll(spectrum, half, 1) * (main_ref[1, first_row + k] * side)
                    )
                    if lines[index] == 0 and first_row == 0:
                        change = sign(depth) * cos_part - sin_roll - spectrum
                        extra = (
                            change * cross_ref[0]
                            + pltpu.roll(change, half, 1) * cross_ref[1] * side
                        )
                        result = result + jnp.where(turn == 0, extra, 0.0)
                    if added is not None:
                        result = result + added_ref[first_row + k]
                    results.append(result)
            else:
                results = [added_ref[first_row + k] for k in ks]
            if keep:
                for k, result in zip(ks, results):
                    keep_ref[k] = result
            if not outs:
                return
            grown = dot(inverse_ref[...], three(jnp.concatenate(results, axis=1)))
            for index, k in enumerate(ks):
                lanes_of = slice(index * lanes, (index + 1) * lanes)
                cos_part, sin_part = grown[:out_count, lanes_of], grown[out_count:, lanes_of]
                grown_out[
                    pl.ds(turn * out_count * block + lines[index], out_count, stride=block), :
                ] = cos_part - sign(
                    out_count
                ) * pltpu.roll(sin_part, half, 1)

        lax.fori_loop(0, rows // block, some, 0)
        for ref, places_ in zip(out_refs, outs):
            for place in places_:
                count = place[1]
                at = planes_of(place, span[1])
                for turn in range(rows // block):
                    ref[place[0] : place[0] + count, turn * block : (turn + 1) * block] = grown_out[
                        at(turn, out_count), :
                    ].reshape(count, block, lanes)

    results = pl.pallas_call(
        body,
        out_shape=out_shape,
        in_specs=[SMEM] + [VMEM] * len(operands),
        out_specs=[VMEM] * len(out_shape),
        scratch_shapes=scratch,
        interpret=INTERPRET,
        compiler_params=pltpu.CompilerParams(vmem_limit_bytes=VMEM_LIMIT),
        name="depth_step",
    )(ids, *operands)
    return results[: len(outs)], (results[-1] if keep else None)


def rows_of(ref, k):
    planes, count, lanes = ref.shape
    return ref.reshape(planes * count, lanes).at[pl.ds(k, planes, stride=count), :]


def cross_tables(first, space_count):
    _, depth, lanes = first.shape
    half = lanes // 2
    device = lax.axis_index("space")
    upper = device >= space_count // 2
    special = (device % (space_count // 2)) == 0
    other = lax.ppermute(first, "space", [(0, space_count // 2), (space_count // 2, 0)])
    change = jnp.where(special, 0.5 * (first - other), 0.0)
    column = jnp.where(upper, change[:, :, half], change[:, :, 0])[:, :, None]
    lane = lax.broadcasted_iota(jnp.int32, (depth, lanes), 1)
    return jnp.stack(
        [
            jnp.where(lane % half == 0, column[0], 0.0),
            jnp.where(lane == 0, -column[1], jnp.where(lane == half, column[1], 0.0)),
        ]
    )


def transfer_table(psf, after, ids, space_count):
    _, depth, rows, lanes = psf.shape
    half = lanes // 2
    block = BLOCK_ROWS

    def body(ids_ref, psf_ref, _, main_ref):
        lane = lax.broadcasted_iota(jnp.int32, (depth, lanes), 1)
        first_lanes = (lane % half == 0) & (ids_ref[0] >= space_count // 2)
        for k in range(block):
            for part in range(2):
                value = rows_of(psf_ref.at[part], k)[...]
                rolled = pltpu.roll(value, half, 1)
                doubled = jnp.where(lane < half, value, rolled)
                other = jnp.where(lane < half, rolled, value)
                packed = jnp.where(first_lanes, other, doubled)
                if part == 1:
                    packed = jnp.where(lane < half, -packed, packed)
                main_ref[part, k] = packed

    return pl.pallas_call(
        body,
        grid_spec=pltpu.PrefetchScalarGridSpec(
            num_scalar_prefetch=1,
            grid=(rows // block,),
            in_specs=[
                pl.BlockSpec((2, depth, block, lanes), lambda i, *_: (0, 0, i, 0)),
                pl.BlockSpec(memory_space=pl.ANY),
            ],
            out_specs=pl.BlockSpec((2, block, depth, lanes), lambda i, *_: (0, i, 0, 0)),
        ),
        out_shape=jax.ShapeDtypeStruct((2, rows, depth, lanes), jnp.float32),
        interpret=INTERPRET,
        compiler_params=pltpu.CompilerParams(vmem_limit_bytes=VMEM_LIMIT),
        name="transfer_table",
    )(ids, psf, after)


def send(array, axis, count, flip):
    if flip == 0:
        return array
    return lax.ppermute(array, axis, [(i, i ^ flip) for i in range(count)])


def join_planes(ids, copies, flips, planes):
    share, rows, lanes = copies[0].shape
    count = len(copies)

    def body(ids_ref, *refs):
        ins, out_ref, sems = refs[:count], refs[count], refs[count + 1]
        moves = [
            pltpu.make_async_copy(
                ref, out_ref.at[pl.ds(flipped(ids_ref, 1, flip, share), share)], sems.at[i]
            )
            for i, (ref, flip) in enumerate(zip(ins, flips))
        ]
        for move in moves:
            move.start()
        for move in moves:
            move.wait()

    return pl.pallas_call(
        body,
        out_shape=jax.ShapeDtypeStruct((planes, rows, lanes), jnp.float32),
        in_specs=[SMEM] + [ANY] * count,
        out_specs=ANY,
        scratch_shapes=[pltpu.SemaphoreType.DMA((count,))],
        interpret=INTERPRET,
        compiler_params=pltpu.CompilerParams(vmem_limit_bytes=VMEM_LIMIT),
        name="join_planes",
    )(ids, *copies)


def shards(estimate, observed, valid, psf_spectrum):
    space_count = lax.axis_size("space")
    views = lax.axis_size("view")
    planes, row_total, lanes = estimate.shape
    depth = planes * space_count
    part_rows = row_total // space_count
    view_count = views * observed.shape[0]
    columns_f, columns_i = column_tables(lanes, 1.0 / (depth * row_total * lanes))
    rows_f, rows_i, masks_f, masks_i = row_tables(row_total, lanes)
    tables = {
        "forward": (jnp.asarray(columns_f), jnp.asarray(rows_f), jnp.asarray(masks_f)),
        "inverse": (jnp.asarray(columns_i), jnp.asarray(rows_i), jnp.asarray(masks_i)),
    }
    observed, valid = observed[0], valid[0]
    ids = jnp.stack([lax.axis_index("space"), lax.axis_index("view")]).astype(jnp.int32)

    shared = planes % views == 0 and views & (views - 1) == 0
    blocks = views if shared else 1
    share = planes // blocks
    strides = [1 << bit for bit in range(blocks.bit_length() - 1)]
    flips = [0]
    for stride in reversed(strides):
        flips = flips + [f ^ stride for f in flips]
    ks = list(range(space_count))
    chunk = planes // 2 if planes % 2 == 0 else planes
    starts = list(range(0, planes, chunk))
    part = part_rows // 2 if part_rows % (2 * BLOCK_ROWS) == 0 else part_rows
    whole_rows = [(0, part_rows)]
    half_rows = [(first, part) for first in range(0, part_rows, part)]

    def row_places(ranges):
        return [(k, first, count) for first, count in ranges for k in ks]

    slabs = np.arange(space_count)[:, None] * planes
    full_tables = depth_tables(depth, np.arange(depth))
    chunk_tables = [
        depth_tables(depth, (slabs + start + np.arange(chunk)[None, :]).reshape(-1)) for start in starts
    ]
    chunk_places = [[(0, chunk, k, 0, 0, 0)] for k in ks]
    view_share = share if shared else 0

    cross = cross_tables(psf_spectrum[0, :, :, 0, :], space_count)
    own = lax.dynamic_slice_in_dim(estimate, ids[1] * share, share, 0) if shared else estimate
    spectrum = lateral_forward(own, ids, tables, part_rows, row_places(whole_rows))
    main = transfer_table(psf_spectrum[0], spectrum[0], ids, space_count)
    transfer = (main, cross)

    def spread(pieces):
        moved = {k: send(pieces[k], "space", space_count, k) for k in reversed(ks)}
        return [moved[k] for k in ks]

    for iteration in range(ITERS):
        last = iteration == ITERS - 1
        pieces, places = [], []
        for k, piece in enumerate(spread(spectrum)):
            copies = [piece]
            for stride in reversed(strides):
                copies = copies + [send(c, "view", views, stride) for c in copies]
            pieces += copies
            places += [[(0, share, k, 0, flip, view_share)] for flip in flips]
        outs, _ = depth_step(
            ids, pieces, places, None, transfer, full_tables[0], full_tables[1],
            [[(0, chunk, k, start, 0, 0)] for start in starts for k in ks],
            False, False, (planes, planes), (0, part_rows),
        )
        ratios = []
        for number, start in enumerate(starts):
            final = number == len(starts) - 1
            ratios.append(
                ratio_step(
                    spread(outs[number * space_count : (number + 1) * space_count]), row_places(whole_rows),
                    observed, valid, start, ids, tables, part_rows,
                    row_places(half_rows if final else whole_rows),
                )
            )
        kept = None
        for number, ratio in enumerate(ratios[:-1]):
            arrived = spread(ratio)
            _, kept = depth_step(
                ids, arrived, chunk_places, kept, transfer, chunk_tables[number][0], full_tables[1],
                [], True, True, (chunk, planes), (0, part_rows),
            )
        arrived = []
        for number in range(len(half_rows)):
            arrived.append(spread(ratios[-1][number * space_count : (number + 1) * space_count]))
        combined = []
        for number, shape in enumerate(half_rows):
            parts, _ = depth_step(
                ids, arrived[number], chunk_places, kept, transfer,
                chunk_tables[-1][0], full_tables[1],
                [[(k * share, share, k, 0, flip, view_share) for k in ks] for flip in flips],
                False, True, (chunk, planes), shape,
            )
            for stride in strides:
                middle = len(parts) // 2
                moved = [send(p, "view", views, stride) for p in parts[middle:]]
                if middle == 1:
                    parts = [parts[0][k * share : (k + 1) * share] + moved[0][k * share : (k + 1) * share] for k in ks]
                else:
                    parts = [own_part + new for own_part, new in zip(parts[:middle], moved)]
            if not strides:
                total = parts[0] if shared else lax.psum(parts[0], "view")
                parts = [total[k * share : (k + 1) * share] for k in ks]
            combined += spread(parts)
        own, spectrum = update_step(
            combined, row_places(half_rows), own, float(view_count), ids, tables, part_rows,
            [] if last else row_places(whole_rows),
        )
    if not shared:
        return own
    copies = [own]
    for stride in reversed(strides):
        copies = copies + [send(c, "view", views, stride) for c in copies]
    return join_planes(ids, copies, flips, planes)


def solution(mesh):
    return jax.shard_map(
        shards,
        mesh=mesh,
        in_specs=(
            P("space", "blocks", None),
            P("view", "space", "blocks", None),
            P("view", "space", "blocks", None),
            P("view", None, None, "space", None),
        ),
        out_specs=P("space", "blocks", None),
        check_vma=False,
    )
```

time: 396 us -> 359 us (0.907)
  Pallas kernels: 143 us -> 76 us
  waiting for transfers between devices: 83.8 us -> 119 us
  starting transfers between devices: 131 us -> 147 us
  other arithmetic: 17.8 us -> 2.71 us
  local copies, waits for them, and re-layouts: 18.1 us -> 12.3 us
    pallas_call x16 -> x17, Pallas kernels: 143 us -> 76 us  [the longest x7 37.1 us: lateral_call(): pl.pallas_call(kernel, in_specs=[SMEM] + [VMEM] * (len(operands) + len(pi...]
    ppermute x75 -> x87, waiting for transfers between devices: 80.9 us -> 119 us  [send(): return lax.ppermute(array, axis, [(i, i ^ flip) for i in range(count)])]
    ppermute x75 -> x87, starting transfers between devices: 126 us -> 145 us  [send(): return lax.ppermute(array, axis, [(i, i ^ flip) for i in range(count)])]
    add x16 -> x13, other arithmetic: 7.72 us -> 0.94 us  [the longest x1 0.51 us: cross_tables(): lane % half == 0]
    concatenate x6 -> x0, other arithmetic: 4.26 us -> none  [depth_table(): return jnp.concatenate([both, both], axis=1).astype(jnp.bfloat16)]
    unnamed x130 -> x38, local copies, waits for them, and re-layouts: 12.3 us -> 11 us
  transfers between devices with their start and end apart: 76 -> 88, of which waited for: 26 -> 30; matrix products, arithmetic and copies ran while one was open for 5% -> 1% of each run, Pallas kernels for 19% -> 13%
where the time goes in v3:
time: 359 us; the launch traced here: 358 us
  starting transfers between devices  147 us (41%)
  waiting for transfers between devices  119 us (33%)
  Pallas kernels  76 us (21%)
  local copies, waits for them, and re-layouts  12.3 us (3%)
    ppermute x87, starting transfers between devices, send(): return lax.ppermute(array, axis, [(i, i ^ flip) for i in range(count)])  145 us
    ppermute x87, waiting for transfers between devices, send(): return lax.ppermute(array, axis, [(i, i ^ flip) for i in range(count)])  119 us
    pallas_call x7, Pallas kernels, lateral_call(): pl.pallas_call(kernel, in_specs=[SMEM] + [VMEM] * (len(operands) + len(pi...  37.1 us
    pallas_call x8, Pallas kernels, depth_step(): pl.pallas_call(body, out_shape=out_shape, in_specs=[SMEM] + [VMEM] * len(...  34 us
    unnamed x38, local copies, waits for them, and re-layouts  11 us
  transfers between devices with their start and end apart: 88, of which 30 were waited for; matrix products, arithmetic and copies ran while one was open for 1% of the time, Pallas kernels for 13%

profile of v3, /device:TPU:0, one launch (start us, length us, event | category | flops | bytes accessed | tf_op | source)
XLA Modules:
  0.0 358.1 jit_solution(12259694418032975598)
XLA Ops:
  29.4 3.4 collective-permute-done.11.refs_12_
  41.4 6.4 %depth_step.8 = (f32[8,64,128]{2,1,0:T(8,128)S(1)}, f32[8,64,128]{2,1,0:T(8,128)S(1)}, f32[8,64,128]{2,1,0:T(8,128)S(1)}, f32[8,64,128]{2,1,0:T(8,128)S(1)}, f32...) custom-call(s32[2]{0:T(128)S(1)} %pad_add_fusion.ids_ref, ...), custom_call_target="tpu_custom_call" | custom-call | tf_op jit(solution)/shard_map/depth_step/pallas_call | solution.py:384
  56.3 5.8 %collective-permute-done.22.refs_3_ = f32[8,64,128]{2,1,0:T(8,128)S(1)} collective-permute-done((f32[8,64,128]{2,1,0:T(8,128)S(1)}, f32[8,64,128]{2,1,0:T(8,128)S(1)}, u32[]{:S(2)}, u32[]{:S(2)}) %collective-permute-start.22) | collective-permute-done | bytes 262176 | tf_op jit(solution)/shard_map/ppermute | solution.py:460
  62.0 3.6 collective-permute-start.18
  65.6 6.4 %collective-permute-done.23.refs_4_ = f32[8,64,128]{2,1,0:T(8,128)S(1)} collective-permute-done((f32[8,64,128]{2,1,0:T(8,128)S(1)}, f32[8,64,128]{2,1,0:T(8,128)S(1)}, u32[]{:S(2)}, u32[]{:S(2)}) %collective-permute-start.23) | collective-permute-done | bytes 262176 | tf_op jit(solution)/shard_map/ppermute | solution.py:460
  72.1 7.1 %shard_map.138 = (f32[8,64,128]{2,1,0:T(8,128)S(1)}, f32[8,64,128]{2,1,0:T(8,128)S(1)}, f32[8,64,128]{2,1,0:T(8,128)S(1)}, f32[8,64,128]{2,1,0:T(8,128)S(1)}) custom-call(s32[2]{0:T(128)S(1)} %pad_add_fusion.ids_ref, f32[16,256,128]{2,1,0:T(8,128)S(1)} %bitcast.6, s32[16,256,128]{2,1,0:T(8,128)S(1)} %bitcast.10, ...), custom_call_target="tpu_custom_call" | custom-call | tf_op jit(solution)/shard_map/pallas_call | solution.py:199
  79.2 17.5 %collective-permute-start.25 = (f32[8,64,128]{2,1,0:T(8,128)S(1)}, f32[8,64,128]{2,1,0:T(8,128)S(1)}, u32[]{:S(2)}, u32[]{:S(2)}) collective-permute-start(f32[8,64,128]{2,1,0:T(8,128)S(1)} %get-tuple-element.87), channel_id=1, source_target_pairs={{0,4},{4,0},{8,12},{12,8},{1,5},{5,1},{9,13},{13,9},{2,6},{6,2},{1... | collective-permute-start | bytes 786440 | tf_op jit(solution)/shard_map/ppermute | solution.py:460
  99.1 7.1 %shard_map.137 = (f32[8,32,128]{2,1,0:T(8,128)S(1)}, f32[8,32,128]{2,1,0:T(8,128)S(1)}, f32[8,32,128]{2,1,0:T(8,128)S(1)}, f32[8,32,128]{2,1,0:T(8,128)S(1)}, f3...) custom-call(s32[2]{0:T(128)S(1)} %pad_add_fusion.ids_ref, ...), custom_call_target="tpu_custom_call" | custom-call | tf_op jit(solution)/shard_map/pallas_call | solution.py:199
  106.2 10.9 %collective-permute-start.19 = (f32[8,32,128]{2,1,0:T(8,128)S(1)}, f32[8,32,128]{2,1,0:T(8,128)S(1)}, u32[]{:S(2)}, u32[]{:S(2)}) collective-permute-start(f32[8,32,128]{2,1,0:T(8,128)S(1)} %get-tuple-element.79), channel_id=1, source_target_pairs={{0,4},{4,0},{8,12},{12,8},{1,5},{5,1},{9,13},{13,9},{2,6},{6,2},{1... | collective-permute-start | bytes 393224 | tf_op jit(solution)/shard_map/ppermute | solution.py:460
  119.8 3.8 %depth_step.9.refs_7_ = f32[64,64,128]{2,1,0:T(8,128)S(1)} custom-call(s32[2]{0:T(128)S(1)} %pad_add_fusion.ids_ref, f32[8,64,128]{2,1,0:T(8,128)S(1)} %get-tuple-element.86.refs_0_, f32[8,64,128]{2,1,0:T(8,128)S(1)} %collective-permute-done.25.refs_1_, f32[8,64,128]{2,1,0:T(8,128)S(1)} %collective-permute-done.26.refs_2_, ...), custom_call_target="tpu_custom_call" | custom-call | tf_op jit(solution)/shard_map/depth_step/pallas_call | solution.py:384
  123.6 7.4 %collective-permute-done.20.refs_2_ = f32[8,32,128]{2,1,0:T(8,128)S(1)} collective-permute-done((f32[8,32,128]{2,1,0:T(8,128)S(1)}, f32[8,32,128]{2,1,0:T(8,128)S(1)}, u32[]{:S(2)}, u32[]{:S(2)}) %collective-permute-start.20) | collective-permute-done | bytes 131104 | tf_op jit(solution)/shard_map/ppermute | solution.py:460
  131.0 3.4 depth_step.10
  142.2 7.5 %collective-permute-done.35.refs_2_ = f32[8,32,128]{2,1,0:T(8,128)S(1)} collective-permute-done((f32[8,32,128]{2,1,0:T(8,128)S(1)}, f32[8,32,128]{2,1,0:T(8,128)S(1)}, u32[]{:S(2)}, u32[]{:S(2)}) %collective-permute-start.35) | collective-permute-done | bytes 131104 | tf_op jit(solution)/shard_map/ppermute | solution.py:460
  156.1 6.9 %collective-permute-done.30 = f32[16,32,128]{2,1,0:T(8,128)S(1)} collective-permute-done((f32[16,32,128]{2,1,0:T(8,128)S(1)}, f32[16,32,128]{2,1,0:T(8,128)S(1)}, u32[]{:S(2)}, u32[]{:S(2)}) %collective-permute-start.30) | collective-permute-done | bytes 262176 | tf_op jit(solution)/shard_map/ppermute | solution.py:460
  173.8 4.5 %collective-permute-done.41.refs_7_ = f32[4,32,128]{2,1,0:T(8,128)S(1)} collective-permute-done((f32[4,32,128]{2,1,0:T(8,128)S(1)}, f32[4,32,128]{2,1,0:T(8,128)S(1)}, u32[]{:S(2)}, u32[]{:S(2)}) %collective-permute-start.41) | collective-permute-done | bytes 65568 | tf_op jit(solution)/shard_map/ppermute | solution.py:460
  178.3 3.8 %shard_map.139 = (f32[4,256,128]{2,1,0:T(8,128)S(1)}, f32[4,64,128]{2,1,0:T(8,128)S(1)}, f32[4,64,128]{2,1,0:T(8,128)S(1)}, f32[4,64,128]{2,1,0:T(8,128)S(1)}, f32[4,64,128]{2,1,0:T(8,128)S(1)}) custom-call(s32[2]{0:T(128)S(1)} %pad_add_fusion.ids_ref, f32[4,256,128]{2,1,0:T(8,128)S(1)} %constant_dynamic-slice_fusion.refs_0_, ...), custom_call_target="tpu_custom_call" | custom-call | tf_op jit(solution)/shard_map/pallas_call | solution.py:199
  189.2 7.6 %collective-permute-done.50.refs_8_ = f32[4,64,128]{2,1,0:T(8,128)S(1)} collective-permute-done((f32[4,64,128]{2,1,0:T(8,128)S(1)}, f32[4,64,128]{2,1,0:T(8,128)S(1)}, u32[]{:S(2)}, u32[]{:S(2)}) %collective-permute-start.50) | collective-permute-done | bytes 131104 | tf_op jit(solution)/shard_map/ppermute | solution.py:460
  199.4 3.6 %collective-permute-done.51.refs_9_ = f32[4,64,128]{2,1,0:T(8,128)S(1)} collective-permute-done((f32[4,64,128]{2,1,0:T(8,128)S(1)}, f32[4,64,128]{2,1,0:T(8,128)S(1)}, u32[]{:S(2)}, u32[]{:S(2)}) %collective-permute-start.51) | collective-permute-done | bytes 131104 | tf_op jit(solution)/shard_map/ppermute | solution.py:460
  205.7 6.6 %depth_step.12 = (f32[8,64,128]{2,1,0:T(8,128)S(1)}, f32[8,64,128]{2,1,0:T(8,128)S(1)}, f32[8,64,128]{2,1,0:T(8,128)S(1)}, f32[8,64,128]{2,1,0:T(8,128)S(1)}, f3...) custom-call(s32[2]{0:T(128)S(1)} %pad_add_fusion.ids_ref, ...), custom_call_target="tpu_custom_call" | custom-call | tf_op jit(solution)/shard_map/depth_step/pallas_call | solution.py:384
  218.8 7.7 %collective-permute-done.64.refs_3_ = f32[8,64,128]{2,1,0:T(8,128)S(1)} collective-permute-done((f32[8,64,128]{2,1,0:T(8,128)S(1)}, f32[8,64,128]{2,1,0:T(8,128)S(1)}, u32[]{:S(2)}, u32[]{:S(2)}) %collective-permute-start.64) | collective-permute-done | bytes 262176 | tf_op jit(solution)/shard_map/ppermute | solution.py:460
  228.0 6.3 %collective-permute-done.65.refs_4_ = f32[8,64,128]{2,1,0:T(8,128)S(1)} collective-permute-done((f32[8,64,128]{2,1,0:T(8,128)S(1)}, f32[8,64,128]{2,1,0:T(8,128)S(1)}, u32[]{:S(2)}, u32[]{:S(2)}) %collective-permute-start.65) | collective-permute-done | bytes 262176 | tf_op jit(solution)/shard_map/ppermute | solution.py:460
  234.3 7.1 %shard_map.141 = (f32[8,64,128]{2,1,0:T(8,128)S(1)}, f32[8,64,128]{2,1,0:T(8,128)S(1)}, f32[8,64,128]{2,1,0:T(8,128)S(1)}, f32[8,64,128]{2,1,0:T(8,128)S(1)}) custom-call(s32[2]{0:T(128)S(1)} %pad_add_fusion.ids_ref, f32[16,256,128]{2,1,0:T(8,128)S(1)} %bitcast.8, s32[16,256,128]{2,1,0:T(8,128)S(1)} %bitcast.12, ...), custom_call_target="tpu_custom_call" | custom-call | tf_op jit(solution)/shard_map/pallas_call | solution.py:199
  241.4 17.5 %collective-permute-start.67 = (f32[8,64,128]{2,1,0:T(8,128)S(1)}, f32[8,64,128]{2,1,0:T(8,128)S(1)}, u32[]{:S(2)}, u32[]{:S(2)}) collective-permute-start(f32[8,64,128]{2,1,0:T(8,128)S(1)} %get-tuple-element.120), channel_id=1, source_target_pairs={{0,4},{4,0},{8,12},{12,8},{1,5},{5,1},{9,13},{13,9},{2,6},{6,2},{1... | collective-permute-start | bytes 786440 | tf_op jit(solution)/shard_map/ppermute | solution.py:460
  262.4 7.1 %shard_map.140 = (f32[8,32,128]{2,1,0:T(8,128)S(1)}, f32[8,32,128]{2,1,0:T(8,128)S(1)}, f32[8,32,128]{2,1,0:T(8,128)S(1)}, f32[8,32,128]{2,1,0:T(8,128)S(1)}, f3...) custom-call(s32[2]{0:T(128)S(1)} %pad_add_fusion.ids_ref, ...), custom_call_target="tpu_custom_call" | custom-call | tf_op jit(solution)/shard_map/pallas_call | solution.py:199
  269.5 11.9 %collective-permute-start.61 = (f32[8,32,128]{2,1,0:T(8,128)S(1)}, f32[8,32,128]{2,1,0:T(8,128)S(1)}, u32[]{:S(2)}, u32[]{:S(2)}) collective-permute-start(f32[8,32,128]{2,1,0:T(8,128)S(1)} %get-tuple-element.112), channel_id=1, source_target_pairs={{0,4},{4,0},{8,12},{12,8},{1,5},{5,1},{9,13},{13,9},{2,6},{6,2},{1... | collective-permute-start | bytes 393224 | tf_op jit(solution)/shard_map/ppermute | solution.py:460
  283.8 3.8 %depth_step.13.refs_7_ = f32[64,64,128]{2,1,0:T(8,128)S(1)} custom-call(s32[2]{0:T(128)S(1)} %pad_add_fusion.ids_ref, f32[8,64,128]{2,1,0:T(8,128)S(1)} %get-tuple-element.119.refs_0_, f32[8,64,128]{2,1,0:T(8,128)S(1)} %collective-permute-done.67.refs_1_, f32[8,64,128]{2,1,0:T(8,128)S(1)} %collective-permute-done.68.refs_2_, ...), custom_call_target="tpu_custom_call" | custom-call | tf_op jit(solution)/shard_map/depth_step/pallas_call | solution.py:384
  287.6 5.7 %collective-permute-done.62.refs_2_ = f32[8,32,128]{2,1,0:T(8,128)S(1)} collective-permute-done((f32[8,32,128]{2,1,0:T(8,128)S(1)}, f32[8,32,128]{2,1,0:T(8,128)S(1)}, u32[]{:S(2)}, u32[]{:S(2)}) %collective-permute-start.62) | collective-permute-done | bytes 131104 | tf_op jit(solution)/shard_map/ppermute | solution.py:460
  293.3 3.4 depth_step.14
  304.7 7.3 %collective-permute-done.77.refs_2_ = f32[8,32,128]{2,1,0:T(8,128)S(1)} collective-permute-done((f32[8,32,128]{2,1,0:T(8,128)S(1)}, f32[8,32,128]{2,1,0:T(8,128)S(1)}, u32[]{:S(2)}, u32[]{:S(2)}) %collective-permute-start.77) | collective-permute-done | bytes 131104 | tf_op jit(solution)/shard_map/ppermute | solution.py:460
  318.7 6.7 %collective-permute-done.72 = f32[16,32,128]{2,1,0:T(8,128)S(1)} collective-permute-done((f32[16,32,128]{2,1,0:T(8,128)S(1)}, f32[16,32,128]{2,1,0:T(8,128)S(1)}, u32[]{:S(2)}, u32[]{:S(2)}) %collective-permute-start.72) | collective-permute-done | bytes 262176 | tf_op jit(solution)/shard_map/ppermute | solution.py:460
  336.3 4.3 %collective-permute-done.83.refs_7_ = f32[4,32,128]{2,1,0:T(8,128)S(1)} collective-permute-done((f32[4,32,128]{2,1,0:T(8,128)S(1)}, f32[4,32,128]{2,1,0:T(8,128)S(1)}, u32[]{:S(2)}, u32[]{:S(2)}) %collective-permute-start.83) | collective-permute-done | bytes 65568 | tf_op jit(solution)/shard_map/ppermute | solution.py:460
  344.3 9.9 %collective-permute-done.85.refs_1_ = f32[4,256,128]{2,1,0:T(8,128)S(1)} collective-permute-done((f32[4,256,128]{2,1,0:T(8,128)S(1)}, f32[4,256,128]{2,1,0:T(8,128)S(1)}, u32[]{:S(2)}, u32[]{:S(2)}) %collective-permute-start.85) | collective-permute-done | bytes 524320 | tf_op jit(solution)/shard_map/ppermute | solution.py:460
  (225 shorter events, 135.6 us)
Async XLA Ops:
  7.5 19.9 %collective-permute-start = (f32[4,64,128]{2,1,0:T(8,128)S(1)}, f32[4,64,128]{2,1,0:T(8,128)S(1)}, u32[]{:S(2)}, u32[]{:S(2)}) collective-permute-start(f32[4,64,128]{2,1,0:T(8,128)S(1)} %get-tuple-element.70._.refs_0_), channel_id=1, source_target_pairs={{0,2},{1,3},{2,0},{3,1},{4,6},{5,7},{6,4},{7,5},{8,10},{9,11},{10,... | collective-permute-start | bytes 393224 | tf_op jit(solution)/shard_map/ppermute | solution.py:460
  10.5 16.9 %collective-permute-start.1 = (f32[4,64,128]{2,1,0:T(8,128)S(1)}, f32[4,64,128]{2,1,0:T(8,128)S(1)}, u32[]{:S(2)}, u32[]{:S(2)}) collective-permute-start(f32[4,64,128]{2,1,0:T(8,128)S(1)} %get-tuple-element.70._.refs_0_), channel_id=1, source_target_pairs={{0,1},{1,0},{2,3},{3,2},{4,5},{5,4},{6,7},{7,6},{8,9},{9,8},{10,11... | collective-permute-start | bytes 393224 | tf_op jit(solution)/shard_map/ppermute | solution.py:460
  10.5 16.3 %collective-permute-start.3 = (f32[4,64,128]{2,1,0:T(8,128)}, f32[4,64,128]{2,1,0:T(8,128)S(1)}, u32[]{:S(2)}, u32[]{:S(2)}) collective-permute-start(f32[4,64,128]{2,1,0:T(8,128)} %get-tuple-element.71), channel_id=1, source_target_pairs={{0,4},{4,0},{8,12},{12,8},{1,5},{5,1},{9,13},{13,9},{2,6},{6,2},{1... | collective-permute-start | bytes 393224 | tf_op jit(solution)/shard_map/ppermute | solution.py:460
  12.1 15.8 %collective-permute-start.7 = (f32[4,64,128]{2,1,0:T(8,128)}, f32[4,64,128]{2,1,0:T(8,128)S(1)}, u32[]{:S(2)}, u32[]{:S(2)}) collective-permute-start(f32[4,64,128]{2,1,0:T(8,128)} %get-tuple-element.72), channel_id=1, source_target_pairs={{0,8},{4,12},{8,0},{12,4},{1,9},{5,13},{9,1},{13,5},{2,10},{6,14},... | collective-permute-start | bytes 393224 | tf_op jit(solution)/shard_map/ppermute | solution.py:460
  47.8 14.3 %collective-permute-start.22 = (f32[8,64,128]{2,1,0:T(8,128)S(1)}, f32[8,64,128]{2,1,0:T(8,128)S(1)}, u32[]{:S(2)}, u32[]{:S(2)}) collective-permute-start(f32[8,64,128]{2,1,0:T(8,128)S(1)} %get-tuple-element.83), channel_id=1, source_target_pairs={{0,4},{4,0},{8,12},{12,8},{1,5},{5,1},{9,13},{13,9},{2,6},{6,2},{1... | collective-permute-start | bytes 786440 | tf_op jit(solution)/shard_map/ppermute | solution.py:460
  50.6 21.4 %collective-permute-start.23 = (f32[8,64,128]{2,1,0:T(8,128)S(1)}, f32[8,64,128]{2,1,0:T(8,128)S(1)}, u32[]{:S(2)}, u32[]{:S(2)}) collective-permute-start(f32[8,64,128]{2,1,0:T(8,128)S(1)} %get-tuple-element.84), channel_id=1, source_target_pairs={{0,8},{4,12},{8,0},{12,4},{1,9},{5,13},{9,1},{13,5},{2,10},{6,14},... | collective-permute-start | bytes 786440 | tf_op jit(solution)/shard_map/ppermute | solution.py:460
  51.9 20.1 %collective-permute-start.24 = (f32[8,64,128]{2,1,0:T(8,128)S(1)}, f32[8,64,128]{2,1,0:T(8,128)S(1)}, u32[]{:S(2)}, u32[]{:S(2)}) collective-permute-start(f32[8,64,128]{2,1,0:T(8,128)S(1)} %get-tuple-element.85), channel_id=1, source_target_pairs={{0,12},{4,8},{8,4},{12,0},{1,13},{5,9},{9,5},{13,1},{2,14},{6,10},... | collective-permute-start | bytes 786440 | tf_op jit(solution)/shard_map/ppermute | solution.py:460
  53.1 43.6 %collective-permute-start.16 = (f32[8,64,128]{2,1,0:T(8,128)S(1)}, f32[8,64,128]{2,1,0:T(8,128)S(1)}, u32[]{:S(2)}, u32[]{:S(2)}) collective-permute-start(f32[8,64,128]{2,1,0:T(8,128)S(1)} %get-tuple-element.75), channel_id=1, source_target_pairs={{0,4},{4,0},{8,12},{12,8},{1,5},{5,1},{9,13},{13,9},{2,6},{6,2},{1... | collective-permute-start | bytes 786440 | tf_op jit(solution)/shard_map/ppermute | solution.py:460
  54.1 45.0 %collective-permute-start.17 = (f32[8,64,128]{2,1,0:T(8,128)S(1)}, f32[8,64,128]{2,1,0:T(8,128)S(1)}, u32[]{:S(2)}, u32[]{:S(2)}) collective-permute-start(f32[8,64,128]{2,1,0:T(8,128)S(1)} %get-tuple-element.76), channel_id=1, source_target_pairs={{0,8},{4,12},{8,0},{12,4},{1,9},{5,13},{9,1},{13,5},{2,10},{6,14},... | collective-permute-start | bytes 786440 | tf_op jit(solution)/shard_map/ppermute | solution.py:460
  62.0 37.1 %collective-permute-start.18 = (f32[8,64,128]{2,1,0:T(8,128)S(1)}, f32[8,64,128]{2,1,0:T(8,128)S(1)}, u32[]{:S(2)}, u32[]{:S(2)}) collective-permute-start(f32[8,64,128]{2,1,0:T(8,128)S(1)} %get-tuple-element.77), channel_id=1, source_target_pairs={{0,12},{4,8},{8,4},{12,0},{1,13},{5,9},{9,5},{13,1},{2,14},{6,10},... | collective-permute-start | bytes 786440 | tf_op jit(solution)/shard_map/ppermute | solution.py:460
  79.2 38.0 %collective-permute-start.25 = (f32[8,64,128]{2,1,0:T(8,128)S(1)}, f32[8,64,128]{2,1,0:T(8,128)S(1)}, u32[]{:S(2)}, u32[]{:S(2)}) collective-permute-start(f32[8,64,128]{2,1,0:T(8,128)S(1)} %get-tuple-element.87), channel_id=1, source_target_pairs={{0,4},{4,0},{8,12},{12,8},{1,5},{5,1},{9,13},{13,9},{2,6},{6,2},{1... | collective-permute-start | bytes 786440 | tf_op jit(solution)/shard_map/ppermute | solution.py:460
  96.6 23.2 %collective-permute-start.26 = (f32[8,64,128]{2,1,0:T(8,128)S(1)}, f32[8,64,128]{2,1,0:T(8,128)S(1)}, u32[]{:S(2)}, u32[]{:S(2)}) collective-permute-start(f32[8,64,128]{2,1,0:T(8,128)S(1)} %get-tuple-element.88), channel_id=1, source_target_pairs={{0,8},{4,12},{8,0},{12,4},{1,9},{5,13},{9,1},{13,5},{2,10},{6,14},... | collective-permute-start | bytes 786440 | tf_op jit(solution)/shard_map/ppermute | solution.py:460
  96.6 23.2 %collective-permute-start.27 = (f32[8,64,128]{2,1,0:T(8,128)S(1)}, f32[8,64,128]{2,1,0:T(8,128)S(1)}, u32[]{:S(2)}, u32[]{:S(2)}) collective-permute-start(f32[8,64,128]{2,1,0:T(8,128)S(1)} %get-tuple-element.89), channel_id=1, source_target_pairs={{0,12},{4,8},{8,4},{12,0},{1,13},{5,9},{9,5},{13,1},{2,14},{6,10},... | collective-permute-start | bytes 786440 | tf_op jit(solution)/shard_map/ppermute | solution.py:460
  106.2 17.4 %collective-permute-start.19 = (f32[8,32,128]{2,1,0:T(8,128)S(1)}, f32[8,32,128]{2,1,0:T(8,128)S(1)}, u32[]{:S(2)}, u32[]{:S(2)}) collective-permute-start(f32[8,32,128]{2,1,0:T(8,128)S(1)} %get-tuple-element.79), channel_id=1, source_target_pairs={{0,4},{4,0},{8,12},{12,8},{1,5},{5,1},{9,13},{13,9},{2,6},{6,2},{1... | collective-permute-start | bytes 393224 | tf_op jit(solution)/shard_map/ppermute | solution.py:460
  117.2 13.9 %collective-permute-start.20 = (f32[8,32,128]{2,1,0:T(8,128)S(1)}, f32[8,32,128]{2,1,0:T(8,128)S(1)}, u32[]{:S(2)}, u32[]{:S(2)}) collective-permute-start(f32[8,32,128]{2,1,0:T(8,128)S(1)} %get-tuple-element.80), channel_id=1, source_target_pairs={{0,8},{4,12},{8,0},{12,4},{1,9},{5,13},{9,1},{13,5},{2,10},{6,14},... | collective-permute-start | bytes 393224 | tf_op jit(solution)/shard_map/ppermute | solution.py:460
  117.2 13.9 %collective-permute-start.21 = (f32[8,32,128]{2,1,0:T(8,128)S(1)}, f32[8,32,128]{2,1,0:T(8,128)S(1)}, u32[]{:S(2)}, u32[]{:S(2)}) collective-permute-start(f32[8,32,128]{2,1,0:T(8,128)S(1)} %get-tuple-element.81), channel_id=1, source_target_pairs={{0,12},{4,8},{8,4},{12,0},{1,13},{5,9},{9,5},{13,1},{2,14},{6,10},... | collective-permute-start | bytes 393224 | tf_op jit(solution)/shard_map/ppermute | solution.py:460
  134.4 19.4 %collective-permute-start.29 = (f32[16,32,128]{2,1,0:T(8,128)S(1)}, f32[16,32,128]{2,1,0:T(8,128)S(1)}, u32[]{:S(2)}, u32[]{:S(2)}) collective-permute-start(f32[16,32,128]{2,1,0:T(8,128)S(1)} %get-tuple-element.93), channel_id=1, source_target_pairs={{0,1},{1,0},{2,3},{3,2},{4,5},{5,4},{6,7},{7,6},{8,9},{9,8},{10,11... | collective-permute-start | bytes 786440 | tf_op jit(solution)/shard_map/ppermute | solution.py:460
  136.9 12.9 %collective-permute-start.35 = (f32[8,32,128]{2,1,0:T(8,128)S(1)}, f32[8,32,128]{2,1,0:T(8,128)S(1)}, u32[]{:S(2)}, u32[]{:S(2)}) collective-permute-start(f32[8,32,128]{2,1,0:T(8,128)S(1)} %get-tuple-element.96), channel_id=1, source_target_pairs={{0,8},{4,12},{8,0},{12,4},{1,9},{5,13},{9,1},{13,5},{2,10},{6,14},... | collective-permute-start | bytes 393224 | tf_op jit(solution)/shard_map/ppermute | solution.py:460
  154.8 13.4 %collective-permute-start.39 = (f32[16,32,128]{2,1,0:T(8,128)S(1)}, f32[16,32,128]{2,1,0:T(8,128)S(1)}, u32[]{:S(2)}, u32[]{:S(2)}) collective-permute-start(f32[16,32,128]{2,1,0:T(8,128)S(1)} %add.96), channel_id=1, source_target_pairs={{0,2},{1,3},{2,0},{3,1},{4,6},{5,7},{6,4},{7,5},{8,10},{9,11},{10,... | collective-permute-start | bytes 786440 | tf_op jit(solution)/shard_map/ppermute | solution.py:460
  184.8 13.4 %collective-permute-start.54 = (f32[4,64,128]{2,1,0:T(8,128)S(1)}, f32[4,64,128]{2,1,0:T(8,128)S(1)}, u32[]{:S(2)}, u32[]{:S(2)}) collective-permute-start(f32[4,64,128]{2,1,0:T(8,128)S(1)} %get-tuple-element.106), channel_id=1, source_target_pairs={{0,12},{4,8},{8,4},{12,0},{1,13},{5,9},{9,5},{13,1},{2,14},{6,10},... | collective-permute-start | bytes 393224 | tf_op jit(solution)/shard_map/ppermute | solution.py:460
  212.3 14.2 %collective-permute-start.64 = (f32[8,64,128]{2,1,0:T(8,128)S(1)}, f32[8,64,128]{2,1,0:T(8,128)S(1)}, u32[]{:S(2)}, u32[]{:S(2)}) collective-permute-start(f32[8,64,128]{2,1,0:T(8,128)S(1)} %get-tuple-element.116), channel_id=1, source_target_pairs={{0,4},{4,0},{8,12},{12,8},{1,5},{5,1},{9,13},{13,9},{2,6},{6,2},{1... | collective-permute-start | bytes 786440 | tf_op jit(solution)/shard_map/ppermute | solution.py:460
  213.0 21.4 %collective-permute-start.65 = (f32[8,64,128]{2,1,0:T(8,128)S(1)}, f32[8,64,128]{2,1,0:T(8,128)S(1)}, u32[]{:S(2)}, u32[]{:S(2)}) collective-permute-start(f32[8,64,128]{2,1,0:T(8,128)S(1)} %get-tuple-element.117), channel_id=1, source_target_pairs={{0,8},{4,12},{8,0},{12,4},{1,9},{5,13},{9,1},{13,5},{2,10},{6,14},... | collective-permute-start | bytes 786440 | tf_op jit(solution)/shard_map/ppermute | solution.py:460
  214.4 19.9 %collective-permute-start.66 = (f32[8,64,128]{2,1,0:T(8,128)S(1)}, f32[8,64,128]{2,1,0:T(8,128)S(1)}, u32[]{:S(2)}, u32[]{:S(2)}) collective-permute-start(f32[8,64,128]{2,1,0:T(8,128)S(1)} %get-tuple-element.118), channel_id=1, source_target_pairs={{0,12},{4,8},{8,4},{12,0},{1,13},{5,9},{9,5},{13,1},{2,14},{6,10},... | collective-permute-start | bytes 786440 | tf_op jit(solution)/shard_map/ppermute | solution.py:460
  216.8 42.2 %collective-permute-start.58 = (f32[8,64,128]{2,1,0:T(8,128)S(1)}, f32[8,64,128]{2,1,0:T(8,128)S(1)}, u32[]{:S(2)}, u32[]{:S(2)}) collective-permute-start(f32[8,64,128]{2,1,0:T(8,128)S(1)} %get-tuple-element.108), channel_id=1, source_target_pairs={{0,4},{4,0},{8,12},{12,8},{1,5},{5,1},{9,13},{13,9},{2,6},{6,2},{1... | collective-permute-start | bytes 786440 | tf_op jit(solution)/shard_map/ppermute | solution.py:460
  216.8 45.6 %collective-permute-start.59 = (f32[8,64,128]{2,1,0:T(8,128)S(1)}, f32[8,64,128]{2,1,0:T(8,128)S(1)}, u32[]{:S(2)}, u32[]{:S(2)}) collective-permute-start(f32[8,64,128]{2,1,0:T(8,128)S(1)} %get-tuple-element.109), channel_id=1, source_target_pairs={{0,8},{4,12},{8,0},{12,4},{1,9},{5,13},{9,1},{13,5},{2,10},{6,14},... | collective-permute-start | bytes 786440 | tf_op jit(solution)/shard_map/ppermute | solution.py:460
  226.5 35.9 %collective-permute-start.60 = (f32[8,64,128]{2,1,0:T(8,128)S(1)}, f32[8,64,128]{2,1,0:T(8,128)S(1)}, u32[]{:S(2)}, u32[]{:S(2)}) collective-permute-start(f32[8,64,128]{2,1,0:T(8,128)S(1)} %get-tuple-element.110), channel_id=1, source_target_pairs={{0,12},{4,8},{8,4},{12,0},{1,13},{5,9},{9,5},{13,1},{2,14},{6,10},... | collective-permute-start | bytes 786440 | tf_op jit(solution)/shard_map/ppermute | solution.py:460
  241.4 40.1 %collective-permute-start.67 = (f32[8,64,128]{2,1,0:T(8,128)S(1)}, f32[8,64,128]{2,1,0:T(8,128)S(1)}, u32[]{:S(2)}, u32[]{:S(2)}) collective-permute-start(f32[8,64,128]{2,1,0:T(8,128)S(1)} %get-tuple-element.120), channel_id=1, source_target_pairs={{0,4},{4,0},{8,12},{12,8},{1,5},{5,1},{9,13},{13,9},{2,6},{6,2},{1... | collective-permute-start | bytes 786440 | tf_op jit(solution)/shard_map/ppermute | solution.py:460
  258.9 24.9 %collective-permute-start.68 = (f32[8,64,128]{2,1,0:T(8,128)S(1)}, f32[8,64,128]{2,1,0:T(8,128)S(1)}, u32[]{:S(2)}, u32[]{:S(2)}) collective-permute-start(f32[8,64,128]{2,1,0:T(8,128)S(1)} %get-tuple-element.121), channel_id=1, source_target_pairs={{0,8},{4,12},{8,0},{12,4},{1,9},{5,13},{9,1},{13,5},{2,10},{6,14},... | collective-permute-start | bytes 786440 | tf_op jit(solution)/shard_map/ppermute | solution.py:460
  259.0 24.8 %collective-permute-start.69 = (f32[8,64,128]{2,1,0:T(8,128)S(1)}, f32[8,64,128]{2,1,0:T(8,128)S(1)}, u32[]{:S(2)}, u32[]{:S(2)}) collective-permute-start(f32[8,64,128]{2,1,0:T(8,128)S(1)} %get-tuple-element.122), channel_id=1, source_target_pairs={{0,12},{4,8},{8,4},{12,0},{1,13},{5,9},{9,5},{13,1},{2,14},{6,10},... | collective-permute-start | bytes 786440 | tf_op jit(solution)/shard_map/ppermute | solution.py:460
  269.5 18.1 %collective-permute-start.61 = (f32[8,32,128]{2,1,0:T(8,128)S(1)}, f32[8,32,128]{2,1,0:T(8,128)S(1)}, u32[]{:S(2)}, u32[]{:S(2)}) collective-permute-start(f32[8,32,128]{2,1,0:T(8,128)S(1)} %get-tuple-element.112), channel_id=1, source_target_pairs={{0,4},{4,0},{8,12},{12,8},{1,5},{5,1},{9,13},{13,9},{2,6},{6,2},{1... | collective-permute-start | bytes 393224 | tf_op jit(solution)/shard_map/ppermute | solution.py:460
  296.7 19.4 %collective-permute-start.71 = (f32[16,32,128]{2,1,0:T(8,128)S(1)}, f32[16,32,128]{2,1,0:T(8,128)S(1)}, u32[]{:S(2)}, u32[]{:S(2)}) collective-permute-start(f32[16,32,128]{2,1,0:T(8,128)S(1)} %get-tuple-element.126), channel_id=1, source_target_pairs={{0,1},{1,0},{2,3},{3,2},{4,5},{5,4},{6,7},{7,6},{8,9},{9,8},{10,11... | collective-permute-start | bytes 786440 | tf_op jit(solution)/shard_map/ppermute | solution.py:460
  299.1 12.9 %collective-permute-start.77 = (f32[8,32,128]{2,1,0:T(8,128)S(1)}, f32[8,32,128]{2,1,0:T(8,128)S(1)}, u32[]{:S(2)}, u32[]{:S(2)}) collective-permute-start(f32[8,32,128]{2,1,0:T(8,128)S(1)} %get-tuple-element.129), channel_id=1, source_target_pairs={{0,8},{4,12},{8,0},{12,4},{1,9},{5,13},{9,1},{13,5},{2,10},{6,14},... | collective-permute-start | bytes 393224 | tf_op jit(solution)/shard_map/ppermute | solution.py:460
  (75 other events, 727.6 us)

commit v4 on v3

--- a/solution.py
+++ b/solution.py
@@ -256,9 +256,9 @@
 BLOCK_ROWS = 8
 
 
-def depth_step(ids, pieces, places, added, transfer, forward, inverse, outs, keep, adjoint, span, shape):
+def depth_step(ids, pieces, places, added, transfer, forward, inverse, outs, keep, adjoint, span, shape, raw=0):
     main, cross = transfer
-    _, _, depth, lanes = main.shape
+    depth, lanes = cross.shape[1:]
     first_row, rows = shape
     half = lanes // 2
     block = BLOCK_ROWS
@@ -283,6 +283,8 @@
         scratch.append(pltpu.VMEM((in_count * rows, lanes), jnp.float32))
     if outs:
         scratch.append(pltpu.VMEM((out_count * rows, lanes), jnp.float32))
+    if raw:
+        scratch.append(pltpu.VMEM((2 * depth * block, lanes), jnp.float32))
 
     def body(ids_ref, *refs):
         refs = list(refs)
@@ -295,6 +297,7 @@
         keep_ref = refs.pop(0) if keep else None
         gathered = refs.pop(0) if pieces else None
         grown_out = refs.pop(0) if outs else None
+        raw_rows = refs.pop(0) if raw else None
 
         def planes_of(place, span):
             _, count, k, extra, flip, share = place
@@ -314,11 +317,21 @@
                 count = place[1]
                 at = planes_of(place, span[0])
                 for turn in range(rows // block):
+                    row = turn * block + (first_row if ref.shape[1] > rows else 0)
                     gathered[at(turn, in_count), :] = ref[
-                        place[0] : place[0] + count, turn * block : (turn + 1) * block
+                        place[0] : place[0] + count, row : row + block
                     ].reshape(count * block, lanes)
 
+        def main_of(part, turn, line):
+            if not raw:
+                return main_ref[part, first_row + turn * block + line]
+            value = raw_rows[pl.ds(part * depth * block + line, depth, stride=block), :]
+            return pack_transfer(value, part, ids_ref[0] >= raw // 2)
+
         def some(turn, carry):
+            if raw:
+                row = pl.multiple_of(first_row + turn * block, block)
+                raw_rows[...] = main_ref[:, :, pl.ds(row, block), :].reshape(2 * depth * block, lanes)
             for pair in range(block // 2):
                 one_pair(turn, (2 * pair, 2 * pair + 1))
             return carry
@@ -341,8 +354,8 @@
                     sin_roll = pltpu.roll(sin_part, half, 1)
                     spectrum = cos_part + sign(depth) * sin_roll
                     result = (
-                        spectrum * main_ref[0, first_row + k]
-                        + pltpu.roll(spectrum, half, 1) * (main_ref[1, first_row + k] * side)
+                        spectrum * main_of(0, turn, lines[index])
+                        + pltpu.roll(spectrum, half, 1) * (main_of(1, turn, lines[index]) * side)
                     )
                     if lines[index] == 0 and first_row == 0:
                         change = sign(depth) * cos_part - sin_roll - spectrum
@@ -417,24 +430,26 @@
     )
 
 
+def pack_transfer(value, part, upper):
+    lanes = value.shape[1]
+    half = lanes // 2
+    lane = lax.broadcasted_iota(jnp.int32, value.shape, 1)
+    rolled = pltpu.roll(value, half, 1)
+    low = lane < half
+    first_lanes = jnp.where(upper, lane, 1) % half == 0
+    packed = jnp.where(low ^ first_lanes, value, rolled)
+    return packed if part == 0 else jnp.where(low, -packed, packed)
+
+
 def transfer_table(psf, after, ids, space_count):
     _, depth, rows, lanes = psf.shape
-    half = lanes // 2
     block = BLOCK_ROWS
 
     def body(ids_ref, psf_ref, _, main_ref):
-        lane = lax.broadcasted_iota(jnp.int32, (depth, lanes), 1)
-        first_lanes = (lane % half == 0) & (ids_ref[0] >= space_count // 2)
+        upper = ids_ref[0] >= space_count // 2
         for k in range(block):
             for part in range(2):
-                value = rows_of(psf_ref.at[part], k)[...]
-                rolled = pltpu.roll(value, half, 1)
-                doubled = jnp.where(lane < half, value, rolled)
-                other = jnp.where(lane < half, rolled, value)
-                packed = jnp.where(first_lanes, other, doubled)
-                if part == 1:
-                    packed = jnp.where(lane < half, -packed, packed)
-                main_ref[part, k] = packed
+                main_ref[part, k] = pack_transfer(rows_of(psf_ref.at[part], k)[...], part, upper)
 
     return pl.pallas_call(
         body,
@@ -460,6 +475,19 @@
     return lax.ppermute(array, axis, [(i, i ^ flip) for i in range(count)])
 
 
+def add_moved(parts, moved, size, share):
+    sums, first = [], 0
+    for part in parts:
+        count = part.shape[0] // size
+        new = moved[first * size : (first + count) * size]
+        first += count
+        if share:
+            sums += [part[i : i + share] + new[i : i + share] for i in range(0, size, share)]
+        else:
+            sums.append(part + new)
+    return sums
+
+
 def join_planes(ids, copies, flips, planes):
     share, rows, lanes = copies[0].shape
     count = len(copies)
@@ -517,6 +545,7 @@
     starts = list(range(0, planes, chunk))
     part = part_rows // 2 if part_rows % (2 * BLOCK_ROWS) == 0 else part_rows
     whole_rows = [(0, part_rows)]
+    sum_groups = [flips[:1]] + [flips[1 << bit : 2 << bit] for bit in range(len(strides))]
     half_rows = [(first, part) for first in range(0, part_rows, part)]
 
     def row_places(ranges):
@@ -533,8 +562,7 @@
     cross = cross_tables(psf_spectrum[0, :, :, 0, :], space_count)
     own = lax.dynamic_slice_in_dim(estimate, ids[1] * share, share, 0) if shared else estimate
     spectrum = lateral_forward(own, ids, tables, part_rows, row_places(whole_rows))
-    main = transfer_table(psf_spectrum[0], spectrum[0], ids, space_count)
-    transfer = (main, cross)
+    transfer = (psf_spectrum[0], cross)
 
     def spread(pieces):
         moved = {k: send(pieces[k], "space", space_count, k) for k in reversed(ks)}
@@ -543,24 +571,30 @@
     for iteration in range(ITERS):
         last = iteration == ITERS - 1
         pieces, places = [], []
-        for k, piece in enumerate(spread(spectrum)):
+        arrived = spread(spectrum)
+        for k, piece in enumerate(arrived):
             copies = [piece]
             for stride in reversed(strides):
                 copies = copies + [send(c, "view", views, stride) for c in copies]
             pieces += copies
             places += [[(0, share, k, 0, flip, view_share)] for flip in flips]
-        outs, _ = depth_step(
-            ids, pieces, places, None, transfer, full_tables[0], full_tables[1],
-            [[(0, chunk, k, start, 0, 0)] for start in starts for k in ks],
-            False, False, (planes, planes), (0, part_rows),
-        )
+        blurred = [[] for _ in starts]
+        for shape in half_rows:
+            outs, _ = depth_step(
+                ids, pieces, places, None, transfer, full_tables[0], full_tables[1],
+                [[(0, chunk, k, start, 0, 0)] for start in starts for k in ks],
+                False, False, (planes, planes), shape, 0 if iteration else space_count,
+            )
+            for number in range(len(starts)):
+                blurred[number] += spread(outs[number * space_count : (number + 1) * space_count])
+        if iteration == 0:
+            transfer = (transfer_table(psf_spectrum[0], outs[0], ids, space_count), cross)
         ratios = []
         for number, start in enumerate(starts):
             final = number == len(starts) - 1
             ratios.append(
                 ratio_step(
-                    spread(outs[number * space_count : (number + 1) * space_count]), row_places(whole_rows),
-                    observed, valid, start, ids, tables, part_rows,
+                    blurred[number], row_places(half_rows), observed, valid, start, ids, tables, part_rows,
                     row_places(half_rows if final else whole_rows),
                 )
             )
@@ -579,16 +613,19 @@
             parts, _ = depth_step(
                 ids, arrived[number], chunk_places, kept, transfer,
                 chunk_tables[-1][0], full_tables[1],
-                [[(k * share, share, k, 0, flip, view_share) for k in ks] for flip in flips],
+                [
+                    [
+                        (k * share + index * share * space_count, share, k, 0, flip, view_share)
+                        for index, flip in enumerate(group)
+                        for k in ks
+                    ]
+                    for group in sum_groups
+                ],
                 False, True, (chunk, planes), shape,
             )
-            for stride in strides:
-                middle = len(parts) // 2
-                moved = [send(p, "view", views, stride) for p in parts[middle:]]
-                if middle == 1:
-                    parts = [parts[0][k * share : (k + 1) * share] + moved[0][k * share : (k + 1) * share] for k in ks]
-                else:
-                    parts = [own_part + new for own_part, new in zip(parts[:middle], moved)]
+            for stride, group in zip(strides, reversed(sum_groups)):
+                moved = send(parts[-1], "view", views, stride)
+                parts = add_moved(parts[:-1], moved, space_count * share, share if len(parts) == 2 else 0)
             if not strides:
                 total = parts[0] if shared else lax.psum(parts[0], "view")
                 parts = [total[k * share : (k + 1) * share] for k in ks]

time: 359 us -> 359 us (level)
  waiting for transfers between devices: 119 us -> 130 us
  starting transfers between devices: 147 us -> 140 us
  local copies, waits for them, and re-layouts: 12.3 us -> 8.05 us
    ppermute x87 -> x95, starting transfers between devices: 145 us -> 138 us  [send(): return lax.ppermute(array, axis, [(i, i ^ flip) for i in range(count)])]
    ppermute x87 -> x95, waiting for transfers between devices: 119 us -> 125 us  [send(): return lax.ppermute(array, axis, [(i, i ^ flip) for i in range(count)])]
    ppermute x1, waiting for transfers between devices: 0.01 us -> 4.63 us  [cross_tables(): lax.ppermute(first, 'space', [(0, space_count // 2), (space_count // 2, 0)])]
    unnamed x38 -> x34, local copies, waits for them, and re-layouts: 11 us -> 6.83 us
    pallas_call x8 -> x10, Pallas kernels: 34 us -> 35.6 us  [depth_step(): pl.pallas_call(body, out_shape=out_shape, in_specs=[SMEM] + [VMEM] * len(...]
  transfers between devices with their start and end apart: 88 -> 96, of which waited for: 30 -> 31; matrix products, arithmetic and copies ran while one was open for 1% -> 1% of each run, Pallas kernels for 13% -> 15%
where the time goes in v4:
time: 359 us
  starting transfers between devices  140 us (39%)
  waiting for transfers between devices  130 us (36%)
  Pallas kernels  77.5 us (22%)
  local copies, waits for them, and re-layouts  8.05 us (2%)
    ppermute x95, starting transfers between devices, send(): return lax.ppermute(array, axis, [(i, i ^ flip) for i in range(count)])  138 us
    ppermute x95, waiting for transfers between devices, send(): return lax.ppermute(array, axis, [(i, i ^ flip) for i in range(count)])  125 us
    pallas_call x7, Pallas kernels, lateral_call(): pl.pallas_call(kernel, in_specs=[SMEM] + [VMEM] * (len(operands) + len(pi...  37 us
    pallas_call x10, Pallas kernels, depth_step(): pl.pallas_call(body, out_shape=out_shape, in_specs=[SMEM] + [VMEM] * len(...  35.6 us
  transfers between devices with their start and end apart: 96, of which 31 were waited for; matrix products, arithmetic and copies ran while one was open for 1% of the time, Pallas kernels for 15%

profile of v4, /device:TPU:0, one launch (start us, length us, event | category | flops | bytes accessed | tf_op | source)
XLA Modules:
  0.0 358.9 jit_solution(9085828927391690022)
XLA Ops:
  18.5 4.6 %collective-permute-done.15 = f32[2,64,128]{2,1,0:T(8,128)} collective-permute-done((f32[2,64,128]{2,1,0:T(8,128)S(1)}, f32[2,64,128]{2,1,0:T(8,128)}, u32[]{:S(2)}, u32[]{:S(2)}) %collective-permute-start.15) | collective-permute-done | bytes 65568 | tf_op jit(solution)/shard_map/ppermute | solution.py:421
  38.6 3.9 %depth_step.10 = (f32[8,32,128]{2,1,0:T(8,128)S(1)}, f32[8,32,128]{2,1,0:T(8,128)S(1)}, f32[8,32,128]{2,1,0:T(8,128)S(1)}, f32[8,32,128]{2,1,0:T(8,128)S(1)}, f3...) custom-call(s32[2]{0:T(128)S(1)} %pad_add_fusion.ids_ref, ...), custom_call_target="tpu_custom_call" | custom-call | tf_op jit(solution)/shard_map/depth_step/pallas_call | solution.py:397
  47.0 3.6 %depth_step.11 = (f32[8,32,128]{2,1,0:T(8,128)S(1)}, f32[8,32,128]{2,1,0:T(8,128)S(1)}, f32[8,32,128]{2,1,0:T(8,128)S(1)}, f32[8,32,128]{2,1,0:T(8,128)S(1)}, f3...) custom-call(s32[2]{0:T(128)S(1)} %pad_add_fusion.ids_ref, ...), custom_call_target="tpu_custom_call" | custom-call | tf_op jit(solution)/shard_map/depth_step/pallas_call | solution.py:397
  50.9 3.8 %collective-permute-start.29 = (f32[8,32,128]{2,1,0:T(8,128)S(1)}, f32[8,32,128]{2,1,0:T(8,128)S(1)}, u32[]{:S(2)}, u32[]{:S(2)}) collective-permute-start(f32[8,32,128]{2,1,0:T(8,128)S(1)} %get-tuple-element.104), channel_id=1, source_target_pairs={{0,8},{4,12},{8,0},{12,4},{1,9},{5,13},{9,1},{13,5},{2,10},{6,14},... | collective-permute-start | bytes 393224 | tf_op jit(solution)/shard_map/ppermute | solution.py:475
  56.6 9.9 %collective-permute-start.17 = (f32[8,32,128]{2,1,0:T(8,128)S(1)}, f32[8,32,128]{2,1,0:T(8,128)S(1)}, u32[]{:S(2)}, u32[]{:S(2)}) collective-permute-start(f32[8,32,128]{2,1,0:T(8,128)S(1)} %get-tuple-element.88), channel_id=1, source_target_pairs={{0,8},{4,12},{8,0},{12,4},{1,9},{5,13},{9,1},{13,5},{2,10},{6,14},... | collective-permute-start | bytes 393224 | tf_op jit(solution)/shard_map/ppermute | solution.py:475
  68.0 3.8 %collective-permute-done.29.refs_8_ = f32[8,32,128]{2,1,0:T(8,128)S(1)} collective-permute-done((f32[8,32,128]{2,1,0:T(8,128)S(1)}, f32[8,32,128]{2,1,0:T(8,128)S(1)}, u32[]{:S(2)}, u32[]{:S(2)}) %collective-permute-start.29) | collective-permute-done | bytes 131104 | tf_op jit(solution)/shard_map/ppermute | solution.py:475
  71.9 7.1 %shard_map.138 = (f32[8,64,128]{2,1,0:T(8,128)S(1)}, f32[8,64,128]{2,1,0:T(8,128)S(1)}, f32[8,64,128]{2,1,0:T(8,128)S(1)}, f32[8,64,128]{2,1,0:T(8,128)S(1)}) custom-call(s32[2]{0:T(128)S(1)} %pad_add_fusion.ids_ref, f32[16,256,128]{2,1,0:T(8,128)S(1)} %bitcast.9, s32[16,256,128]{2,1,0:T(8,128)S(1)} %bitcast.13, ...), custom_call_target="tpu_custom_call" | custom-call | tf_op jit(solution)/shard_map/pallas_call | solution.py:199
  79.0 5.1 %collective-permute-start.31 = (f32[8,64,128]{2,1,0:T(8,128)S(1)}, f32[8,64,128]{2,1,0:T(8,128)S(1)}, u32[]{:S(2)}, u32[]{:S(2)}) collective-permute-start(f32[8,64,128]{2,1,0:T(8,128)S(1)} %get-tuple-element.107), channel_id=1, source_target_pairs={{0,4},{4,0},{8,12},{12,8},{1,5},{5,1},{9,13},{13,9},{2,6},{6,2},{1... | collective-permute-start | bytes 786440 | tf_op jit(solution)/shard_map/ppermute | solution.py:475
  90.0 16.2 %collective-permute-done.20.refs_8_ = f32[8,32,128]{2,1,0:T(8,128)S(1)} collective-permute-done((f32[8,32,128]{2,1,0:T(8,128)S(1)}, f32[8,32,128]{2,1,0:T(8,128)S(1)}, u32[]{:S(2)}, u32[]{:S(2)}) %collective-permute-start.20) | collective-permute-done | bytes 131104 | tf_op jit(solution)/shard_map/ppermute | solution.py:475
  106.2 7.1 %shard_map.137 = (f32[8,32,128]{2,1,0:T(8,128)S(1)}, f32[8,32,128]{2,1,0:T(8,128)S(1)}, f32[8,32,128]{2,1,0:T(8,128)S(1)}, f32[8,32,128]{2,1,0:T(8,128)S(1)}, f3...) custom-call(s32[2]{0:T(128)S(1)} %pad_add_fusion.ids_ref, ...), custom_call_target="tpu_custom_call" | custom-call | tf_op jit(solution)/shard_map/pallas_call | solution.py:199
  113.3 8.3 %collective-permute-start.22 = (f32[8,32,128]{2,1,0:T(8,128)S(1)}, f32[8,32,128]{2,1,0:T(8,128)S(1)}, u32[]{:S(2)}, u32[]{:S(2)}) collective-permute-start(f32[8,32,128]{2,1,0:T(8,128)S(1)} %get-tuple-element.95), channel_id=1, source_target_pairs={{0,4},{4,0},{8,12},{12,8},{1,5},{5,1},{9,13},{13,9},{2,6},{6,2},{1... | collective-permute-start | bytes 393224 | tf_op jit(solution)/shard_map/ppermute | solution.py:475
  127.2 3.8 %depth_step.12.refs_7_ = f32[64,64,128]{2,1,0:T(8,128)S(1)} custom-call(s32[2]{0:T(128)S(1)} %pad_add_fusion.ids_ref, f32[8,64,128]{2,1,0:T(8,128)S(1)} %get-tuple-element.106.refs_0_, f32[8,64,128]{2,1,0:T(8,128)S(1)} %collective-permute-done.31.refs_1_, f32[8,64,128]{2,1,0:T(8,128)S(1)} %collective-permute-done.32.refs_2_, ...), custom_call_target="tpu_custom_call" | custom-call | tf_op jit(solution)/shard_map/depth_step/pallas_call | solution.py:397
  138.9 3.5 collective-permute-done.39.refs_1_
  142.4 6.3 %collective-permute-done.40.refs_2_ = f32[8,32,128]{2,1,0:T(8,128)S(1)} collective-permute-done((f32[8,32,128]{2,1,0:T(8,128)S(1)}, f32[8,32,128]{2,1,0:T(8,128)S(1)}, u32[]{:S(2)}, u32[]{:S(2)}) %collective-permute-start.40) | collective-permute-done | bytes 131104 | tf_op jit(solution)/shard_map/ppermute | solution.py:475
  154.7 6.8 %collective-permute-done.35 = f32[16,32,128]{2,1,0:T(8,128)S(1)} collective-permute-done((f32[16,32,128]{2,1,0:T(8,128)S(1)}, f32[16,32,128]{2,1,0:T(8,128)S(1)}, u32[]{:S(2)}, u32[]{:S(2)}) %collective-permute-start.35) | collective-permute-done | bytes 262176 | tf_op jit(solution)/shard_map/ppermute | solution.py:475
  172.6 4.4 %collective-permute-done.45.refs_7_ = f32[4,32,128]{2,1,0:T(8,128)S(1)} collective-permute-done((f32[4,32,128]{2,1,0:T(8,128)S(1)}, f32[4,32,128]{2,1,0:T(8,128)S(1)}, u32[]{:S(2)}, u32[]{:S(2)}) %collective-permute-start.45) | collective-permute-done | bytes 65568 | tf_op jit(solution)/shard_map/ppermute | solution.py:475
  177.0 3.8 %shard_map.139 = (f32[4,256,128]{2,1,0:T(8,128)S(1)}, f32[4,64,128]{2,1,0:T(8,128)S(1)}, f32[4,64,128]{2,1,0:T(8,128)S(1)}, f32[4,64,128]{2,1,0:T(8,128)S(1)}, f32[4,64,128]{2,1,0:T(8,128)S(1)}) custom-call(s32[2]{0:T(128)S(1)} %pad_add_fusion.ids_ref, f32[4,256,128]{2,1,0:T(8,128)S(1)} %constant_dynamic-slice_fusion.refs_0_, ...), custom_call_target="tpu_custom_call" | custom-call | tf_op jit(solution)/shard_map/pallas_call | solution.py:199
  187.9 7.5 %collective-permute-done.54.refs_8_ = f32[4,64,128]{2,1,0:T(8,128)S(1)} collective-permute-done((f32[4,64,128]{2,1,0:T(8,128)S(1)}, f32[4,64,128]{2,1,0:T(8,128)S(1)}, u32[]{:S(2)}, u32[]{:S(2)}) %collective-permute-start.54) | collective-permute-done | bytes 131104 | tf_op jit(solution)/shard_map/ppermute | solution.py:475
  198.1 3.6 %collective-permute-done.55.refs_9_ = f32[4,64,128]{2,1,0:T(8,128)S(1)} collective-permute-done((f32[4,64,128]{2,1,0:T(8,128)S(1)}, f32[4,64,128]{2,1,0:T(8,128)S(1)}, u32[]{:S(2)}, u32[]{:S(2)}) %collective-permute-start.55) | collective-permute-done | bytes 131104 | tf_op jit(solution)/shard_map/ppermute | solution.py:475
  212.4 3.7 %depth_step.16 = (f32[8,32,128]{2,1,0:T(8,128)S(1)}, f32[8,32,128]{2,1,0:T(8,128)S(1)}, f32[8,32,128]{2,1,0:T(8,128)S(1)}, f32[8,32,128]{2,1,0:T(8,128)S(1)}, f3...) custom-call(s32[2]{0:T(128)S(1)} %pad_add_fusion.ids_ref, ...), custom_call_target="tpu_custom_call" | custom-call | tf_op jit(solution)/shard_map/depth_step/pallas_call | solution.py:397
  221.5 9.4 %collective-permute-start.63 = (f32[8,32,128]{2,1,0:T(8,128)S(1)}, f32[8,32,128]{2,1,0:T(8,128)S(1)}, u32[]{:S(2)}, u32[]{:S(2)}) collective-permute-start(f32[8,32,128]{2,1,0:T(8,128)S(1)} %get-tuple-element.127), channel_id=1, source_target_pairs={{0,8},{4,12},{8,0},{12,4},{1,9},{5,13},{9,1},{13,5},{2,10},{6,14},... | collective-permute-start | bytes 393224 | tf_op jit(solution)/shard_map/ppermute | solution.py:475
  232.9 5.5 %collective-permute-done.75.refs_8_ = f32[8,32,128]{2,1,0:T(8,128)S(1)} collective-permute-done((f32[8,32,128]{2,1,0:T(8,128)S(1)}, f32[8,32,128]{2,1,0:T(8,128)S(1)}, u32[]{:S(2)}, u32[]{:S(2)}) %collective-permute-start.75) | collective-permute-done | bytes 131104 | tf_op jit(solution)/shard_map/ppermute | solution.py:475
  238.4 7.1 %shard_map.141 = (f32[8,64,128]{2,1,0:T(8,128)S(1)}, f32[8,64,128]{2,1,0:T(8,128)S(1)}, f32[8,64,128]{2,1,0:T(8,128)S(1)}, f32[8,64,128]{2,1,0:T(8,128)S(1)}) custom-call(s32[2]{0:T(128)S(1)} %pad_add_fusion.ids_ref, f32[16,256,128]{2,1,0:T(8,128)S(1)} %bitcast.11, s32[16,256,128]{2,1,0:T(8,128)S(1)} %bitcast.15, ...), custom_call_target="tpu_custom_call" | custom-call | tf_op jit(solution)/shard_map/pallas_call | solution.py:199
  254.8 15.3 %collective-permute-done.66.refs_8_ = f32[8,32,128]{2,1,0:T(8,128)S(1)} collective-permute-done((f32[8,32,128]{2,1,0:T(8,128)S(1)}, f32[8,32,128]{2,1,0:T(8,128)S(1)}, u32[]{:S(2)}, u32[]{:S(2)}) %collective-permute-start.66) | collective-permute-done | bytes 131104 | tf_op jit(solution)/shard_map/ppermute | solution.py:475
  270.1 7.1 %shard_map.140 = (f32[8,32,128]{2,1,0:T(8,128)S(1)}, f32[8,32,128]{2,1,0:T(8,128)S(1)}, f32[8,32,128]{2,1,0:T(8,128)S(1)}, f32[8,32,128]{2,1,0:T(8,128)S(1)}, f3...) custom-call(s32[2]{0:T(128)S(1)} %pad_add_fusion.ids_ref, ...), custom_call_target="tpu_custom_call" | custom-call | tf_op jit(solution)/shard_map/pallas_call | solution.py:199
  277.1 8.5 %collective-permute-start.68 = (f32[8,32,128]{2,1,0:T(8,128)S(1)}, f32[8,32,128]{2,1,0:T(8,128)S(1)}, u32[]{:S(2)}, u32[]{:S(2)}) collective-permute-start(f32[8,32,128]{2,1,0:T(8,128)S(1)} %get-tuple-element.134), channel_id=1, source_target_pairs={{0,4},{4,0},{8,12},{12,8},{1,5},{5,1},{9,13},{13,9},{2,6},{6,2},{1... | collective-permute-start | bytes 393224 | tf_op jit(solution)/shard_map/ppermute | solution.py:475
  288.1 3.8 %depth_step.17.refs_7_ = f32[64,64,128]{2,1,0:T(8,128)S(1)} custom-call(s32[2]{0:T(128)S(1)} %pad_add_fusion.ids_ref, f32[8,64,128]{2,1,0:T(8,128)S(1)} %get-tuple-element.145.refs_0_, f32[8,64,128]{2,1,0:T(8,128)S(1)} %collective-permute-done.77.refs_1_, f32[8,64,128]{2,1,0:T(8,128)S(1)} %collective-permute-done.78.refs_2_, ...), custom_call_target="tpu_custom_call" | custom-call | tf_op jit(solution)/shard_map/depth_step/pallas_call | solution.py:397
  302.3 3.5 collective-permute-done.85.refs_1_
  305.8 6.9 %collective-permute-done.86.refs_2_ = f32[8,32,128]{2,1,0:T(8,128)S(1)} collective-permute-done((f32[8,32,128]{2,1,0:T(8,128)S(1)}, f32[8,32,128]{2,1,0:T(8,128)S(1)}, u32[]{:S(2)}, u32[]{:S(2)}) %collective-permute-start.86) | collective-permute-done | bytes 131104 | tf_op jit(solution)/shard_map/ppermute | solution.py:475
  319.7 5.8 %collective-permute-done.81 = f32[16,32,128]{2,1,0:T(8,128)S(1)} collective-permute-done((f32[16,32,128]{2,1,0:T(8,128)S(1)}, f32[16,32,128]{2,1,0:T(8,128)S(1)}, u32[]{:S(2)}, u32[]{:S(2)}) %collective-permute-start.81) | collective-permute-done | bytes 262176 | tf_op jit(solution)/shard_map/ppermute | solution.py:475
  336.6 4.5 %collective-permute-done.91.refs_7_ = f32[4,32,128]{2,1,0:T(8,128)S(1)} collective-permute-done((f32[4,32,128]{2,1,0:T(8,128)S(1)}, f32[4,32,128]{2,1,0:T(8,128)S(1)}, u32[]{:S(2)}, u32[]{:S(2)}) %collective-permute-start.91) | collective-permute-done | bytes 65568 | tf_op jit(solution)/shard_map/ppermute | solution.py:475
  344.8 10.1 %collective-permute-done.93.refs_1_ = f32[4,256,128]{2,1,0:T(8,128)S(1)} collective-permute-done((f32[4,256,128]{2,1,0:T(8,128)S(1)}, f32[4,256,128]{2,1,0:T(8,128)S(1)}, u32[]{:S(2)}, u32[]{:S(2)}) %collective-permute-start.93) | collective-permute-done | bytes 524320 | tf_op jit(solution)/shard_map/ppermute | solution.py:475
  (235 shorter events, 153.5 us)
Async XLA Ops:
  7.5 17.1 %collective-permute-start = (f32[4,64,128]{2,1,0:T(8,128)S(1)}, f32[4,64,128]{2,1,0:T(8,128)S(1)}, u32[]{:S(2)}, u32[]{:S(2)}) collective-permute-start(f32[4,64,128]{2,1,0:T(8,128)S(1)} %get-tuple-element.82.refs_0_), channel_id=1, source_target_pairs={{0,2},{1,3},{2,0},{3,1},{4,6},{5,7},{6,4},{7,5},{8,10},{9,11},{10,... | collective-permute-start | bytes 393224 | tf_op jit(solution)/shard_map/ppermute | solution.py:475
  10.5 14.2 %collective-permute-start.1 = (f32[4,64,128]{2,1,0:T(8,128)S(1)}, f32[4,64,128]{2,1,0:T(8,128)S(1)}, u32[]{:S(2)}, u32[]{:S(2)}) collective-permute-start(f32[4,64,128]{2,1,0:T(8,128)S(1)} %get-tuple-element.82.refs_0_), channel_id=1, source_target_pairs={{0,1},{1,0},{2,3},{3,2},{4,5},{5,4},{6,7},{7,6},{8,9},{9,8},{10,11... | collective-permute-start | bytes 393224 | tf_op jit(solution)/shard_map/ppermute | solution.py:475
  10.5 13.5 %collective-permute-start.3 = (f32[4,64,128]{2,1,0:T(8,128)}, f32[4,64,128]{2,1,0:T(8,128)S(1)}, u32[]{:S(2)}, u32[]{:S(2)}) collective-permute-start(f32[4,64,128]{2,1,0:T(8,128)} %get-tuple-element.83), channel_id=1, source_target_pairs={{0,4},{4,0},{8,12},{12,8},{1,5},{5,1},{9,13},{13,9},{2,6},{6,2},{1... | collective-permute-start | bytes 393224 | tf_op jit(solution)/shard_map/ppermute | solution.py:475
  43.1 13.5 %collective-permute-start.26 = (f32[8,32,128]{2,1,0:T(8,128)S(1)}, f32[8,32,128]{2,1,0:T(8,128)S(1)}, u32[]{:S(2)}, u32[]{:S(2)}) collective-permute-start(f32[8,32,128]{2,1,0:T(8,128)S(1)} %get-tuple-element.101), channel_id=1, source_target_pairs={{0,8},{4,12},{8,0},{12,4},{1,9},{5,13},{9,1},{13,5},{2,10},{6,14},... | collective-permute-start | bytes 393224 | tf_op jit(solution)/shard_map/ppermute | solution.py:475
  50.6 15.9 %collective-permute-start.28 = (f32[8,32,128]{2,1,0:T(8,128)S(1)}, f32[8,32,128]{2,1,0:T(8,128)S(1)}, u32[]{:S(2)}, u32[]{:S(2)}) collective-permute-start(f32[8,32,128]{2,1,0:T(8,128)S(1)} %get-tuple-element.103), channel_id=1, source_target_pairs={{0,4},{4,0},{8,12},{12,8},{1,5},{5,1},{9,13},{13,9},{2,6},{6,2},{1... | collective-permute-start | bytes 393224 | tf_op jit(solution)/shard_map/ppermute | solution.py:475
  50.9 20.9 %collective-permute-start.29 = (f32[8,32,128]{2,1,0:T(8,128)S(1)}, f32[8,32,128]{2,1,0:T(8,128)S(1)}, u32[]{:S(2)}, u32[]{:S(2)}) collective-permute-start(f32[8,32,128]{2,1,0:T(8,128)S(1)} %get-tuple-element.104), channel_id=1, source_target_pairs={{0,8},{4,12},{8,0},{12,4},{1,9},{5,13},{9,1},{13,5},{2,10},{6,14},... | collective-permute-start | bytes 393224 | tf_op jit(solution)/shard_map/ppermute | solution.py:475
  54.7 17.1 %collective-permute-start.30 = (f32[8,32,128]{2,1,0:T(8,128)S(1)}, f32[8,32,128]{2,1,0:T(8,128)S(1)}, u32[]{:S(2)}, u32[]{:S(2)}) collective-permute-start(f32[8,32,128]{2,1,0:T(8,128)S(1)} %get-tuple-element.105), channel_id=1, source_target_pairs={{0,12},{4,8},{8,4},{12,0},{1,13},{5,9},{9,5},{13,1},{2,14},{6,10},... | collective-permute-start | bytes 393224 | tf_op jit(solution)/shard_map/ppermute | solution.py:475
  56.6 27.5 %collective-permute-start.16 = (f32[8,32,128]{2,1,0:T(8,128)S(1)}, f32[8,32,128]{2,1,0:T(8,128)S(1)}, u32[]{:S(2)}, u32[]{:S(2)}) collective-permute-start(f32[8,32,128]{2,1,0:T(8,128)S(1)} %get-tuple-element.87), channel_id=1, source_target_pairs={{0,4},{4,0},{8,12},{12,8},{1,5},{5,1},{9,13},{13,9},{2,6},{6,2},{1... | collective-permute-start | bytes 393224 | tf_op jit(solution)/shard_map/ppermute | solution.py:475
  56.6 28.5 %collective-permute-start.17 = (f32[8,32,128]{2,1,0:T(8,128)S(1)}, f32[8,32,128]{2,1,0:T(8,128)S(1)}, u32[]{:S(2)}, u32[]{:S(2)}) collective-permute-start(f32[8,32,128]{2,1,0:T(8,128)S(1)} %get-tuple-element.88), channel_id=1, source_target_pairs={{0,8},{4,12},{8,0},{12,4},{1,9},{5,13},{9,1},{13,5},{2,10},{6,14},... | collective-permute-start | bytes 393224 | tf_op jit(solution)/shard_map/ppermute | solution.py:475
  66.5 20.0 %collective-permute-start.18 = (f32[8,32,128]{2,1,0:T(8,128)S(1)}, f32[8,32,128]{2,1,0:T(8,128)S(1)}, u32[]{:S(2)}, u32[]{:S(2)}) collective-permute-start(f32[8,32,128]{2,1,0:T(8,128)S(1)} %get-tuple-element.89), channel_id=1, source_target_pairs={{0,12},{4,8},{8,4},{12,0},{1,13},{5,9},{9,5},{13,1},{2,14},{6,10},... | collective-permute-start | bytes 393224 | tf_op jit(solution)/shard_map/ppermute | solution.py:475
  71.8 16.7 %collective-permute-start.19 = (f32[8,32,128]{2,1,0:T(8,128)S(1)}, f32[8,32,128]{2,1,0:T(8,128)S(1)}, u32[]{:S(2)}, u32[]{:S(2)}) collective-permute-start(f32[8,32,128]{2,1,0:T(8,128)S(1)} %get-tuple-element.91), channel_id=1, source_target_pairs={{0,4},{4,0},{8,12},{12,8},{1,5},{5,1},{9,13},{13,9},{2,6},{6,2},{1... | collective-permute-start | bytes 393224 | tf_op jit(solution)/shard_map/ppermute | solution.py:475
  79.0 43.2 %collective-permute-start.31 = (f32[8,64,128]{2,1,0:T(8,128)S(1)}, f32[8,64,128]{2,1,0:T(8,128)S(1)}, u32[]{:S(2)}, u32[]{:S(2)}) collective-permute-start(f32[8,64,128]{2,1,0:T(8,128)S(1)} %get-tuple-element.107), channel_id=1, source_target_pairs={{0,4},{4,0},{8,12},{12,8},{1,5},{5,1},{9,13},{13,9},{2,6},{6,2},{1... | collective-permute-start | bytes 786440 | tf_op jit(solution)/shard_map/ppermute | solution.py:475
  84.1 22.1 %collective-permute-start.20 = (f32[8,32,128]{2,1,0:T(8,128)S(1)}, f32[8,32,128]{2,1,0:T(8,128)S(1)}, u32[]{:S(2)}, u32[]{:S(2)}) collective-permute-start(f32[8,32,128]{2,1,0:T(8,128)S(1)} %get-tuple-element.92), channel_id=1, source_target_pairs={{0,8},{4,12},{8,0},{12,4},{1,9},{5,13},{9,1},{13,5},{2,10},{6,14},... | collective-permute-start | bytes 393224 | tf_op jit(solution)/shard_map/ppermute | solution.py:475
  85.1 21.1 %collective-permute-start.21 = (f32[8,32,128]{2,1,0:T(8,128)S(1)}, f32[8,32,128]{2,1,0:T(8,128)S(1)}, u32[]{:S(2)}, u32[]{:S(2)}) collective-permute-start(f32[8,32,128]{2,1,0:T(8,128)S(1)} %get-tuple-element.93), channel_id=1, source_target_pairs={{0,12},{4,8},{8,4},{12,0},{1,13},{5,9},{9,5},{13,1},{2,14},{6,10},... | collective-permute-start | bytes 393224 | tf_op jit(solution)/shard_map/ppermute | solution.py:475
  86.5 40.6 %collective-permute-start.32 = (f32[8,64,128]{2,1,0:T(8,128)S(1)}, f32[8,64,128]{2,1,0:T(8,128)S(1)}, u32[]{:S(2)}, u32[]{:S(2)}) collective-permute-start(f32[8,64,128]{2,1,0:T(8,128)S(1)} %get-tuple-element.108), channel_id=1, source_target_pairs={{0,8},{4,12},{8,0},{12,4},{1,9},{5,13},{9,1},{13,5},{2,10},{6,14},... | collective-permute-start | bytes 786440 | tf_op jit(solution)/shard_map/ppermute | solution.py:475
  88.5 38.7 %collective-permute-start.33 = (f32[8,64,128]{2,1,0:T(8,128)S(1)}, f32[8,64,128]{2,1,0:T(8,128)S(1)}, u32[]{:S(2)}, u32[]{:S(2)}) collective-permute-start(f32[8,64,128]{2,1,0:T(8,128)S(1)} %get-tuple-element.109), channel_id=1, source_target_pairs={{0,12},{4,8},{8,4},{12,0},{1,13},{5,9},{9,5},{13,1},{2,14},{6,10},... | collective-permute-start | bytes 786440 | tf_op jit(solution)/shard_map/ppermute | solution.py:475
  113.3 17.7 %collective-permute-start.22 = (f32[8,32,128]{2,1,0:T(8,128)S(1)}, f32[8,32,128]{2,1,0:T(8,128)S(1)}, u32[]{:S(2)}, u32[]{:S(2)}) collective-permute-start(f32[8,32,128]{2,1,0:T(8,128)S(1)} %get-tuple-element.95), channel_id=1, source_target_pairs={{0,4},{4,0},{8,12},{12,8},{1,5},{5,1},{9,13},{13,9},{2,6},{6,2},{1... | collective-permute-start | bytes 393224 | tf_op jit(solution)/shard_map/ppermute | solution.py:475
  134.4 17.8 %collective-permute-start.34 = (f32[32,32,128]{2,1,0:T(8,128)S(1)}, f32[32,32,128]{2,1,0:T(8,128)S(1)}, u32[]{:S(2)}, u32[]{:S(2)}) collective-permute-start(f32[32,32,128]{2,1,0:T(8,128)S(1)} %get-tuple-element.111), channel_id=1, source_target_pairs={{0,1},{1,0},{2,3},{3,2},{4,5},{5,4},{6,7},{7,6},{8,9},{9,8},{10,11... | collective-permute-start | bytes 1572872 | tf_op jit(solution)/shard_map/ppermute | solution.py:475
  216.1 14.9 %collective-permute-start.74 = (f32[8,32,128]{2,1,0:T(8,128)S(1)}, f32[8,32,128]{2,1,0:T(8,128)S(1)}, u32[]{:S(2)}, u32[]{:S(2)}) collective-permute-start(f32[8,32,128]{2,1,0:T(8,128)S(1)} %get-tuple-element.142), channel_id=1, source_target_pairs={{0,4},{4,0},{8,12},{12,8},{1,5},{5,1},{9,13},{13,9},{2,6},{6,2},{1... | collective-permute-start | bytes 393224 | tf_op jit(solution)/shard_map/ppermute | solution.py:475
  216.1 22.2 %collective-permute-start.75 = (f32[8,32,128]{2,1,0:T(8,128)S(1)}, f32[8,32,128]{2,1,0:T(8,128)S(1)}, u32[]{:S(2)}, u32[]{:S(2)}) collective-permute-start(f32[8,32,128]{2,1,0:T(8,128)S(1)} %get-tuple-element.143), channel_id=1, source_target_pairs={{0,8},{4,12},{8,0},{12,4},{1,9},{5,13},{9,1},{13,5},{2,10},{6,14},... | collective-permute-start | bytes 393224 | tf_op jit(solution)/shard_map/ppermute | solution.py:475
  218.6 19.8 %collective-permute-start.76 = (f32[8,32,128]{2,1,0:T(8,128)S(1)}, f32[8,32,128]{2,1,0:T(8,128)S(1)}, u32[]{:S(2)}, u32[]{:S(2)}) collective-permute-start(f32[8,32,128]{2,1,0:T(8,128)S(1)} %get-tuple-element.144), channel_id=1, source_target_pairs={{0,12},{4,8},{8,4},{12,0},{1,13},{5,9},{9,5},{13,1},{2,14},{6,10},... | collective-permute-start | bytes 393224 | tf_op jit(solution)/shard_map/ppermute | solution.py:475
  221.5 27.4 %collective-permute-start.62 = (f32[8,32,128]{2,1,0:T(8,128)S(1)}, f32[8,32,128]{2,1,0:T(8,128)S(1)}, u32[]{:S(2)}, u32[]{:S(2)}) collective-permute-start(f32[8,32,128]{2,1,0:T(8,128)S(1)} %get-tuple-element.126), channel_id=1, source_target_pairs={{0,4},{4,0},{8,12},{12,8},{1,5},{5,1},{9,13},{13,9},{2,6},{6,2},{1... | collective-permute-start | bytes 393224 | tf_op jit(solution)/shard_map/ppermute | solution.py:475
  221.5 27.9 %collective-permute-start.63 = (f32[8,32,128]{2,1,0:T(8,128)S(1)}, f32[8,32,128]{2,1,0:T(8,128)S(1)}, u32[]{:S(2)}, u32[]{:S(2)}) collective-permute-start(f32[8,32,128]{2,1,0:T(8,128)S(1)} %get-tuple-element.127), channel_id=1, source_target_pairs={{0,8},{4,12},{8,0},{12,4},{1,9},{5,13},{9,1},{13,5},{2,10},{6,14},... | collective-permute-start | bytes 393224 | tf_op jit(solution)/shard_map/ppermute | solution.py:475
  230.9 20.4 %collective-permute-start.64 = (f32[8,32,128]{2,1,0:T(8,128)S(1)}, f32[8,32,128]{2,1,0:T(8,128)S(1)}, u32[]{:S(2)}, u32[]{:S(2)}) collective-permute-start(f32[8,32,128]{2,1,0:T(8,128)S(1)} %get-tuple-element.128), channel_id=1, source_target_pairs={{0,12},{4,8},{8,4},{12,0},{1,13},{5,9},{9,5},{13,1},{2,14},{6,10},... | collective-permute-start | bytes 393224 | tf_op jit(solution)/shard_map/ppermute | solution.py:475
  238.4 14.5 %collective-permute-start.65 = (f32[8,32,128]{2,1,0:T(8,128)S(1)}, f32[8,32,128]{2,1,0:T(8,128)S(1)}, u32[]{:S(2)}, u32[]{:S(2)}) collective-permute-start(f32[8,32,128]{2,1,0:T(8,128)S(1)} %get-tuple-element.130), channel_id=1, source_target_pairs={{0,4},{4,0},{8,12},{12,8},{1,5},{5,1},{9,13},{13,9},{2,6},{6,2},{1... | collective-permute-start | bytes 393224 | tf_op jit(solution)/shard_map/ppermute | solution.py:475
  245.5 40.8 %collective-permute-start.77 = (f32[8,64,128]{2,1,0:T(8,128)S(1)}, f32[8,64,128]{2,1,0:T(8,128)S(1)}, u32[]{:S(2)}, u32[]{:S(2)}) collective-permute-start(f32[8,64,128]{2,1,0:T(8,128)S(1)} %get-tuple-element.146), channel_id=1, source_target_pairs={{0,4},{4,0},{8,12},{12,8},{1,5},{5,1},{9,13},{13,9},{2,6},{6,2},{1... | collective-permute-start | bytes 786440 | tf_op jit(solution)/shard_map/ppermute | solution.py:475
  248.9 21.2 %collective-permute-start.66 = (f32[8,32,128]{2,1,0:T(8,128)S(1)}, f32[8,32,128]{2,1,0:T(8,128)S(1)}, u32[]{:S(2)}, u32[]{:S(2)}) collective-permute-start(f32[8,32,128]{2,1,0:T(8,128)S(1)} %get-tuple-element.131), channel_id=1, source_target_pairs={{0,8},{4,12},{8,0},{12,4},{1,9},{5,13},{9,1},{13,5},{2,10},{6,14},... | collective-permute-start | bytes 393224 | tf_op jit(solution)/shard_map/ppermute | solution.py:475
  249.4 20.7 %collective-permute-start.67 = (f32[8,32,128]{2,1,0:T(8,128)S(1)}, f32[8,32,128]{2,1,0:T(8,128)S(1)}, u32[]{:S(2)}, u32[]{:S(2)}) collective-permute-start(f32[8,32,128]{2,1,0:T(8,128)S(1)} %get-tuple-element.132), channel_id=1, source_target_pairs={{0,12},{4,8},{8,4},{12,0},{1,13},{5,9},{9,5},{13,1},{2,14},{6,10},... | collective-permute-start | bytes 393224 | tf_op jit(solution)/shard_map/ppermute | solution.py:475
  251.3 36.8 %collective-permute-start.78 = (f32[8,64,128]{2,1,0:T(8,128)S(1)}, f32[8,64,128]{2,1,0:T(8,128)S(1)}, u32[]{:S(2)}, u32[]{:S(2)}) collective-permute-start(f32[8,64,128]{2,1,0:T(8,128)S(1)} %get-tuple-element.147), channel_id=1, source_target_pairs={{0,8},{4,12},{8,0},{12,4},{1,9},{5,13},{9,1},{13,5},{2,10},{6,14},... | collective-permute-start | bytes 786440 | tf_op jit(solution)/shard_map/ppermute | solution.py:475
  252.8 35.3 %collective-permute-start.79 = (f32[8,64,128]{2,1,0:T(8,128)S(1)}, f32[8,64,128]{2,1,0:T(8,128)S(1)}, u32[]{:S(2)}, u32[]{:S(2)}) collective-permute-start(f32[8,64,128]{2,1,0:T(8,128)S(1)} %get-tuple-element.148), channel_id=1, source_target_pairs={{0,12},{4,8},{8,4},{12,0},{1,13},{5,9},{9,5},{13,1},{2,14},{6,10},... | collective-permute-start | bytes 786440 | tf_op jit(solution)/shard_map/ppermute | solution.py:475
  277.1 14.8 %collective-permute-start.68 = (f32[8,32,128]{2,1,0:T(8,128)S(1)}, f32[8,32,128]{2,1,0:T(8,128)S(1)}, u32[]{:S(2)}, u32[]{:S(2)}) collective-permute-start(f32[8,32,128]{2,1,0:T(8,128)S(1)} %get-tuple-element.134), channel_id=1, source_target_pairs={{0,4},{4,0},{8,12},{12,8},{1,5},{5,1},{9,13},{13,9},{2,6},{6,2},{1... | collective-permute-start | bytes 393224 | tf_op jit(solution)/shard_map/ppermute | solution.py:475
  297.8 18.5 %collective-permute-start.80 = (f32[32,32,128]{2,1,0:T(8,128)S(1)}, f32[32,32,128]{2,1,0:T(8,128)S(1)}, u32[]{:S(2)}, u32[]{:S(2)}) collective-permute-start(f32[32,32,128]{2,1,0:T(8,128)S(1)} %get-tuple-element.150), channel_id=1, source_target_pairs={{0,1},{1,0},{2,3},{3,2},{4,5},{5,4},{6,7},{7,6},{8,9},{9,8},{10,11... | collective-permute-start | bytes 1572872 | tf_op jit(solution)/shard_map/ppermute | solution.py:475
  (81 other events, 788.1 us)

commit v5 on v4

--- a/solution.py
+++ b/solution.py
@@ -174,7 +174,8 @@
 
         def row_range(place):
             k, first, count = place
-            return pl.ds(pl.multiple_of(flipped(ids_ref, 0, k, part_rows) + first, count), count)
+            start = flipped(ids_ref, 0, k, part_rows) + first
+            return pl.ds(pl.multiple_of(start, BLOCK_ROWS), count)
 
         def turn(number, carry):
             indices = [number * step + i for i in range(step)]
@@ -543,10 +544,15 @@
     ks = list(range(space_count))
     chunk = planes // 2 if planes % 2 == 0 else planes
     starts = list(range(0, planes, chunk))
-    part = part_rows // 2 if part_rows % (2 * BLOCK_ROWS) == 0 else part_rows
     whole_rows = [(0, part_rows)]
     sum_groups = [flips[:1]] + [flips[1 << bit : 2 << bit] for bit in range(len(strides))]
-    half_rows = [(first, part) for first in range(0, part_rows, part)]
+    turns = part_rows // BLOCK_ROWS
+    small = max(3 * turns // 8, 1) * BLOCK_ROWS
+    if turns > 1:
+        blur_rows = [(0, small), (small, part_rows - small)]
+        back_rows = [(0, turns // 2 * BLOCK_ROWS), (turns // 2 * BLOCK_ROWS, (turns + 1) // 2 * BLOCK_ROWS)]
+    else:
+        blur_rows = back_rows = whole_rows
 
     def row_places(ranges):
         return [(k, first, count) for first, count in ranges for k in ks]
@@ -565,8 +571,10 @@
     transfer = (psf_spectrum[0], cross)
 
     def spread(pieces):
-        moved = {k: send(pieces[k], "space", space_count, k) for k in reversed(ks)}
-        return [moved[k] for k in ks]
+        moved = []
+        for k in ks:
+            moved.append(send(pieces[k], "space", space_count, k))
+        return moved
 
     for iteration in range(ITERS):
         last = iteration == ITERS - 1
@@ -579,7 +587,7 @@
             pieces += copies
             places += [[(0, share, k, 0, flip, view_share)] for flip in flips]
         blurred = [[] for _ in starts]
-        for shape in half_rows:
+        for shape in blur_rows:
             outs, _ = depth_step(
                 ids, pieces, places, None, transfer, full_tables[0], full_tables[1],
                 [[(0, chunk, k, start, 0, 0)] for start in starts for k in ks],
@@ -592,12 +600,11 @@
         ratios = []
         for number, start in enumerate(starts):
             final = number == len(starts) - 1
-            ratios.append(
-                ratio_step(
-                    blurred[number], row_places(half_rows), observed, valid, start, ids, tables, part_rows,
-                    row_places(half_rows if final else whole_rows),
-                )
+            ratio = ratio_step(
+                blurred[number], row_places(blur_rows), observed, valid, start, ids, tables, part_rows,
+                row_places(back_rows if final else whole_rows),
             )
+            ratios.append(ratio)
         kept = None
         for number, ratio in enumerate(ratios[:-1]):
             arrived = spread(ratio)
@@ -606,10 +613,10 @@
                 [], True, True, (chunk, planes), (0, part_rows),
             )
         arrived = []
-        for number in range(len(half_rows)):
+        for number in range(len(back_rows)):
             arrived.append(spread(ratios[-1][number * space_count : (number + 1) * space_count]))
         combined = []
-        for number, shape in enumerate(half_rows):
+        for number, shape in enumerate(back_rows):
             parts, _ = depth_step(
                 ids, arrived[number], chunk_places, kept, transfer,
                 chunk_tables[-1][0], full_tables[1],
@@ -631,7 +638,7 @@
                 parts = [total[k * share : (k + 1) * share] for k in ks]
             combined += spread(parts)
         own, spectrum = update_step(
-            combined, row_places(half_rows), own, float(view_count), ids, tables, part_rows,
+            combined, row_places(back_rows), own, float(view_count), ids, tables, part_rows,
             [] if last else row_places(whole_rows),
         )
     if not shared:

time: 359 us -> 374 us (1.042)
  waiting for transfers between devices: 130 us -> 174 us
  starting transfers between devices: 140 us -> 111 us
    ppermute x95, waiting for transfers between devices: 125 us -> 169 us  [send(): return lax.ppermute(array, axis, [(i, i ^ flip) for i in range(count)])]
    ppermute x95, starting transfers between devices: 138 us -> 109 us  [send(): return lax.ppermute(array, axis, [(i, i ^ flip) for i in range(count)])]
  transfers between devices with their start and end apart: 96 -> 96, of which waited for: 31 -> 32; matrix products, arithmetic and copies ran while one was open for 1% -> 1% of each run, Pallas kernels for 15% -> 15%
where the time goes in v5:
time: 374 us
  waiting for transfers between devices  174 us (47%)
  starting transfers between devices  111 us (30%)
  Pallas kernels  77.6 us (21%)
  local copies, waits for them, and re-layouts  8.06 us (2%)
    ppermute x95, waiting for transfers between devices, send(): return lax.ppermute(array, axis, [(i, i ^ flip) for i in range(count)])  169 us
    ppermute x95, starting transfers between devices, send(): return lax.ppermute(array, axis, [(i, i ^ flip) for i in range(count)])  109 us
    pallas_call x7, Pallas kernels, lateral_call(): pl.pallas_call(kernel, in_specs=[SMEM] + [VMEM] * (len(operands) + len(pi...  37.1 us
    pallas_call x10, Pallas kernels, depth_step(): pl.pallas_call(body, out_shape=out_shape, in_specs=[SMEM] + [VMEM] * len(...  35.5 us
  transfers between devices with their start and end apart: 96, of which 32 were waited for; matrix products, arithmetic and copies ran while one was open for 1% of the time, Pallas kernels for 15%

profile of v5, /device:TPU:0, one launch (start us, length us, event | category | flops | bytes accessed | tf_op | source)
XLA Modules:
  0.0 373.9 jit_solution(2567976706298674543)
XLA Ops:
  18.5 4.6 %collective-permute-done.15 = f32[2,64,128]{2,1,0:T(8,128)} collective-permute-done((f32[2,64,128]{2,1,0:T(8,128)S(1)}, f32[2,64,128]{2,1,0:T(8,128)}, u32[]{:S(2)}, u32[]{:S(2)}) %collective-permute-start.15) | collective-permute-done | bytes 65568 | tf_op jit(solution)/shard_map/ppermute | solution.py:422
  26.6 3.4 collective-permute-done.11.refs_12_
  42.3 4.4 %depth_step.11 = (f32[8,40,128]{2,1,0:T(8,128)S(1)}, f32[8,40,128]{2,1,0:T(8,128)S(1)}, f32[8,40,128]{2,1,0:T(8,128)S(1)}, f32[8,40,128]{2,1,0:T(8,128)S(1)}, f3...) custom-call(s32[2]{0:T(128)S(1)} %pad_add_fusion.ids_ref, ...), custom_call_target="tpu_custom_call" | custom-call | tf_op jit(solution)/shard_map/depth_step/pallas_call | solution.py:398
  54.7 18.1 %collective-permute-done.26.refs_4_ = f32[8,24,128]{2,1,0:T(8,128)S(1)} collective-permute-done((f32[8,24,128]{2,1,0:T(8,128)S(1)}, f32[8,24,128]{2,1,0:T(8,128)S(1)}, u32[]{:S(2)}, u32[]{:S(2)}) %collective-permute-start.26) | collective-permute-done | bytes 98336 | tf_op jit(solution)/shard_map/ppermute | solution.py:476
  76.7 7.1 %shard_map.138 = (f32[8,64,128]{2,1,0:T(8,128)S(1)}, f32[8,64,128]{2,1,0:T(8,128)S(1)}, f32[8,64,128]{2,1,0:T(8,128)S(1)}, f32[8,64,128]{2,1,0:T(8,128)S(1)}) custom-call(s32[2]{0:T(128)S(1)} %pad_add_fusion.ids_ref, f32[16,256,128]{2,1,0:T(8,128)S(1)} %bitcast.9, s32[16,256,128]{2,1,0:T(8,128)S(1)} %bitcast.13, ...), custom_call_target="tpu_custom_call" | custom-call | tf_op jit(solution)/shard_map/pallas_call | solution.py:200
  89.7 6.1 %collective-permute-done.18.refs_5_ = f32[8,24,128]{2,1,0:T(8,128)S(1)} collective-permute-done((f32[8,24,128]{2,1,0:T(8,128)S(1)}, f32[8,24,128]{2,1,0:T(8,128)S(1)}, u32[]{:S(2)}, u32[]{:S(2)}) %collective-permute-start.18) | collective-permute-done | bytes 98336 | tf_op jit(solution)/shard_map/ppermute | solution.py:476
  98.9 15.9 %collective-permute-done.20.refs_8_ = f32[8,40,128]{2,1,0:T(8,128)S(1)} collective-permute-done((f32[8,40,128]{2,1,0:T(8,128)S(1)}, f32[8,40,128]{2,1,0:T(8,128)S(1)}, u32[]{:S(2)}, u32[]{:S(2)}) %collective-permute-start.20) | collective-permute-done | bytes 163872 | tf_op jit(solution)/shard_map/ppermute | solution.py:476
  114.8 7.1 %shard_map.137 = (f32[8,32,128]{2,1,0:T(8,128)S(1)}, f32[8,32,128]{2,1,0:T(8,128)S(1)}, f32[8,32,128]{2,1,0:T(8,128)S(1)}, f32[8,32,128]{2,1,0:T(8,128)S(1)}, f3...) custom-call(s32[2]{0:T(128)S(1)} %pad_add_fusion.ids_ref, ...), custom_call_target="tpu_custom_call" | custom-call | tf_op jit(solution)/shard_map/pallas_call | solution.py:200
  121.9 4.1 %collective-permute-start.22 = (f32[8,32,128]{2,1,0:T(8,128)S(1)}, f32[8,32,128]{2,1,0:T(8,128)S(1)}, u32[]{:S(2)}, u32[]{:S(2)}) collective-permute-start(f32[8,32,128]{2,1,0:T(8,128)S(1)} %get-tuple-element.95), channel_id=1, source_target_pairs={{0,4},{4,0},{8,12},{12,8},{1,5},{5,1},{9,13},{13,9},{2,6},{6,2},{1... | collective-permute-start | bytes 393224 | tf_op jit(solution)/shard_map/ppermute | solution.py:476
  131.6 3.8 %depth_step.12.refs_7_ = f32[64,64,128]{2,1,0:T(8,128)S(1)} custom-call(s32[2]{0:T(128)S(1)} %pad_add_fusion.ids_ref, f32[8,64,128]{2,1,0:T(8,128)S(1)} %get-tuple-element.106.refs_0_, f32[8,64,128]{2,1,0:T(8,128)S(1)} %collective-permute-done.31.refs_1_, f32[8,64,128]{2,1,0:T(8,128)S(1)} %collective-permute-done.32.refs_2_, ...), custom_call_target="tpu_custom_call" | custom-call | tf_op jit(solution)/shard_map/depth_step/pallas_call | solution.py:398
  137.5 3.4 depth_step.13
  145.5 3.7 collective-permute-done.39.refs_1_
  149.3 6.8 %collective-permute-done.40.refs_2_ = f32[8,32,128]{2,1,0:T(8,128)S(1)} collective-permute-done((f32[8,32,128]{2,1,0:T(8,128)S(1)}, f32[8,32,128]{2,1,0:T(8,128)S(1)}, u32[]{:S(2)}, u32[]{:S(2)}) %collective-permute-start.40) | collective-permute-done | bytes 131104 | tf_op jit(solution)/shard_map/ppermute | solution.py:476
  162.0 6.8 %collective-permute-done.35 = f32[16,32,128]{2,1,0:T(8,128)S(1)} collective-permute-done((f32[16,32,128]{2,1,0:T(8,128)S(1)}, f32[16,32,128]{2,1,0:T(8,128)S(1)}, u32[]{:S(2)}, u32[]{:S(2)}) %collective-permute-start.35) | collective-permute-done | bytes 262176 | tf_op jit(solution)/shard_map/ppermute | solution.py:476
  180.1 4.3 %collective-permute-done.45.refs_7_ = f32[4,32,128]{2,1,0:T(8,128)S(1)} collective-permute-done((f32[4,32,128]{2,1,0:T(8,128)S(1)}, f32[4,32,128]{2,1,0:T(8,128)S(1)}, u32[]{:S(2)}, u32[]{:S(2)}) %collective-permute-start.45) | collective-permute-done | bytes 65568 | tf_op jit(solution)/shard_map/ppermute | solution.py:476
  184.4 3.8 %shard_map.139 = (f32[4,256,128]{2,1,0:T(8,128)S(1)}, f32[4,64,128]{2,1,0:T(8,128)S(1)}, f32[4,64,128]{2,1,0:T(8,128)S(1)}, f32[4,64,128]{2,1,0:T(8,128)S(1)}, f32[4,64,128]{2,1,0:T(8,128)S(1)}) custom-call(s32[2]{0:T(128)S(1)} %pad_add_fusion.ids_ref, f32[4,256,128]{2,1,0:T(8,128)S(1)} %constant_dynamic-slice_fusion.refs_0_, ...), custom_call_target="tpu_custom_call" | custom-call | tf_op jit(solution)/shard_map/pallas_call | solution.py:200
  195.2 7.5 %collective-permute-done.54.refs_8_ = f32[4,64,128]{2,1,0:T(8,128)S(1)} collective-permute-done((f32[4,64,128]{2,1,0:T(8,128)S(1)}, f32[4,64,128]{2,1,0:T(8,128)S(1)}, u32[]{:S(2)}, u32[]{:S(2)}) %collective-permute-start.54) | collective-permute-done | bytes 131104 | tf_op jit(solution)/shard_map/ppermute | solution.py:476
  205.4 3.6 collective-permute-done.55.refs_9_
  215.2 4.4 %depth_step.16 = (f32[8,40,128]{2,1,0:T(8,128)S(1)}, f32[8,40,128]{2,1,0:T(8,128)S(1)}, f32[8,40,128]{2,1,0:T(8,128)S(1)}, f32[8,40,128]{2,1,0:T(8,128)S(1)}, f3...) custom-call(s32[2]{0:T(128)S(1)} %pad_add_fusion.ids_ref, ...), custom_call_target="tpu_custom_call" | custom-call | tf_op jit(solution)/shard_map/depth_step/pallas_call | solution.py:398
  226.9 18.7 %collective-permute-done.72.refs_4_ = f32[8,24,128]{2,1,0:T(8,128)S(1)} collective-permute-done((f32[8,24,128]{2,1,0:T(8,128)S(1)}, f32[8,24,128]{2,1,0:T(8,128)S(1)}, u32[]{:S(2)}, u32[]{:S(2)}) %collective-permute-start.72) | collective-permute-done | bytes 98336 | tf_op jit(solution)/shard_map/ppermute | solution.py:476
  248.3 7.1 %shard_map.141 = (f32[8,64,128]{2,1,0:T(8,128)S(1)}, f32[8,64,128]{2,1,0:T(8,128)S(1)}, f32[8,64,128]{2,1,0:T(8,128)S(1)}, f32[8,64,128]{2,1,0:T(8,128)S(1)}) custom-call(s32[2]{0:T(128)S(1)} %pad_add_fusion.ids_ref, f32[16,256,128]{2,1,0:T(8,128)S(1)} %bitcast.11, s32[16,256,128]{2,1,0:T(8,128)S(1)} %bitcast.15, ...), custom_call_target="tpu_custom_call" | custom-call | tf_op jit(solution)/shard_map/pallas_call | solution.py:200
  261.3 7.2 %collective-permute-done.64.refs_5_ = f32[8,24,128]{2,1,0:T(8,128)S(1)} collective-permute-done((f32[8,24,128]{2,1,0:T(8,128)S(1)}, f32[8,24,128]{2,1,0:T(8,128)S(1)}, u32[]{:S(2)}, u32[]{:S(2)}) %collective-permute-start.64) | collective-permute-done | bytes 98336 | tf_op jit(solution)/shard_map/ppermute | solution.py:476
  270.5 15.7 %collective-permute-done.66.refs_8_ = f32[8,40,128]{2,1,0:T(8,128)S(1)} collective-permute-done((f32[8,40,128]{2,1,0:T(8,128)S(1)}, f32[8,40,128]{2,1,0:T(8,128)S(1)}, u32[]{:S(2)}, u32[]{:S(2)}) %collective-permute-start.66) | collective-permute-done | bytes 163872 | tf_op jit(solution)/shard_map/ppermute | solution.py:476
  286.2 7.1 %shard_map.140 = (f32[8,32,128]{2,1,0:T(8,128)S(1)}, f32[8,32,128]{2,1,0:T(8,128)S(1)}, f32[8,32,128]{2,1,0:T(8,128)S(1)}, f32[8,32,128]{2,1,0:T(8,128)S(1)}, f3...) custom-call(s32[2]{0:T(128)S(1)} %pad_add_fusion.ids_ref, ...), custom_call_target="tpu_custom_call" | custom-call | tf_op jit(solution)/shard_map/pallas_call | solution.py:200
  293.3 4.1 %collective-permute-start.68 = (f32[8,32,128]{2,1,0:T(8,128)S(1)}, f32[8,32,128]{2,1,0:T(8,128)S(1)}, u32[]{:S(2)}, u32[]{:S(2)}) collective-permute-start(f32[8,32,128]{2,1,0:T(8,128)S(1)} %get-tuple-element.134), channel_id=1, source_target_pairs={{0,4},{4,0},{8,12},{12,8},{1,5},{5,1},{9,13},{13,9},{2,6},{6,2},{1... | collective-permute-start | bytes 393224 | tf_op jit(solution)/shard_map/ppermute | solution.py:476
  299.9 3.8 %depth_step.17.refs_7_ = f32[64,64,128]{2,1,0:T(8,128)S(1)} custom-call(s32[2]{0:T(128)S(1)} %pad_add_fusion.ids_ref, f32[8,64,128]{2,1,0:T(8,128)S(1)} %get-tuple-element.145.refs_0_, f32[8,64,128]{2,1,0:T(8,128)S(1)} %collective-permute-done.77.refs_1_, f32[8,64,128]{2,1,0:T(8,128)S(1)} %collective-permute-done.78.refs_2_, ...), custom_call_target="tpu_custom_call" | custom-call | tf_op jit(solution)/shard_map/depth_step/pallas_call | solution.py:398
  303.7 5.5 %collective-permute-done.69.refs_2_ = f32[8,32,128]{2,1,0:T(8,128)S(1)} collective-permute-done((f32[8,32,128]{2,1,0:T(8,128)S(1)}, f32[8,32,128]{2,1,0:T(8,128)S(1)}, u32[]{:S(2)}, u32[]{:S(2)}) %collective-permute-start.69) | collective-permute-done | bytes 131104 | tf_op jit(solution)/shard_map/ppermute | solution.py:476
  317.2 3.6 collective-permute-done.85.refs_1_
  320.8 6.9 %collective-permute-done.86.refs_2_ = f32[8,32,128]{2,1,0:T(8,128)S(1)} collective-permute-done((f32[8,32,128]{2,1,0:T(8,128)S(1)}, f32[8,32,128]{2,1,0:T(8,128)S(1)}, u32[]{:S(2)}, u32[]{:S(2)}) %collective-permute-start.86) | collective-permute-done | bytes 131104 | tf_op jit(solution)/shard_map/ppermute | solution.py:476
  334.6 5.8 %collective-permute-done.81 = f32[16,32,128]{2,1,0:T(8,128)S(1)} collective-permute-done((f32[16,32,128]{2,1,0:T(8,128)S(1)}, f32[16,32,128]{2,1,0:T(8,128)S(1)}, u32[]{:S(2)}, u32[]{:S(2)}) %collective-permute-start.81) | collective-permute-done | bytes 262176 | tf_op jit(solution)/shard_map/ppermute | solution.py:476
  351.6 4.4 %collective-permute-done.91.refs_7_ = f32[4,32,128]{2,1,0:T(8,128)S(1)} collective-permute-done((f32[4,32,128]{2,1,0:T(8,128)S(1)}, f32[4,32,128]{2,1,0:T(8,128)S(1)}, u32[]{:S(2)}, u32[]{:S(2)}) %collective-permute-start.91) | collective-permute-done | bytes 65568 | tf_op jit(solution)/shard_map/ppermute | solution.py:476
  359.7 10.2 %collective-permute-done.93.refs_1_ = f32[4,256,128]{2,1,0:T(8,128)S(1)} collective-permute-done((f32[4,256,128]{2,1,0:T(8,128)S(1)}, f32[4,256,128]{2,1,0:T(8,128)S(1)}, u32[]{:S(2)}, u32[]{:S(2)}) %collective-permute-start.93) | collective-permute-done | bytes 524320 | tf_op jit(solution)/shard_map/ppermute | solution.py:476
  (235 shorter events, 154.1 us)
Async XLA Ops:
  7.5 17.1 %collective-permute-start = (f32[4,64,128]{2,1,0:T(8,128)S(1)}, f32[4,64,128]{2,1,0:T(8,128)S(1)}, u32[]{:S(2)}, u32[]{:S(2)}) collective-permute-start(f32[4,64,128]{2,1,0:T(8,128)S(1)} %get-tuple-element.82.refs_0_), channel_id=1, source_target_pairs={{0,2},{1,3},{2,0},{3,1},{4,6},{5,7},{6,4},{7,5},{8,10},{9,11},{10,... | collective-permute-start | bytes 393224 | tf_op jit(solution)/shard_map/ppermute | solution.py:476
  10.5 14.2 %collective-permute-start.1 = (f32[4,64,128]{2,1,0:T(8,128)S(1)}, f32[4,64,128]{2,1,0:T(8,128)S(1)}, u32[]{:S(2)}, u32[]{:S(2)}) collective-permute-start(f32[4,64,128]{2,1,0:T(8,128)S(1)} %get-tuple-element.82.refs_0_), channel_id=1, source_target_pairs={{0,1},{1,0},{2,3},{3,2},{4,5},{5,4},{6,7},{7,6},{8,9},{9,8},{10,11... | collective-permute-start | bytes 393224 | tf_op jit(solution)/shard_map/ppermute | solution.py:476
  10.5 13.5 %collective-permute-start.3 = (f32[4,64,128]{2,1,0:T(8,128)}, f32[4,64,128]{2,1,0:T(8,128)S(1)}, u32[]{:S(2)}, u32[]{:S(2)}) collective-permute-start(f32[4,64,128]{2,1,0:T(8,128)} %get-tuple-element.83), channel_id=1, source_target_pairs={{0,4},{4,0},{8,12},{12,8},{1,5},{5,1},{9,13},{13,9},{2,6},{6,2},{1... | collective-permute-start | bytes 393224 | tf_op jit(solution)/shard_map/ppermute | solution.py:476
  12.1 13.1 %collective-permute-start.7 = (f32[4,64,128]{2,1,0:T(8,128)}, f32[4,64,128]{2,1,0:T(8,128)S(1)}, u32[]{:S(2)}, u32[]{:S(2)}) collective-permute-start(f32[4,64,128]{2,1,0:T(8,128)} %get-tuple-element.84), channel_id=1, source_target_pairs={{0,8},{4,12},{8,0},{12,4},{1,9},{5,13},{9,1},{13,5},{2,10},{6,14},... | collective-permute-start | bytes 393224 | tf_op jit(solution)/shard_map/ppermute | solution.py:476
  46.7 28.1 %collective-permute-start.28 = (f32[8,40,128]{2,1,0:T(8,128)S(1)}, f32[8,40,128]{2,1,0:T(8,128)S(1)}, u32[]{:S(2)}, u32[]{:S(2)}) collective-permute-start(f32[8,40,128]{2,1,0:T(8,128)S(1)} %get-tuple-element.103), channel_id=1, source_target_pairs={{0,4},{4,0},{8,12},{12,8},{1,5},{5,1},{9,13},{13,9},{2,6},{6,2},{1... | collective-permute-start | bytes 491528 | tf_op jit(solution)/shard_map/ppermute | solution.py:476
  48.3 28.3 %collective-permute-start.29 = (f32[8,40,128]{2,1,0:T(8,128)S(1)}, f32[8,40,128]{2,1,0:T(8,128)S(1)}, u32[]{:S(2)}, u32[]{:S(2)}) collective-permute-start(f32[8,40,128]{2,1,0:T(8,128)S(1)} %get-tuple-element.104), channel_id=1, source_target_pairs={{0,8},{4,12},{8,0},{12,4},{1,9},{5,13},{9,1},{13,5},{2,10},{6,14},... | collective-permute-start | bytes 491528 | tf_op jit(solution)/shard_map/ppermute | solution.py:476
  50.4 26.2 %collective-permute-start.30 = (f32[8,40,128]{2,1,0:T(8,128)S(1)}, f32[8,40,128]{2,1,0:T(8,128)S(1)}, u32[]{:S(2)}, u32[]{:S(2)}) collective-permute-start(f32[8,40,128]{2,1,0:T(8,128)S(1)} %get-tuple-element.105), channel_id=1, source_target_pairs={{0,12},{4,8},{8,4},{12,0},{1,13},{5,9},{9,5},{13,1},{2,14},{6,10},... | collective-permute-start | bytes 491528 | tf_op jit(solution)/shard_map/ppermute | solution.py:476
  51.8 21.1 %collective-permute-start.26 = (f32[8,24,128]{2,1,0:T(8,128)S(1)}, f32[8,24,128]{2,1,0:T(8,128)S(1)}, u32[]{:S(2)}, u32[]{:S(2)}) collective-permute-start(f32[8,24,128]{2,1,0:T(8,128)S(1)} %get-tuple-element.101), channel_id=1, source_target_pairs={{0,8},{4,12},{8,0},{12,4},{1,9},{5,13},{9,1},{13,5},{2,10},{6,14},... | collective-permute-start | bytes 294920 | tf_op jit(solution)/shard_map/ppermute | solution.py:476
  53.8 19.3 %collective-permute-start.27 = (f32[8,24,128]{2,1,0:T(8,128)S(1)}, f32[8,24,128]{2,1,0:T(8,128)S(1)}, u32[]{:S(2)}, u32[]{:S(2)}) collective-permute-start(f32[8,24,128]{2,1,0:T(8,128)S(1)} %get-tuple-element.102), channel_id=1, source_target_pairs={{0,12},{4,8},{8,4},{12,0},{1,13},{5,9},{9,5},{13,1},{2,14},{6,10},... | collective-permute-start | bytes 294920 | tf_op jit(solution)/shard_map/ppermute | solution.py:476
  72.8 23.0 %collective-permute-start.19 = (f32[8,40,128]{2,1,0:T(8,128)S(1)}, f32[8,40,128]{2,1,0:T(8,128)S(1)}, u32[]{:S(2)}, u32[]{:S(2)}) collective-permute-start(f32[8,40,128]{2,1,0:T(8,128)S(1)} %get-tuple-element.91), channel_id=1, source_target_pairs={{0,4},{4,0},{8,12},{12,8},{1,5},{5,1},{9,13},{13,9},{2,6},{6,2},{1... | collective-permute-start | bytes 491528 | tf_op jit(solution)/shard_map/ppermute | solution.py:476
  73.1 13.4 %collective-permute-start.16 = (f32[8,24,128]{2,1,0:T(8,128)S(1)}, f32[8,24,128]{2,1,0:T(8,128)S(1)}, u32[]{:S(2)}, u32[]{:S(2)}) collective-permute-start(f32[8,24,128]{2,1,0:T(8,128)S(1)} %get-tuple-element.87), channel_id=1, source_target_pairs={{0,4},{4,0},{8,12},{12,8},{1,5},{5,1},{9,13},{13,9},{2,6},{6,2},{1... | collective-permute-start | bytes 294920 | tf_op jit(solution)/shard_map/ppermute | solution.py:476
  83.8 43.1 %collective-permute-start.31 = (f32[8,64,128]{2,1,0:T(8,128)S(1)}, f32[8,64,128]{2,1,0:T(8,128)S(1)}, u32[]{:S(2)}, u32[]{:S(2)}) collective-permute-start(f32[8,64,128]{2,1,0:T(8,128)S(1)} %get-tuple-element.107), channel_id=1, source_target_pairs={{0,4},{4,0},{8,12},{12,8},{1,5},{5,1},{9,13},{13,9},{2,6},{6,2},{1... | collective-permute-start | bytes 786440 | tf_op jit(solution)/shard_map/ppermute | solution.py:476
  86.5 28.3 %collective-permute-start.20 = (f32[8,40,128]{2,1,0:T(8,128)S(1)}, f32[8,40,128]{2,1,0:T(8,128)S(1)}, u32[]{:S(2)}, u32[]{:S(2)}) collective-permute-start(f32[8,40,128]{2,1,0:T(8,128)S(1)} %get-tuple-element.92), channel_id=1, source_target_pairs={{0,8},{4,12},{8,0},{12,4},{1,9},{5,13},{9,1},{13,5},{2,10},{6,14},... | collective-permute-start | bytes 491528 | tf_op jit(solution)/shard_map/ppermute | solution.py:476
  87.4 27.4 %collective-permute-start.21 = (f32[8,40,128]{2,1,0:T(8,128)S(1)}, f32[8,40,128]{2,1,0:T(8,128)S(1)}, u32[]{:S(2)}, u32[]{:S(2)}) collective-permute-start(f32[8,40,128]{2,1,0:T(8,128)S(1)} %get-tuple-element.93), channel_id=1, source_target_pairs={{0,12},{4,8},{8,4},{12,0},{1,13},{5,9},{9,5},{13,1},{2,14},{6,10},... | collective-permute-start | bytes 491528 | tf_op jit(solution)/shard_map/ppermute | solution.py:476
  95.8 35.8 %collective-permute-start.32 = (f32[8,64,128]{2,1,0:T(8,128)S(1)}, f32[8,64,128]{2,1,0:T(8,128)S(1)}, u32[]{:S(2)}, u32[]{:S(2)}) collective-permute-start(f32[8,64,128]{2,1,0:T(8,128)S(1)} %get-tuple-element.108), channel_id=1, source_target_pairs={{0,8},{4,12},{8,0},{12,4},{1,9},{5,13},{9,1},{13,5},{2,10},{6,14},... | collective-permute-start | bytes 786440 | tf_op jit(solution)/shard_map/ppermute | solution.py:476
  95.8 35.8 %collective-permute-start.33 = (f32[8,64,128]{2,1,0:T(8,128)S(1)}, f32[8,64,128]{2,1,0:T(8,128)S(1)}, u32[]{:S(2)}, u32[]{:S(2)}) collective-permute-start(f32[8,64,128]{2,1,0:T(8,128)S(1)} %get-tuple-element.109), channel_id=1, source_target_pairs={{0,12},{4,8},{8,4},{12,0},{1,13},{5,9},{9,5},{13,1},{2,14},{6,10},... | collective-permute-start | bytes 786440 | tf_op jit(solution)/shard_map/ppermute | solution.py:476
  121.9 13.5 %collective-permute-start.22 = (f32[8,32,128]{2,1,0:T(8,128)S(1)}, f32[8,32,128]{2,1,0:T(8,128)S(1)}, u32[]{:S(2)}, u32[]{:S(2)}) collective-permute-start(f32[8,32,128]{2,1,0:T(8,128)S(1)} %get-tuple-element.95), channel_id=1, source_target_pairs={{0,4},{4,0},{8,12},{12,8},{1,5},{5,1},{9,13},{13,9},{2,6},{6,2},{1... | collective-permute-start | bytes 393224 | tf_op jit(solution)/shard_map/ppermute | solution.py:476
  140.9 18.6 %collective-permute-start.34 = (f32[32,32,128]{2,1,0:T(8,128)S(1)}, f32[32,32,128]{2,1,0:T(8,128)S(1)}, u32[]{:S(2)}, u32[]{:S(2)}) collective-permute-start(f32[32,32,128]{2,1,0:T(8,128)S(1)} %get-tuple-element.111), channel_id=1, source_target_pairs={{0,1},{1,0},{2,3},{3,2},{4,5},{5,4},{6,7},{7,6},{8,9},{9,8},{10,11... | collective-permute-start | bytes 1572872 | tf_op jit(solution)/shard_map/ppermute | solution.py:476
  191.3 13.0 %collective-permute-start.58 = (f32[4,64,128]{2,1,0:T(8,128)S(1)}, f32[4,64,128]{2,1,0:T(8,128)S(1)}, u32[]{:S(2)}, u32[]{:S(2)}) collective-permute-start(f32[4,64,128]{2,1,0:T(8,128)S(1)} %get-tuple-element.124), channel_id=1, source_target_pairs={{0,12},{4,8},{8,4},{12,0},{1,13},{5,9},{9,5},{13,1},{2,14},{6,10},... | collective-permute-start | bytes 393224 | tf_op jit(solution)/shard_map/ppermute | solution.py:476
  219.6 28.1 %collective-permute-start.74 = (f32[8,40,128]{2,1,0:T(8,128)S(1)}, f32[8,40,128]{2,1,0:T(8,128)S(1)}, u32[]{:S(2)}, u32[]{:S(2)}) collective-permute-start(f32[8,40,128]{2,1,0:T(8,128)S(1)} %get-tuple-element.142), channel_id=1, source_target_pairs={{0,4},{4,0},{8,12},{12,8},{1,5},{5,1},{9,13},{13,9},{2,6},{6,2},{1... | collective-permute-start | bytes 491528 | tf_op jit(solution)/shard_map/ppermute | solution.py:476
  221.1 27.2 %collective-permute-start.75 = (f32[8,40,128]{2,1,0:T(8,128)S(1)}, f32[8,40,128]{2,1,0:T(8,128)S(1)}, u32[]{:S(2)}, u32[]{:S(2)}) collective-permute-start(f32[8,40,128]{2,1,0:T(8,128)S(1)} %get-tuple-element.143), channel_id=1, source_target_pairs={{0,8},{4,12},{8,0},{12,4},{1,9},{5,13},{9,1},{13,5},{2,10},{6,14},... | collective-permute-start | bytes 491528 | tf_op jit(solution)/shard_map/ppermute | solution.py:476
  222.2 26.1 %collective-permute-start.76 = (f32[8,40,128]{2,1,0:T(8,128)S(1)}, f32[8,40,128]{2,1,0:T(8,128)S(1)}, u32[]{:S(2)}, u32[]{:S(2)}) collective-permute-start(f32[8,40,128]{2,1,0:T(8,128)S(1)} %get-tuple-element.144), channel_id=1, source_target_pairs={{0,12},{4,8},{8,4},{12,0},{1,13},{5,9},{9,5},{13,1},{2,14},{6,10},... | collective-permute-start | bytes 491528 | tf_op jit(solution)/shard_map/ppermute | solution.py:476
  224.0 21.6 %collective-permute-start.72 = (f32[8,24,128]{2,1,0:T(8,128)S(1)}, f32[8,24,128]{2,1,0:T(8,128)S(1)}, u32[]{:S(2)}, u32[]{:S(2)}) collective-permute-start(f32[8,24,128]{2,1,0:T(8,128)S(1)} %get-tuple-element.139), channel_id=1, source_target_pairs={{0,8},{4,12},{8,0},{12,4},{1,9},{5,13},{9,1},{13,5},{2,10},{6,14},... | collective-permute-start | bytes 294920 | tf_op jit(solution)/shard_map/ppermute | solution.py:476
  225.1 20.5 %collective-permute-start.73 = (f32[8,24,128]{2,1,0:T(8,128)S(1)}, f32[8,24,128]{2,1,0:T(8,128)S(1)}, u32[]{:S(2)}, u32[]{:S(2)}) collective-permute-start(f32[8,24,128]{2,1,0:T(8,128)S(1)} %get-tuple-element.140), channel_id=1, source_target_pairs={{0,12},{4,8},{8,4},{12,0},{1,13},{5,9},{9,5},{13,1},{2,14},{6,10},... | collective-permute-start | bytes 294920 | tf_op jit(solution)/shard_map/ppermute | solution.py:476
  245.6 22.9 %collective-permute-start.65 = (f32[8,40,128]{2,1,0:T(8,128)S(1)}, f32[8,40,128]{2,1,0:T(8,128)S(1)}, u32[]{:S(2)}, u32[]{:S(2)}) collective-permute-start(f32[8,40,128]{2,1,0:T(8,128)S(1)} %get-tuple-element.130), channel_id=1, source_target_pairs={{0,4},{4,0},{8,12},{12,8},{1,5},{5,1},{9,13},{13,9},{2,6},{6,2},{1... | collective-permute-start | bytes 491528 | tf_op jit(solution)/shard_map/ppermute | solution.py:476
  245.6 13.6 %collective-permute-start.62 = (f32[8,24,128]{2,1,0:T(8,128)S(1)}, f32[8,24,128]{2,1,0:T(8,128)S(1)}, u32[]{:S(2)}, u32[]{:S(2)}) collective-permute-start(f32[8,24,128]{2,1,0:T(8,128)S(1)} %get-tuple-element.126), channel_id=1, source_target_pairs={{0,4},{4,0},{8,12},{12,8},{1,5},{5,1},{9,13},{13,9},{2,6},{6,2},{1... | collective-permute-start | bytes 294920 | tf_op jit(solution)/shard_map/ppermute | solution.py:476
  255.4 42.7 %collective-permute-start.77 = (f32[8,64,128]{2,1,0:T(8,128)S(1)}, f32[8,64,128]{2,1,0:T(8,128)S(1)}, u32[]{:S(2)}, u32[]{:S(2)}) collective-permute-start(f32[8,64,128]{2,1,0:T(8,128)S(1)} %get-tuple-element.146), channel_id=1, source_target_pairs={{0,4},{4,0},{8,12},{12,8},{1,5},{5,1},{9,13},{13,9},{2,6},{6,2},{1... | collective-permute-start | bytes 786440 | tf_op jit(solution)/shard_map/ppermute | solution.py:476
  259.2 27.0 %collective-permute-start.66 = (f32[8,40,128]{2,1,0:T(8,128)S(1)}, f32[8,40,128]{2,1,0:T(8,128)S(1)}, u32[]{:S(2)}, u32[]{:S(2)}) collective-permute-start(f32[8,40,128]{2,1,0:T(8,128)S(1)} %get-tuple-element.131), channel_id=1, source_target_pairs={{0,8},{4,12},{8,0},{12,4},{1,9},{5,13},{9,1},{13,5},{2,10},{6,14},... | collective-permute-start | bytes 491528 | tf_op jit(solution)/shard_map/ppermute | solution.py:476
  259.3 27.0 %collective-permute-start.67 = (f32[8,40,128]{2,1,0:T(8,128)S(1)}, f32[8,40,128]{2,1,0:T(8,128)S(1)}, u32[]{:S(2)}, u32[]{:S(2)}) collective-permute-start(f32[8,40,128]{2,1,0:T(8,128)S(1)} %get-tuple-element.132), channel_id=1, source_target_pairs={{0,12},{4,8},{8,4},{12,0},{1,13},{5,9},{9,5},{13,1},{2,14},{6,10},... | collective-permute-start | bytes 491528 | tf_op jit(solution)/shard_map/ppermute | solution.py:476
  268.5 31.4 %collective-permute-start.78 = (f32[8,64,128]{2,1,0:T(8,128)S(1)}, f32[8,64,128]{2,1,0:T(8,128)S(1)}, u32[]{:S(2)}, u32[]{:S(2)}) collective-permute-start(f32[8,64,128]{2,1,0:T(8,128)S(1)} %get-tuple-element.147), channel_id=1, source_target_pairs={{0,8},{4,12},{8,0},{12,4},{1,9},{5,13},{9,1},{13,5},{2,10},{6,14},... | collective-permute-start | bytes 786440 | tf_op jit(solution)/shard_map/ppermute | solution.py:476
  268.5 31.4 %collective-permute-start.79 = (f32[8,64,128]{2,1,0:T(8,128)S(1)}, f32[8,64,128]{2,1,0:T(8,128)S(1)}, u32[]{:S(2)}, u32[]{:S(2)}) collective-permute-start(f32[8,64,128]{2,1,0:T(8,128)S(1)} %get-tuple-element.148), channel_id=1, source_target_pairs={{0,12},{4,8},{8,4},{12,0},{1,13},{5,9},{9,5},{13,1},{2,14},{6,10},... | collective-permute-start | bytes 786440 | tf_op jit(solution)/shard_map/ppermute | solution.py:476
  312.6 18.5 %collective-permute-start.80 = (f32[32,32,128]{2,1,0:T(8,128)S(1)}, f32[32,32,128]{2,1,0:T(8,128)S(1)}, u32[]{:S(2)}, u32[]{:S(2)}) collective-permute-start(f32[32,32,128]{2,1,0:T(8,128)S(1)} %get-tuple-element.150), channel_id=1, source_target_pairs={{0,1},{1,0},{2,3},{3,2},{4,5},{5,4},{6,7},{7,6},{8,9},{9,8},{10,11... | collective-permute-start | bytes 1572872 | tf_op jit(solution)/shard_map/ppermute | solution.py:476
  (81 other events, 859.5 us)
